TPU v7x, 32 devices: a whole 2x2x4 slice. The times are simulated.
32 devices in a mesh: blk: 16 (over z, y, core), grp: 2 (over x).
Axes of the slice: x: 2, y: 2, z: 4, core: 2. Of those that a mesh axis runs over, the one named last changes fastest.
Arguments:
- images: float32 [4096, 768], P(('blk', 'grp')), may hold values from -0.24 to 0.24
- texts: float32 [4096, 768], P(('blk', 'grp')), may hold values from -0.24 to 0.24
- log_temp: float32 [1], replicated, may hold values from 2.3 to 3
- bias: float32 [1], replicated, may hold values from -3 to -1
- row_weight: float32 [4096], P(('blk', 'grp')), may hold values from 0.5 to 2
Outputs:
- row_loss: float32 [4096], P(('blk', 'grp'))
- grad_images: float32 [4096, 768], P(('blk', 'grp'))
- grad_texts: float32 [4096, 768], P(('blk', 'grp'))
All inputs are finite; a program needn't handle non-finite values.
Results may differ from a plain program's by a relative error of at most 0.00013.
Values sent between devices are 32-bit elements; how exact they have to be, the bound alone decides.
No kernel may reach another device: no remote copies, remote signals or barrier semaphores. Data moves between devices by JAX's collectives and lax.ppermute only.
A program may use at most 64 MiB of HBM per device.

v0:
```python
import functools

import jax
import jax.numpy as jnp
from jax import lax
from jax.experimental import pallas as pl
from jax.experimental.pallas import tpu as pltpu
from jax.sharding import PartitionSpec as P


BF = jnp.bfloat16
F32 = jnp.float32
VMEM = pl.BlockSpec(memory_space=pltpu.VMEM)
SMEM = pl.BlockSpec(memory_space=pltpu.SMEM)
HBM = pl.BlockSpec(memory_space=pltpu.HBM)
CHUNKS = 4
NT = ((1,), (1,))
NN = ((1,), (0,))


def swapped(x, axis, near):
    length = lax.axis_size(axis)
    if near:
        pairs = [(i, i + 1) for i in range(0, length, 2)]
    else:
        pairs = [(i, (i + 1) % length) for i in range(1, length, 2)]
    return lax.ppermute(x, axis, pairs + [(b, a) for (a, b) in pairs])


def shifted(x, axis, by):
    length = lax.axis_size(axis)
    return lax.ppermute(x, axis, [(i, (i + by) % length) for i in range(length)])


def unit_of(raw):
    return raw * lax.rsqrt(jnp.sum(raw * raw, axis=1, keepdims=True) + 1e-06)


def stacked(v):
    high = v.astype(BF)
    return jnp.concatenate([high, (v - high.astype(F32)).astype(BF)], axis=0)


def mm(a, b, dims):
    rows = a.shape[0] // 2
    deep = b.shape[0] // 2

    def one(p, q):
        return lax.dot_general(p, q, (dims, ((), ())), preferred_element_type=F32)

    both = one(a[...], b[:deep])
    return both[:rows] + (both[rows:] + one(a[:rows], b[deep:]))


def log_one_plus(t):
    series = t * (1.0 + t * (-0.5 + t * (1.0 / 3.0 + t * (-0.25 + t * 0.2))))
    return jnp.where(t < 0.03125, series, jnp.log(1.0 + t))


def gated(z, weight, diagonal=None):
    signed = z if diagonal is None else jnp.where(diagonal, -z, z)
    small = jnp.exp(-jnp.abs(signed))
    loss = jnp.maximum(signed, 0.0) + log_one_plus(small)
    slope = jnp.where(signed >= 0.0, 1.0, small) / (1.0 + small) * weight
    if diagonal is not None:
        slope = jnp.where(diagonal, -slope, slope)
    return jnp.sum(loss, axis=0, keepdims=True), slope


def temper_of(lt):
    return jnp.exp(jnp.full((1, 1), lt[0], F32))


def first_body(lt, bi, x_any, y_any, near_ref, w_ref, *refs):
    x_ref, y_ref, xs_ref, ys_ref, gx_ref, gy_ref, sum_ref, sem = refs
    copies = [
        pltpu.make_async_copy(x_any, x_ref, sem.at[0]),
        pltpu.make_async_copy(y_any, y_ref, sem.at[1]),
    ]
    for copy in copies:
        copy.start()
    temper = temper_of(lt)
    count = near_ref.shape[0]
    near = unit_of(near_ref[...])
    copies[0].wait()
    xs_ref[...] = stacked(unit_of(x_ref[...]))
    copies[1].wait()
    ys_ref[...] = stacked(jnp.concatenate([unit_of(y_ref[...]), near], axis=0))
    rows = lax.broadcasted_iota(jnp.int32, (2 * count, count), 0)
    cols = lax.broadcasted_iota(jnp.int32, (2 * count, count), 1)
    z = temper * mm(ys_ref, xs_ref, NT) + bi[0]
    sums, slope = gated(z, w_ref[...] * temper, rows == cols)
    sum_ref[...] = sums
    gx_ref[...] = mm(stacked(slope.T), ys_ref, NN)
    gy_ref[...] = mm(stacked(slope), xs_ref, NN)


def second_body(others, lt, bi, *refs):
    raw_refs, refs = refs[:others], refs[others:]
    w_refs, refs = refs[:others], refs[others:]
    ys_ref, refs = refs[0], refs[1:]
    px_refs, refs = refs[:others], refs[others:]
    gp_refs, refs = refs[:others], refs[others:]
    sump_refs, slope_refs = refs[:others], refs[others:]
    temper = temper_of(lt)
    for s in range(others):
        px_refs[s][...] = stacked(unit_of(raw_refs[s][...]))
        z = temper * mm(ys_ref, px_refs[s], NT) + bi[0]
        sump_refs[s][...], slope = gated(z, w_refs[s][...] * temper)
        slope_refs[s][...] = slope
        gp_refs[s][...] = mm(stacked(slope.T), ys_ref, NN)


def third_body(others, lt, bi, *refs):
    members = others + 1
    far_ref, refs = refs[0], refs[1:]
    w_refs, refs = refs[:members], refs[members:]
    x_refs, refs = refs[:members], refs[members:]
    gp_in, refs = refs[:others], refs[others:]
    sum_in, refs = refs[:members], refs[members:]
    gfar_ref, refs = refs[0], refs[1:]
    gp_refs, refs = refs[:others], refs[others:]
    sum_refs, refs = refs[:members], refs[members:]
    fs_ref, slope_ref = refs
    temper = temper_of(lt)
    fs_ref[...] = stacked(unit_of(far_ref[...]))
    gfar = None
    for s in range(members):
        z = temper * mm(fs_ref, x_refs[s], NT) + bi[0]
        sums, slope = gated(z, w_refs[s][...] * temper)
        sum_refs[s][...] = sum_in[s][...] + sums
        g = mm(stacked(slope), x_refs[s], NN)
        gfar = g if gfar is None else gfar + g
        if s == 0:
            slope_ref[...] = slope
        else:
            gp_refs[s - 1][...] = gp_in[s - 1][...] + mm(stacked(slope.T), fs_ref, NN)
    gfar_ref[...] = gfar


def fourth_body(others, gx_in, gy_in, slope_ref, fs_ref, *refs):
    slopes, refs = refs[:others], refs[others:]
    px_refs, (gx_ref, gown_ref, gnear_ref) = refs[:others], refs[others:]
    count = gx_in.shape[0]
    gy = gy_in[...]
    for s in range(others):
        gy = gy + mm(stacked(slopes[s][...]), px_refs[s], NN)
    gown_ref[...] = gy[:count]
    gnear_ref[...] = gy[count:]
    gx_ref[...] = gx_in[...] + mm(stacked(slope_ref[...].T), fs_ref, NN)


def last_body(parts, lines, pairs, *refs):
    held, line, sem = refs[-3:]
    refs, outs = refs[:-6], refs[-6:-3]
    copies = []

    def send(source, target):
        copies.append(pltpu.make_async_copy(source, target, sem.at[len(copies)]))
        copies[-1].start()

    for k, terms in enumerate(parts):
        raw_ref, grads, refs = refs[0], refs[1 : 1 + terms], refs[1 + terms :]
        rows = raw_ref.shape[0] // CHUNKS
        for c in range(CHUNKS):
            here = pl.ds(c * rows, rows)
            raw = raw_ref[here, :]
            grad = grads[0][here, :]
            for r in grads[1:]:
                grad = grad + r[here, :]
            scale = lax.rsqrt(jnp.sum(raw * raw, axis=1, keepdims=True) + 1e-06)
            unit = raw * scale
            inner = jnp.sum(unit * grad, axis=1, keepdims=True)
            held[k, here, :] = scale * (grad - unit * inner)
            send(held.at[k, here, :], outs[k].at[here, :])
    total = refs[0][...]
    for r in refs[1:lines]:
        total = total + r[...]
    line[...] = total / pairs
    send(line, outs[2])
    for copy in copies:
        copy.wait()


def shape(*dims, kind=F32):
    return jax.ShapeDtypeStruct(dims, kind)


PARAMS = pltpu.CompilerParams(vmem_limit_bytes=16 * 1024 * 1024)


def in_hbm(args):
    return [pltpu.with_memory_space_constraint(a, pltpu.HBM) for a in args]


def in_vmem(args):
    return [pltpu.with_memory_space_constraint(a, pltpu.VMEM) for a in args]


def call(body, outs, scalars, *args, scratch=(), anywhere=0):
    return pl.pallas_call(
        body,
        out_shape=[pltpu.VMEM(o.shape, o.dtype) for o in outs],
        in_specs=[SMEM] * len(scalars) + [HBM] * anywhere + [VMEM] * (len(args) - anywhere),
        out_specs=[VMEM] * len(outs),
        scratch_shapes=list(scratch),
        compiler_params=PARAMS,
    )(*scalars, *in_hbm(args[:anywhere]), *in_vmem(args[anywhere:]))


def finish(x_terms, y_terms, lines, pairs):
    full = shape(*x_terms[0].shape)
    line = shape(1, full.shape[0])
    args = [*x_terms, *y_terms, *lines]
    return pl.pallas_call(
        functools.partial(last_body, (len(x_terms) - 1, len(y_terms) - 1), len(lines), pairs),
        out_shape=[full, full, line],
        in_specs=[VMEM] * len(args),
        out_specs=[HBM] * 3,
        scratch_shapes=[
            pltpu.VMEM((2, *full.shape), F32),
            pltpu.VMEM(line.shape, F32),
            pltpu.SemaphoreType.DMA((2 * CHUNKS + 1,)),
        ],
        compiler_params=PARAMS,
    )(*in_vmem(args))


def body(images, texts, log_temp, bias, row_weight):
    members = lax.axis_size("grp")
    others = members - 1
    count, width = images.shape
    weight = row_weight.reshape(1, count)
    scalars = (log_temp, bias)
    raws = [shifted(images, "grp", -s) for s in range(1, members)]
    far = swapped(texts, "blk", False)
    near = swapped(texts, "blk", True)
    weights = [weight] + [shifted(weight, "grp", -s) for s in range(1, members)]
    full = shape(count, width)
    line = shape(1, count)
    stack = shape(2 * count, width, kind=BF)
    x_raw, y_raw, xs, ys, gx, gy, sums = call(
        first_body,
        [
            full,
            full,
            stack,
            shape(4 * count, width, kind=BF),
            full,
            shape(2 * count, width),
            line,
        ],
        scalars,
        images,
        texts,
        near,
        weight,
        scratch=[pltpu.SemaphoreType.DMA((2,))],
        anywhere=2,
    )
    outs = call(
        functools.partial(second_body, others),
        [stack] * others
        + [full] * others
        + [line] * others
        + [shape(2 * count, count)] * others,
        scalars,
        *raws,
        *weights[1:],
        ys,
    )
    px, outs = outs[:others], outs[others:]
    gp, outs = outs[:others], outs[others:]
    sump, slopes = outs[:others], outs[others:]
    outs = call(
        functools.partial(third_body, others),
        [full]
        + [full] * others
        + [line] * members
        + [stack, shape(count, count)],
        scalars,
        far,
        *weights,
        xs,
        *px,
        *gp,
        sums,
        *sump,
    )
    g_far, outs = outs[0], outs[1:]
    gp, outs = outs[:others], outs[others:]
    sums, (fs, slope) = outs[:members], outs[members:]
    back_far = swapped(g_far, "blk", False)
    back_x = [shifted(gp[s - 1], "grp", s) for s in range(1, members)]
    back_sum = [shifted(sums[s], "grp", s) for s in range(1, members)]
    gx, g_own, g_near = call(
        functools.partial(fourth_body, others),
        [full] * 3,
        (),
        gx,
        gy,
        slope,
        fs,
        *slopes,
        *px,
    )
    back_near = swapped(g_near, "blk", True)
    grad_x, grad_y, row_loss = finish(
        [x_raw, gx, *back_x],
        [y_raw, g_own, back_near, back_far],
        [sums[0], *back_sum],
        3.0 * members * count,
    )
    return (row_loss.reshape(count), grad_x, grad_y)


def solution(mesh):
    placed = (P(("blk", "grp"), None), P(("blk", "grp"), None), P(), P(), P(("blk", "grp")))
    return jax.shard_map(
        body,
        mesh=mesh,
        in_specs=placed,
        out_specs=(P(("blk", "grp")), P(("blk", "grp"), None), P(("blk", "grp"), None)),
        check_vma=False,
    )
```

profile of v0, /device:TPU:1, one launch (start us, length us, event | category | flops | bytes accessed | tf_op | source)
XLA Modules:
  0.0 31.5 jit_solution(4838688486430462115)
XLA Ops:
  0.6 0.0 copy-start
  0.6 0.1 collective-permute-start
  0.7 2.7 %collective-permute-start.3 = (f32[128,768]{1,0:T(8,128)}, f32[128,768]{1,0:T(8,128)S(1)}, u32[]{:S(2)}, u32[]{:S(2)}) collective-permute-start(f32[128,768]{1,0:T(8,128)} %x_any.1), channel_id=1, source_target_pairs={{0,1},{1,0},{2,3},{3,2},{4,5},{5,4},{6,7},{7,6},{8,9},{9,8},{10,11... | collective-permute-start | bytes 1179656 | tf_op jit(solution)/shard_map/ppermute | solution.py:32
  3.4 1.5 %collective-permute-start.1 = (f32[128,768]{1,0:T(8,128)}, f32[128,768]{1,0:T(8,128)S(1)}, u32[]{:S(2)}, u32[]{:S(2)}) collective-permute-start(f32[128,768]{1,0:T(8,128)} %y_any.1), channel_id=1, source_target_pairs={{2,4},{6,8},{10,12},{14,16},{18,20},{22,24},{26,28},{30,0},{4,2},{... | collective-permute-start | bytes 1179656 | tf_op jit(solution)/shard_map/ppermute | solution.py:27
  4.9 0.0 copy-done
  4.9 0.3 collective-permute-start.2
  6.4 0.0 collective-permute-done.near_ref
  6.5 3.0 %shard_map.76 = (f32[128,768]{1,0:T(8,128)S(1)}, f32[128,768]{1,0:T(8,128)S(1)}, bf16[256,768]{1,0:T(8,128)(2,1)S(1)}, bf16[512,768]{1,0:T(8,128)(2,1)S(1)}, f32...) custom-call(f32[1]{0:T(128)S(6)} %copy.8.lt, f32[1]{0:T(128)S(6)} %copy.9.bi, f32[128,768]{1,0:T(8,128)} %x_any.1, ...), custom_call_target="tpu_custom_call" | custom-call | tf_op jit(solution)/shard_map/pallas_call | solution.py:201
  9.5 3.5 %collective-permute-done.2.refs_1_.refs_2_ = f32[1,128]{1,0:T(1,128)S(1)} collective-permute-done((f32[1,128]{1,0:T(1,128)S(1)}, f32[1,128]{1,0:T(1,128)S(1)}, u32[]{:S(2)}, u32[]{:S(2)}) %collective-permute-start.2) | collective-permute-done | bytes 544 | tf_op jit(solution)/shard_map/ppermute | solution.py:32
  13.0 0.0 collective-permute-done.3.refs_0_
  13.0 1.2 %shard_map.77 = (bf16[256,768]{1,0:T(8,128)(2,1)S(1)}, f32[128,768]{1,0:T(8,128)S(1)}, f32[1,128]{1,0:T(1,128)S(1)}, f32[256,128]{1,0:T(8,128)S(1)}) custom-call(f32[1]{0:T(128)S(6)} %copy.8.lt, f32[1]{0:T(128)S(6)} %copy.9.bi, f32[128,768]{1,0:T(8,128)S(1)} %collective-permute-done.3.refs_0_, f32[1,128]{1,0:T(1,128)S(1)} %collective-permute-done.2.refs_1_.refs_2_, ...), custom_call_target="tpu_custom_call" | custom-call | tf_op jit(solution)/shard_map/pallas_call | solution.py:201
  14.3 0.7 %collective-permute-done.1.refs_0_ = f32[128,768]{1,0:T(8,128)S(1)} collective-permute-done((f32[128,768]{1,0:T(8,128)}, f32[128,768]{1,0:T(8,128)S(1)}, u32[]{:S(2)}, u32[]{:S(2)}) %collective-permute-start.1) | collective-permute-done | bytes 393248 | tf_op jit(solution)/shard_map/ppermute | solution.py:27
  15.0 1.6 %shard_map.78 = (f32[128,768]{1,0:T(8,128)S(1)}, f32[128,768]{1,0:T(8,128)S(1)}, f32[1,128]{1,0:T(1,128)S(1)}, f32[1,128]{1,0:T(1,128)S(1)}, bf16[256,768]{1,0:T(8,128)(2,1)S(1)}, /*index=5*/f32[128,128]{1,0:T(8,128)S(1)}) custom-call(f32[1]{0:T(128)S(6)} %copy.8.lt, f32[1]{0:T(128)S(6)} %copy.9.bi, f32[128,768]{1,0:T(8,128)S(1)} %collective-permute-done.1.refs_0_, ...), custom_call_target="tpu_custom_call" | custom-call | tf_op jit(solution)/shard_map/pallas_call | solution.py:201
  16.7 0.6 %shard_map.79 = (f32[128,768]{1,0:T(8,128)S(1)}, f32[128,768]{1,0:T(8,128)S(1)}, f32[128,768]{1,0:T(8,128)S(1)}) custom-call(f32[128,768]{1,0:T(8,128)S(1)} %get-tuple-element.27.gx_in, f32[256,768]{1,0:T(8,128)S(1)} %get-tuple-element.28.gy_in, f32[128,128]{1,0:T(8,128)S(1)} %get-tuple-element.35.slope_ref, bf16[256,768]{1,0:T(8,128)(2,1)S(1)} %get-tuple-element.36.fs_ref, ...), custom_call_target="tpu_custom_call" | custom-call | tf_op jit(solution)/shard_map/pallas_call | solution.py:201
  17.3 0.1 collective-permute-start.5
  17.4 1.5 %collective-permute-start.4 = (f32[128,768]{1,0:T(8,128)S(1)}, f32[128,768]{1,0:T(8,128)S(1)}, u32[]{:S(2)}, u32[]{:S(2)}) collective-permute-start(f32[128,768]{1,0:T(8,128)S(1)} %get-tuple-element.39), channel_id=1, source_target_pairs={{0,1},{1,0},{2,3},{3,2},{4,5},{5,4},{6,7},{7,6},{8,9},{9,8},{10,11... | collective-permute-start | bytes 1179656 | tf_op jit(solution)/shard_map/ppermute | solution.py:32
  18.9 1.5 %collective-permute-start.6 = (f32[128,768]{1,0:T(8,128)S(1)}, f32[128,768]{1,0:T(8,128)S(1)}, u32[]{:S(2)}, u32[]{:S(2)}) collective-permute-start(f32[128,768]{1,0:T(8,128)S(1)} %get-tuple-element.43), channel_id=1, source_target_pairs={{2,4},{6,8},{10,12},{14,16},{18,20},{22,24},{26,28},{30,0},{4,2},{... | collective-permute-start | bytes 1179656 | tf_op jit(solution)/shard_map/ppermute | solution.py:27
  20.3 0.3 %collective-permute-start.7 = (f32[1,128]{1,0:T(1,128)S(1)}, f32[1,128]{1,0:T(1,128)S(1)}, u32[]{:S(2)}, u32[]{:S(2)}) collective-permute-start(f32[1,128]{1,0:T(1,128)S(1)} %get-tuple-element.45), channel_id=1, source_target_pairs={{0,1},{1,0},{2,3},{3,2},{4,5},{5,4},{6,7},{7,6},{8,9},{9,8},{10,11... | collective-permute-start | bytes 1544 | tf_op jit(solution)/shard_map/ppermute | solution.py:32
  20.7 7.0 %collective-permute-done.7.refs_8_ = f32[1,128]{1,0:T(1,128)S(1)} collective-permute-done((f32[1,128]{1,0:T(1,128)S(1)}, f32[1,128]{1,0:T(1,128)S(1)}, u32[]{:S(2)}, u32[]{:S(2)}) %collective-permute-start.7) | collective-permute-done | bytes 544 | tf_op jit(solution)/shard_map/ppermute | solution.py:32
  27.7 0.0 collective-permute-done.5.refs_5_
  27.7 0.0 collective-permute-done.4.refs_2_
  27.7 2.6 %collective-permute-done.6.refs_6_ = f32[128,768]{1,0:T(8,128)S(1)} collective-permute-done((f32[128,768]{1,0:T(8,128)S(1)}, f32[128,768]{1,0:T(8,128)S(1)}, u32[]{:S(2)}, u32[]{:S(2)}) %collective-permute-start.6) | collective-permute-done | bytes 393248 | tf_op jit(solution)/shard_map/ppermute | solution.py:27
  30.3 1.2 %shard_map.80 = (f32[128,768]{1,0:T(8,128)}, f32[128,768]{1,0:T(8,128)}, f32[1,128]{1,0:T(1,128)}) custom-call(f32[128,768]{1,0:T(8,128)S(1)} %get-tuple-element.26.refs_0_, f32[128,768]{1,0:T(8,128)S(1)} %get-tuple-element.38.refs_1_, f32[128,768]{1,0:T(8,128)S(1)} %collective-permute-done.4.refs_2_, f32[128,768]{1,0:T(8,128)S(1)} %get-tuple-element.40.refs_3_, ...), custom_call_target="tpu_custom_call" | custom-call | tf_op jit(solution)/shard_map/pallas_call | solution.py:215
Async XLA Ops:
  0.6 4.3 %copy-start = (f32[128]{0:T(128)S(1)}, f32[128]{0:T(128)}, u32[]{:S(2)}) copy-start(f32[128]{0:T(128)} %param.9) | copy-start | bytes 1540
  0.6 5.8 %collective-permute-start = (f32[128,768]{1,0:T(8,128)}, f32[128,768]{1,0:T(8,128)S(1)}, u32[]{:S(2)}, u32[]{:S(2)}) collective-permute-start(f32[128,768]{1,0:T(8,128)} %y_any.1), channel_id=1, source_target_pairs={{0,2},{4,6},{8,10},{12,14},{16,18},{20,22},{24,26},{28,30},{2,0},{... | collective-permute-start | bytes 1179656 | tf_op jit(solution)/shard_map/ppermute | solution.py:27
  0.7 12.3 %collective-permute-start.3 = (f32[128,768]{1,0:T(8,128)}, f32[128,768]{1,0:T(8,128)S(1)}, u32[]{:S(2)}, u32[]{:S(2)}) collective-permute-start(f32[128,768]{1,0:T(8,128)} %x_any.1), channel_id=1, source_target_pairs={{0,1},{1,0},{2,3},{3,2},{4,5},{5,4},{6,7},{7,6},{8,9},{9,8},{10,11... | collective-permute-start | bytes 1179656 | tf_op jit(solution)/shard_map/ppermute | solution.py:32
  3.4 11.6 %collective-permute-start.1 = (f32[128,768]{1,0:T(8,128)}, f32[128,768]{1,0:T(8,128)S(1)}, u32[]{:S(2)}, u32[]{:S(2)}) collective-permute-start(f32[128,768]{1,0:T(8,128)} %y_any.1), channel_id=1, source_target_pairs={{2,4},{6,8},{10,12},{14,16},{18,20},{22,24},{26,28},{30,0},{4,2},{... | collective-permute-start | bytes 1179656 | tf_op jit(solution)/shard_map/ppermute | solution.py:27
  4.9 8.1 %collective-permute-start.2 = (f32[1,128]{1,0:T(1,128)S(1)}, f32[1,128]{1,0:T(1,128)S(1)}, u32[]{:S(2)}, u32[]{:S(2)}) collective-permute-start(f32[1,128]{1,0:T(1,128)S(1)} %bitcast.2), channel_id=1, source_target_pairs={{0,1},{1,0},{2,3},{3,2},{4,5},{5,4},{6,7},{7,6},{8,9},{9,8},{10,11... | collective-permute-start | bytes 1544 | tf_op jit(solution)/shard_map/ppermute | solution.py:32
  17.3 10.4 %collective-permute-start.5 = (f32[128,768]{1,0:T(8,128)S(1)}, f32[128,768]{1,0:T(8,128)S(1)}, u32[]{:S(2)}, u32[]{:S(2)}) collective-permute-start(f32[128,768]{1,0:T(8,128)S(1)} %get-tuple-element.42), channel_id=1, source_target_pairs={{0,2},{4,6},{8,10},{12,14},{16,18},{20,22},{24,26},{28,30},{2,0},{... | collective-permute-start | bytes 1179656 | tf_op jit(solution)/shard_map/ppermute | solution.py:27
  17.4 10.3 %collective-permute-start.4 = (f32[128,768]{1,0:T(8,128)S(1)}, f32[128,768]{1,0:T(8,128)S(1)}, u32[]{:S(2)}, u32[]{:S(2)}) collective-permute-start(f32[128,768]{1,0:T(8,128)S(1)} %get-tuple-element.39), channel_id=1, source_target_pairs={{0,1},{1,0},{2,3},{3,2},{4,5},{5,4},{6,7},{7,6},{8,9},{9,8},{10,11... | collective-permute-start | bytes 1179656 | tf_op jit(solution)/shard_map/ppermute | solution.py:32
  18.9 11.4 %collective-permute-start.6 = (f32[128,768]{1,0:T(8,128)S(1)}, f32[128,768]{1,0:T(8,128)S(1)}, u32[]{:S(2)}, u32[]{:S(2)}) collective-permute-start(f32[128,768]{1,0:T(8,128)S(1)} %get-tuple-element.43), channel_id=1, source_target_pairs={{2,4},{6,8},{10,12},{14,16},{18,20},{22,24},{26,28},{30,0},{4,2},{... | collective-permute-start | bytes 1179656 | tf_op jit(solution)/shard_map/ppermute | solution.py:27
  20.3 7.4 %collective-permute-start.7 = (f32[1,128]{1,0:T(1,128)S(1)}, f32[1,128]{1,0:T(1,128)S(1)}, u32[]{:S(2)}, u32[]{:S(2)}) collective-permute-start(f32[1,128]{1,0:T(1,128)S(1)} %get-tuple-element.45), channel_id=1, source_target_pairs={{0,1},{1,0},{2,3},{3,2},{4,5},{5,4},{6,7},{7,6},{8,9},{9,8},{10,11... | collective-permute-start | bytes 1544 | tf_op jit(solution)/shard_map/ppermute | solution.py:32
where the time goes:
time: 31.6 us; the launch traced here: 31.5 us
  waiting for transfers between devices  13.9 us (44%)
  starting transfers between devices  7.88 us (25%)
  Pallas kernels  7.74 us (24%)
  between operations  1.98 us (6%)
    ppermute x4, waiting for transfers between devices, shifted(): lax.ppermute(x, axis, [(i, (i + by) % length) for i in range(length)])  10.6 us
    pallas_call x4, Pallas kernels, call(): pl.pallas_call(body, out_shape=[pltpu.VMEM(o.shape, o.dtype) for o in out...  6.54 us
    ppermute x4, starting transfers between devices, shifted(): lax.ppermute(x, axis, [(i, (i + by) % length) for i in range(length)])  4.75 us
    ppermute x4, waiting for transfers between devices, swapped(): return lax.ppermute(x, axis, pairs + [(b, a) for a, b in pairs])  3.3 us
    ppermute x4, starting transfers between devices, swapped(): return lax.ppermute(x, axis, pairs + [(b, a) for a, b in pairs])  3.14 us
    pallas_call x1, Pallas kernels, finish(): pl.pallas_call(functools.partial(last_body, (len(x_terms) - 1, len(y_term...  1.2 us
  transfers between devices with their start and end apart: 8, of which 4 were waited for; matrix products, arithmetic and copies ran while one was open for 0% of the time, Pallas kernels for 14%

commit v1 on v0

v1 whole, which is shorter than its diff:
```python
import functools

import jax
import jax.numpy as jnp
from jax import lax
from jax.experimental import pallas as pl
from jax.experimental.pallas import tpu as pltpu
from jax.sharding import PartitionSpec as P


BF = jnp.bfloat16
F32 = jnp.float32
VMEM = pl.BlockSpec(memory_space=pltpu.VMEM)
SMEM = pl.BlockSpec(memory_space=pltpu.SMEM)
HBM = pl.BlockSpec(memory_space=pltpu.HBM)
CHUNKS = 4
NT = ((1,), (1,))
NN = ((1,), (0,))


def swapped(x, axis, near):
    length = lax.axis_size(axis)
    if near:
        pairs = [(i, i + 1) for i in range(0, length, 2)]
    else:
        pairs = [(i, (i + 1) % length) for i in range(1, length, 2)]
    return lax.ppermute(x, axis, pairs + [(b, a) for (a, b) in pairs])


def shifted(x, axis, by):
    length = lax.axis_size(axis)
    return lax.ppermute(x, axis, [(i, (i + by) % length) for i in range(length)])


def stacked(v):
    high = v.astype(BF)
    return jnp.concatenate([high, (v - high.astype(F32)).astype(BF)], axis=0)


def mm(a, b, dims):
    rows = a.shape[0] // 2
    deep = b.shape[0] // 2

    def one(p, q):
        return lax.dot_general(p, q, (dims, ((), ())), preferred_element_type=F32)

    both = one(a[...], b[:deep])
    return both[:rows] + (both[rows:] + one(a[:rows], b[deep:]))


def log_one_plus(t):
    series = t * (1.0 + t * (-0.5 + t * (1.0 / 3.0 + t * (-0.25 + t * 0.2))))
    return jnp.where(t < 0.03125, series, jnp.log(1.0 + t))


def gated(z, weight, diagonal=None):
    signed = z if diagonal is None else jnp.where(diagonal, -z, z)
    small = jnp.exp(-jnp.abs(signed))
    loss = jnp.maximum(signed, 0.0) + log_one_plus(small)
    slope = jnp.where(signed >= 0.0, 1.0, small) / (1.0 + small) * weight
    if diagonal is not None:
        slope = jnp.where(diagonal, -slope, slope)
    return loss, slope


def scale_of(raw):
    return lax.rsqrt(jnp.sum(raw * raw, axis=1, keepdims=True) + 1e-06)


def square(count):
    rows = lax.broadcasted_iota(jnp.int32, (count, count), 0)
    return rows == lax.broadcasted_iota(jnp.int32, (count, count), 1)


def temper_of(lt):
    return jnp.exp(jnp.full((1, 1), lt[0], F32))


def first_body(lt, bi, x_any, y_any, near_ref, w_ref, *refs):
    x_ref, xc_ref, y_ref, yc_ref, xs_ref, ys_ref, gx_ref, gy_ref, sum_ref, sem = refs
    copies = [
        pltpu.make_async_copy(x_any, x_ref, sem.at[0]),
        pltpu.make_async_copy(y_any, y_ref, sem.at[1]),
    ]
    for copy in copies:
        copy.start()
    temper = temper_of(lt)
    count = near_ref.shape[0]
    near = near_ref[...] * scale_of(near_ref[...])
    for copy, ref, scale_ref in zip(copies, (x_ref, y_ref), (xc_ref, yc_ref)):
        copy.wait()
        scale_ref[...] = scale_of(ref[...])
        ref[...] = ref[...] * scale_ref[...]
    xs_ref[...] = stacked(x_ref[...])
    ys_ref[...] = stacked(jnp.concatenate([y_ref[...], near], axis=0))
    rows = lax.broadcasted_iota(jnp.int32, (2 * count, count), 0)
    cols = lax.broadcasted_iota(jnp.int32, (2 * count, count), 1)
    z = temper * mm(ys_ref, xs_ref, NT) + bi[0]
    loss, slope = gated(z, w_ref[...] * temper, rows == cols)
    sum_ref[...] = jnp.sum(loss, axis=0, keepdims=True)
    gx_ref[...] = mm(stacked(slope.T), ys_ref, NN)
    gy_ref[...] = mm(stacked(slope), xs_ref, NN)


def second_body(others, lt, bi, *refs):
    raw_refs, refs = refs[:others], refs[others:]
    w_refs, refs = refs[:others], refs[others:]
    xs_ref, ys_ref, all_ref, refs = *refs[:3], refs[3:]
    gp_refs, refs = refs[:others], refs[others:]
    sump_refs, slope_refs = refs[:others], refs[others:]
    temper = temper_of(lt)
    count = raw_refs[0].shape[0]
    deep = (others + 1) * count
    eye = square(count)
    all_ref[:count] = xs_ref[:count]
    all_ref[deep : deep + count] = xs_ref[count:]
    for s in range(others):
        raw = raw_refs[s][...]
        px = stacked(raw * scale_of(raw))
        here = (s + 1) * count
        all_ref[here : here + count] = px[:count]
        all_ref[deep + here : deep + here + count] = px[count:]
        z = temper * mm(px, ys_ref, NT) + bi[0]
        weight = jnp.sum(jnp.where(eye, w_refs[s][...], 0.0), axis=1, keepdims=True)
        loss, slope = gated(z, weight * temper)
        sums = jnp.sum(loss, axis=1, keepdims=True)
        sump_refs[s][...] = jnp.sum(jnp.where(eye, sums, 0.0), axis=0, keepdims=True)
        slope_refs[s][...] = slope
        gp_refs[s][...] = mm(stacked(slope), ys_ref, NN)


def third_body(others, lt, bi, *refs):
    members = others + 1
    far_ref, refs = refs[0], refs[1:]
    w_refs, refs = refs[:members], refs[members:]
    all_ref, refs = refs[0], refs[1:]
    gp_in, refs = refs[:others], refs[others:]
    sum_in, refs = refs[:members], refs[members:]
    gfar_ref, refs = refs[0], refs[1:]
    gp_refs, refs = refs[:others], refs[others:]
    sum_refs, refs = refs[:members], refs[members:]
    fs_ref, slope_ref = refs
    temper = temper_of(lt)
    count = far_ref.shape[0]
    fs_ref[...] = stacked(far_ref[...])
    scale = scale_of(far_ref[...])
    z = (temper * scale) * mm(fs_ref, all_ref, NT) + bi[0]
    weight = jnp.concatenate([w[...] for w in w_refs], axis=1) * temper
    loss, slope = gated(z, weight)
    gfar_ref[...] = mm(stacked(slope), all_ref, NN)
    slope = slope * scale
    sums = jnp.sum(loss, axis=0, keepdims=True)
    for s in range(members):
        part = slice(s * count, (s + 1) * count)
        sum_refs[s][...] = sum_in[s][...] + sums[:, part]
        if s == 0:
            slope_ref[...] = slope[:, part]
        else:
            gp_refs[s - 1][...] = gp_in[s - 1][...] + mm(stacked(slope[:, part].T), fs_ref, NN)


def fourth_body(others, gx_in, gy_in, slope_ref, fs_ref, all_ref, *refs):
    slopes, (gx_ref, gown_ref, gnear_ref) = refs[:others], refs[others:]
    count = gx_in.shape[0]
    deep = (others + 1) * count
    gy = gy_in[...]
    for s in range(others):
        here = (s + 1) * count
        px = jnp.concatenate(
            [all_ref[here : here + count], all_ref[deep + here : deep + here + count]], axis=0
        )
        gy = gy + mm(stacked(slopes[s][...].T), px, NN)
    gown_ref[...] = gy[:count]
    gnear_ref[...] = gy[count:]
    gx_ref[...] = gx_in[...] + mm(stacked(slope_ref[...].T), fs_ref, NN)


def last_body(terms, lines, pairs, unit_ref, scale_ref, *refs):
    grads, refs = refs[:terms], refs[terms:]
    sums, refs = refs[:lines], refs[lines:]
    if lines:
        out_ref, loss_ref, held, sem, line = refs
    else:
        out_ref, held, sem = refs
    rows = unit_ref.shape[0] // CHUNKS
    copies = []
    if lines:
        total = sums[0][...]
        for r in sums[1:]:
            total = total + r[...]
        line[...] = total / pairs
        copies.append(pltpu.make_async_copy(line, loss_ref, sem.at[CHUNKS]))
        copies[-1].start()
    for c in range(CHUNKS):
        here = pl.ds(c * rows, rows)
        grad = grads[0][here, :]
        for r in grads[1:]:
            grad = grad + r[here, :]
        unit = unit_ref[here, :]
        inner = jnp.sum(unit * grad, axis=1, keepdims=True)
        held[here, :] = scale_ref[here, :] * (grad - unit * inner)
        copies.append(pltpu.make_async_copy(held.at[here, :], out_ref.at[here, :], sem.at[c]))
        copies[-1].start()
    for copy in copies:
        copy.wait()


def shape(*dims, kind=F32):
    return jax.ShapeDtypeStruct(dims, kind)


PARAMS = pltpu.CompilerParams(vmem_limit_bytes=16 * 1024 * 1024)


def in_hbm(args):
    return [pltpu.with_memory_space_constraint(a, pltpu.HBM) for a in args]


def in_vmem(args):
    return [pltpu.with_memory_space_constraint(a, pltpu.VMEM) for a in args]


def call(body, outs, scalars, *args, scratch=(), anywhere=0):
    return pl.pallas_call(
        body,
        out_shape=[pltpu.VMEM(o.shape, o.dtype) for o in outs],
        in_specs=[SMEM] * len(scalars) + [HBM] * anywhere + [VMEM] * (len(args) - anywhere),
        out_specs=[VMEM] * len(outs),
        scratch_shapes=list(scratch),
        compiler_params=PARAMS,
    )(*scalars, *in_hbm(args[:anywhere]), *in_vmem(args[anywhere:]))


def finish(unit, scale, grads, sums=(), pairs=None):
    full = shape(*unit.shape)
    line = shape(1, unit.shape[0])
    args = [unit, scale, *grads, *sums]
    extra = [pltpu.VMEM(line.shape, F32)] if sums else []
    outs = [full, line] if sums else [full]
    return pl.pallas_call(
        functools.partial(last_body, len(grads), len(sums), pairs),
        out_shape=outs,
        in_specs=[VMEM] * len(args),
        out_specs=[HBM] * len(outs),
        scratch_shapes=[
            pltpu.VMEM(full.shape, F32),
            pltpu.SemaphoreType.DMA((CHUNKS + 1,)),
            *extra,
        ],
        compiler_params=PARAMS,
    )(*in_vmem(args))


def body(images, texts, log_temp, bias, row_weight):
    members = lax.axis_size("grp")
    others = members - 1
    count, width = images.shape
    weight = row_weight.reshape(1, count)
    scalars = (log_temp, bias)
    raws = [shifted(images, "grp", -s) for s in range(1, members)]
    far = swapped(texts, "blk", False)
    near = swapped(texts, "blk", True)
    weights = [weight] + [shifted(weight, "grp", -s) for s in range(1, members)]
    full = shape(count, width)
    line = shape(1, count)
    stack = shape(2 * count, width, kind=BF)
    unit_x, scale_x, unit_y, scale_y, xs, ys, gx, gy, sums = call(
        first_body,
        [
            full,
            shape(count, 1),
            full,
            shape(count, 1),
            stack,
            shape(4 * count, width, kind=BF),
            full,
            shape(2 * count, width),
            line,
        ],
        scalars,
        images,
        texts,
        near,
        weight,
        scratch=[pltpu.SemaphoreType.DMA((2,))],
        anywhere=2,
    )
    outs = call(
        functools.partial(second_body, others),
        [shape(2 * members * count, width, kind=BF)]
        + [full] * others
        + [line] * others
        + [shape(count, 2 * count)] * others,
        scalars,
        *raws,
        *weights[1:],
        xs,
        ys,
    )
    everyone, outs = outs[0], outs[1:]
    gp, outs = outs[:others], outs[others:]
    sump, slopes = outs[:others], outs[others:]
    outs = call(
        functools.partial(third_body, others),
        [full] + [full] * others + [line] * members + [stack, shape(count, count)],
        scalars,
        far,
        *weights,
        everyone,
        *gp,
        sums,
        *sump,
    )
    g_far, outs = outs[0], outs[1:]
    gp, outs = outs[:others], outs[others:]
    sums, (fs, slope) = outs[:members], outs[members:]
    back_far = swapped(g_far, "blk", False)
    back_x = [shifted(gp[s - 1], "grp", s) for s in range(1, members)]
    back_sum = [shifted(sums[s], "grp", s) for s in range(1, members)]
    gx, g_own, g_near = call(
        functools.partial(fourth_body, others),
        [full] * 3,
        (),
        gx,
        gy,
        slope,
        fs,
        everyone,
        *slopes,
    )
    back_near = swapped(g_near, "blk", True)
    pairs = 3.0 * members * count
    grad_x, row_loss = finish(unit_x, scale_x, [gx, *back_x], [sums[0], *back_sum], pairs)
    (grad_y,) = finish(unit_y, scale_y, [g_own, back_near, back_far])
    return (row_loss.reshape(count), grad_x, grad_y)


def solution(mesh):
    placed = (P(("blk", "grp"), None), P(("blk", "grp"), None), P(), P(), P(("blk", "grp")))
    return jax.shard_map(
        body,
        mesh=mesh,
        in_specs=placed,
        out_specs=(P(("blk", "grp")), P(("blk", "grp"), None), P(("blk", "grp"), None)),
        check_vma=False,
    )
```

time: 31.6 us -> 31.3 us (level); the launches traced: 31.5 us -> 30.8 us
  waiting for transfers between devices: 13.9 us -> 13.1 us
  Pallas kernels: 7.74 us -> 8.07 us
    ppermute x4, waiting for transfers between devices: 10.6 us -> 3.39 us  [shifted(): lax.ppermute(x, axis, [(i, (i + by) % length) for i in range(length)])]
    ppermute x4, waiting for transfers between devices: 3.3 us -> 9.71 us  [swapped(): return lax.ppermute(x, axis, pairs + [(b, a) for a, b in pairs])]
    pallas_call x1 -> x2, Pallas kernels: 1.2 us -> 1.91 us  [finish(): pl.pallas_call(functools.partial(last_body, len(grads), len(sums), pairs)...]
    pallas_call x4, Pallas kernels: 6.54 us -> 6.16 us  [call(): pl.pallas_call(body, out_shape=[pltpu.VMEM(o.shape, o.dtype) for o in out...]
    ppermute x4, starting transfers between devices: 4.75 us -> 4.41 us  [shifted(): lax.ppermute(x, axis, [(i, (i + by) % length) for i in range(length)])]
  transfers between devices with their start and end apart: 8 -> 8, of which waited for: 4 -> 3; matrix products, arithmetic and copies ran while one was open for 0% -> 0% of each run, Pallas kernels for 14% -> 17%
where the time goes in v1:
time: 31.3 us; the launch traced here: 30.8 us
  waiting for transfers between devices  13.1 us (42%)
  Pallas kernels  8.07 us (26%)
  starting transfers between devices  7.59 us (24%)
  between operations  2.01 us (6%)
    ppermute x4, waiting for transfers between devices, swapped(): return lax.ppermute(x, axis, pairs + [(b, a) for a, b in pairs])  9.71 us
    pallas_call x4, Pallas kernels, call(): pl.pallas_call(body, out_shape=[pltpu.VMEM(o.shape, o.dtype) for o in out...  6.16 us
    ppermute x4, starting transfers between devices, shifted(): lax.ppermute(x, axis, [(i, (i + by) % length) for i in range(length)])  4.41 us
    ppermute x4, waiting for transfers between devices, shifted(): lax.ppermute(x, axis, [(i, (i + by) % length) for i in range(length)])  3.39 us
    ppermute x4, starting transfers between devices, swapped(): return lax.ppermute(x, axis, pairs + [(b, a) for a, b in pairs])  3.19 us
    pallas_call x2, Pallas kernels, finish(): pl.pallas_call(functools.partial(last_body, len(grads), len(sums), pairs)...  1.91 us
  transfers between devices with their start and end apart: 8, of which 3 were waited for; matrix products, arithmetic and copies ran while one was open for 0% of the time, Pallas kernels for 17%

profile of v1, /device:TPU:1, one launch (start us, length us, event | category | flops | bytes accessed | tf_op | source)
XLA Modules:
  0.0 30.8 jit_solution(3453274681505264790)
XLA Ops:
  0.6 0.0 copy-start
  0.6 0.1 collective-permute-start
  0.7 2.7 %collective-permute-start.3 = (f32[128,768]{1,0:T(8,128)}, f32[128,768]{1,0:T(8,128)S(1)}, u32[]{:S(2)}, u32[]{:S(2)}) collective-permute-start(f32[128,768]{1,0:T(8,128)} %x_any.1), channel_id=1, source_target_pairs={{0,1},{1,0},{2,3},{3,2},{4,5},{5,4},{6,7},{7,6},{8,9},{9,8},{10,11... | collective-permute-start | bytes 1179656 | tf_op jit(solution)/shard_map/ppermute | solution.py:32
  3.4 1.5 %collective-permute-start.1 = (f32[128,768]{1,0:T(8,128)}, f32[128,768]{1,0:T(8,128)S(1)}, u32[]{:S(2)}, u32[]{:S(2)}) collective-permute-start(f32[128,768]{1,0:T(8,128)} %y_any.1), channel_id=1, source_target_pairs={{2,4},{6,8},{10,12},{14,16},{18,20},{22,24},{26,28},{30,0},{4,2},{... | collective-permute-start | bytes 1179656 | tf_op jit(solution)/shard_map/ppermute | solution.py:27
  4.9 0.0 copy-done
  4.9 0.3 collective-permute-start.2
  6.4 0.0 collective-permute-done.near_ref
  6.5 3.2 %shard_map.76 = (f32[128,768]{1,0:T(8,128)S(1)}, f32[128,1]{1,0:T(8,128)S(1)}, f32[128,768]{1,0:T(8,128)S(1)}, f32[128,1]{1,0:T(8,128)S(1)}, bf16[256,768]{1,0:T...) custom-call(f32[1]{0:T(128)S(6)} %copy.8.lt, ...), custom_call_target="tpu_custom_call" | custom-call | tf_op jit(solution)/shard_map/pallas_call | solution.py:224
  9.7 3.4 %collective-permute-done.2.refs_1_.refs_2_ = f32[1,128]{1,0:T(1,128)S(1)} collective-permute-done((f32[1,128]{1,0:T(1,128)S(1)}, f32[1,128]{1,0:T(1,128)S(1)}, u32[]{:S(2)}, u32[]{:S(2)}) %collective-permute-start.2) | collective-permute-done | bytes 544 | tf_op jit(solution)/shard_map/ppermute | solution.py:32
  13.0 0.0 collective-permute-done.3.refs_0_
  13.0 1.0 %shard_map.77 = (bf16[512,768]{1,0:T(8,128)(2,1)S(1)}, f32[128,768]{1,0:T(8,128)S(1)}, f32[1,128]{1,0:T(1,128)S(1)}, f32[128,256]{1,0:T(8,128)S(1)}) custom-call(f32[1]{0:T(128)S(6)} %copy.8.lt, f32[1]{0:T(128)S(6)} %copy.9.bi, f32[128,768]{1,0:T(8,128)S(1)} %collective-permute-done.3.refs_0_, f32[1,128]{1,0:T(1,128)S(1)} %collective-permute-done.2.refs_1_.refs_2_, ...), custom_call_target="tpu_custom_call" | custom-call | tf_op jit(solution)/shard_map/pallas_call | solution.py:224
  14.1 1.0 %collective-permute-done.1.refs_0_ = f32[128,768]{1,0:T(8,128)S(1)} collective-permute-done((f32[128,768]{1,0:T(8,128)}, f32[128,768]{1,0:T(8,128)S(1)}, u32[]{:S(2)}, u32[]{:S(2)}) %collective-permute-start.1) | collective-permute-done | bytes 393248 | tf_op jit(solution)/shard_map/ppermute | solution.py:27
  15.0 1.3 %shard_map.78 = (f32[128,768]{1,0:T(8,128)S(1)}, f32[128,768]{1,0:T(8,128)S(1)}, f32[1,128]{1,0:T(1,128)S(1)}, f32[1,128]{1,0:T(1,128)S(1)}, bf16[256,768]{1,0:T(8,128)(2,1)S(1)}, /*index=5*/f32[128,128]{1,0:T(8,128)S(1)}) custom-call(f32[1]{0:T(128)S(6)} %copy.8.lt, f32[1]{0:T(128)S(6)} %copy.9.bi, f32[128,768]{1,0:T(8,128)S(1)} %collective-permute-done.1.refs_0_, ...), custom_call_target="tpu_custom_call" | custom-call | tf_op jit(solution)/shard_map/pallas_call | solution.py:224
  16.3 0.7 %shard_map.79 = (f32[128,768]{1,0:T(8,128)S(1)}, f32[128,768]{1,0:T(8,128)S(1)}, f32[128,768]{1,0:T(8,128)S(1)}) custom-call(f32[128,768]{1,0:T(8,128)S(1)} %get-tuple-element.29.gx_in, f32[256,768]{1,0:T(8,128)S(1)} %get-tuple-element.30.gy_in, f32[128,128]{1,0:T(8,128)S(1)} %get-tuple-element.37.slope_ref, bf16[256,768]{1,0:T(8,128)(2,1)S(1)} %get-tuple-element.38.fs_ref, ...), custom_call_target="tpu_custom_call" | custom-call | tf_op jit(solution)/shard_map/pallas_call | solution.py:224
  17.0 0.1 collective-permute-start.6
  17.1 1.5 %collective-permute-start.7 = (f32[128,768]{1,0:T(8,128)S(1)}, f32[128,768]{1,0:T(8,128)S(1)}, u32[]{:S(2)}, u32[]{:S(2)}) collective-permute-start(f32[128,768]{1,0:T(8,128)S(1)} %get-tuple-element.50), channel_id=1, source_target_pairs={{2,4},{6,8},{10,12},{14,16},{18,20},{22,24},{26,28},{30,0},{4,2},{... | collective-permute-start | bytes 1179656 | tf_op jit(solution)/shard_map/ppermute | solution.py:27
  18.6 0.9 %collective-permute-start.4 = (f32[128,768]{1,0:T(8,128)S(1)}, f32[128,768]{1,0:T(8,128)S(1)}, u32[]{:S(2)}, u32[]{:S(2)}) collective-permute-start(f32[128,768]{1,0:T(8,128)S(1)} %get-tuple-element.41), channel_id=1, source_target_pairs={{0,1},{1,0},{2,3},{3,2},{4,5},{5,4},{6,7},{7,6},{8,9},{9,8},{10,11... | collective-permute-start | bytes 1179656 | tf_op jit(solution)/shard_map/ppermute | solution.py:32
  19.5 0.6 %collective-permute-start.5 = (f32[1,128]{1,0:T(1,128)S(1)}, f32[1,128]{1,0:T(1,128)S(1)}, u32[]{:S(2)}, u32[]{:S(2)}) collective-permute-start(f32[1,128]{1,0:T(1,128)S(1)} %get-tuple-element.43), channel_id=1, source_target_pairs={{0,1},{1,0},{2,3},{3,2},{4,5},{5,4},{6,7},{7,6},{8,9},{9,8},{10,11... | collective-permute-start | bytes 1544 | tf_op jit(solution)/shard_map/ppermute | solution.py:32
  20.1 0.0 collective-permute-done.6.refs_1_
  20.1 8.8 %collective-permute-done.7.refs_2_ = f32[128,768]{1,0:T(8,128)S(1)} collective-permute-done((f32[128,768]{1,0:T(8,128)S(1)}, f32[128,768]{1,0:T(8,128)S(1)}, u32[]{:S(2)}, u32[]{:S(2)}) %collective-permute-start.7) | collective-permute-done | bytes 393248 | tf_op jit(solution)/shard_map/ppermute | solution.py:27
  28.8 1.0 %shard_map.81 = f32[128,768]{1,0:T(8,128)} custom-call(f32[128,768]{1,0:T(8,128)S(1)} %get-tuple-element.46.unit_ref, f32[128,1]{1,0:T(8,128)S(1)} %get-tuple-element.47.scale_ref, f32[128,768]{1,0:T(8,128)S(1)} %get-tuple-element.48.refs_0_, f32[128,768]{1,0:T(8,128)S(1)} %collective-permute-done.6.refs_1_, f32[128,768]{1,0:T(8,128)S(1)} %collective-permute-done.7.refs_2_), custom_call_target="tpu_custom_call" | custom-call | tf_op jit(solution)/shard_map/pallas_call | solution.py:240
  29.8 0.0 collective-permute-done.5.refs_3_
  29.8 0.0 collective-permute-done.4.refs_1_
  29.8 0.9 %shard_map.80 = (f32[128,768]{1,0:T(8,128)}, f32[1,128]{1,0:T(1,128)}) custom-call(f32[128,768]{1,0:T(8,128)S(1)} %get-tuple-element.27.unit_ref, f32[128,1]{1,0:T(8,128)S(1)} %get-tuple-element.28.scale_ref, f32[128,768]{1,0:T(8,128)S(1)} %get-tuple-element.40.refs_0_, f32[128,768]{1,0:T(8,128)S(1)} %collective-permute-done.4.refs_1_, ...), custom_call_target="tpu_custom_call" | custom-call | tf_op jit(solution)/shard_map/pallas_call | solution.py:240
Async XLA Ops:
  0.6 4.3 %copy-start = (f32[128]{0:T(128)S(1)}, f32[128]{0:T(128)}, u32[]{:S(2)}) copy-start(f32[128]{0:T(128)} %param.9) | copy-start | bytes 1540
  0.6 5.8 %collective-permute-start = (f32[128,768]{1,0:T(8,128)}, f32[128,768]{1,0:T(8,128)S(1)}, u32[]{:S(2)}, u32[]{:S(2)}) collective-permute-start(f32[128,768]{1,0:T(8,128)} %y_any.1), channel_id=1, source_target_pairs={{0,2},{4,6},{8,10},{12,14},{16,18},{20,22},{24,26},{28,30},{2,0},{... | collective-permute-start | bytes 1179656 | tf_op jit(solution)/shard_map/ppermute | solution.py:27
  0.7 12.3 %collective-permute-start.3 = (f32[128,768]{1,0:T(8,128)}, f32[128,768]{1,0:T(8,128)S(1)}, u32[]{:S(2)}, u32[]{:S(2)}) collective-permute-start(f32[128,768]{1,0:T(8,128)} %x_any.1), channel_id=1, source_target_pairs={{0,1},{1,0},{2,3},{3,2},{4,5},{5,4},{6,7},{7,6},{8,9},{9,8},{10,11... | collective-permute-start | bytes 1179656 | tf_op jit(solution)/shard_map/ppermute | solution.py:32
  3.4 11.6 %collective-permute-start.1 = (f32[128,768]{1,0:T(8,128)}, f32[128,768]{1,0:T(8,128)S(1)}, u32[]{:S(2)}, u32[]{:S(2)}) collective-permute-start(f32[128,768]{1,0:T(8,128)} %y_any.1), channel_id=1, source_target_pairs={{2,4},{6,8},{10,12},{14,16},{18,20},{22,24},{26,28},{30,0},{4,2},{... | collective-permute-start | bytes 1179656 | tf_op jit(solution)/shard_map/ppermute | solution.py:27
  4.9 8.1 %collective-permute-start.2 = (f32[1,128]{1,0:T(1,128)S(1)}, f32[1,128]{1,0:T(1,128)S(1)}, u32[]{:S(2)}, u32[]{:S(2)}) collective-permute-start(f32[1,128]{1,0:T(1,128)S(1)} %bitcast.2), channel_id=1, source_target_pairs={{0,1},{1,0},{2,3},{3,2},{4,5},{5,4},{6,7},{7,6},{8,9},{9,8},{10,11... | collective-permute-start | bytes 1544 | tf_op jit(solution)/shard_map/ppermute | solution.py:32
  17.0 3.1 %collective-permute-start.6 = (f32[128,768]{1,0:T(8,128)S(1)}, f32[128,768]{1,0:T(8,128)S(1)}, u32[]{:S(2)}, u32[]{:S(2)}) collective-permute-start(f32[128,768]{1,0:T(8,128)S(1)} %get-tuple-element.49), channel_id=1, source_target_pairs={{0,2},{4,6},{8,10},{12,14},{16,18},{20,22},{24,26},{28,30},{2,0},{... | collective-permute-start | bytes 1179656 | tf_op jit(solution)/shard_map/ppermute | solution.py:27
  17.1 11.8 %collective-permute-start.7 = (f32[128,768]{1,0:T(8,128)S(1)}, f32[128,768]{1,0:T(8,128)S(1)}, u32[]{:S(2)}, u32[]{:S(2)}) collective-permute-start(f32[128,768]{1,0:T(8,128)S(1)} %get-tuple-element.50), channel_id=1, source_target_pairs={{2,4},{6,8},{10,12},{14,16},{18,20},{22,24},{26,28},{30,0},{4,2},{... | collective-permute-start | bytes 1179656 | tf_op jit(solution)/shard_map/ppermute | solution.py:27
  18.6 11.2 %collective-permute-start.4 = (f32[128,768]{1,0:T(8,128)S(1)}, f32[128,768]{1,0:T(8,128)S(1)}, u32[]{:S(2)}, u32[]{:S(2)}) collective-permute-start(f32[128,768]{1,0:T(8,128)S(1)} %get-tuple-element.41), channel_id=1, source_target_pairs={{0,1},{1,0},{2,3},{3,2},{4,5},{5,4},{6,7},{7,6},{8,9},{9,8},{10,11... | collective-permute-start | bytes 1179656 | tf_op jit(solution)/shard_map/ppermute | solution.py:32
  19.5 10.3 %collective-permute-start.5 = (f32[1,128]{1,0:T(1,128)S(1)}, f32[1,128]{1,0:T(1,128)S(1)}, u32[]{:S(2)}, u32[]{:S(2)}) collective-permute-start(f32[1,128]{1,0:T(1,128)S(1)} %get-tuple-element.43), channel_id=1, source_target_pairs={{0,1},{1,0},{2,3},{3,2},{4,5},{5,4},{6,7},{7,6},{8,9},{9,8},{10,11... | collective-permute-start | bytes 1544 | tf_op jit(solution)/shard_map/ppermute | solution.py:32

commit v2 on v1

--- a/solution.py
+++ b/solution.py
@@ -18,13 +18,13 @@
 NN = ((1,), (0,))
 
 
-def swapped(x, axis, near):
-    length = lax.axis_size(axis)
-    if near:
-        pairs = [(i, i + 1) for i in range(0, length, 2)]
-    else:
-        pairs = [(i, (i + 1) % length) for i in range(1, length, 2)]
+def exchanged(x, axis, pairs):
     return lax.ppermute(x, axis, pairs + [(b, a) for (a, b) in pairs])
+
+
+def far_pairs(length):
+    pairs = [(i, (i + 1) % length) for i in range(1, length, 2)]
+    return [pairs[0::2], pairs[1::2]]
 
 
 def shifted(x, axis, by):
@@ -131,7 +131,7 @@
 
 def third_body(others, lt, bi, *refs):
     members = others + 1
-    far_ref, refs = refs[0], refs[1:]
+    early_ref, late_ref, refs = *refs[:2], refs[2:]
     w_refs, refs = refs[:members], refs[members:]
     all_ref, refs = refs[0], refs[1:]
     gp_in, refs = refs[:others], refs[others:]
@@ -141,9 +141,10 @@
     sum_refs, refs = refs[:members], refs[members:]
     fs_ref, slope_ref = refs
     temper = temper_of(lt)
-    count = far_ref.shape[0]
-    fs_ref[...] = stacked(far_ref[...])
-    scale = scale_of(far_ref[...])
+    count = early_ref.shape[0]
+    far = early_ref[...] + late_ref[...]
+    fs_ref[...] = stacked(far)
+    scale = scale_of(far)
     z = (temper * scale) * mm(fs_ref, all_ref, NT) + bi[0]
     weight = jnp.concatenate([w[...] for w in w_refs], axis=1) * temper
     loss, slope = gated(z, weight)
@@ -257,9 +258,13 @@
     count, width = images.shape
     weight = row_weight.reshape(1, count)
     scalars = (log_temp, bias)
+    length = lax.axis_size("blk")
+    near_pairs = [(i, i + 1) for i in range(0, length, 2)]
+    early, late = far_pairs(length)
+    far_early = exchanged(texts, "blk", early)
     raws = [shifted(images, "grp", -s) for s in range(1, members)]
-    far = swapped(texts, "blk", False)
-    near = swapped(texts, "blk", True)
+    far_late = exchanged(texts, "blk", late)
+    near = exchanged(texts, "blk", near_pairs)
     weights = [weight] + [shifted(weight, "grp", -s) for s in range(1, members)]
     full = shape(count, width)
     line = shape(1, count)
@@ -304,7 +309,8 @@
         functools.partial(third_body, others),
         [full] + [full] * others + [line] * members + [stack, shape(count, count)],
         scalars,
-        far,
+        far_early,
+        far_late,
         *weights,
         everyone,
         *gp,
@@ -314,8 +320,9 @@
     g_far, outs = outs[0], outs[1:]
     gp, outs = outs[:others], outs[others:]
     sums, (fs, slope) = outs[:members], outs[members:]
-    back_far = swapped(g_far, "blk", False)
+    back_early = exchanged(g_far, "blk", early)
     back_x = [shifted(gp[s - 1], "grp", s) for s in range(1, members)]
+    back_late = exchanged(g_far, "blk", late)
     back_sum = [shifted(sums[s], "grp", s) for s in range(1, members)]
     gx, g_own, g_near = call(
         functools.partial(fourth_body, others),
@@ -328,10 +335,10 @@
         everyone,
         *slopes,
     )
-    back_near = swapped(g_near, "blk", True)
+    back_near = exchanged(g_near, "blk", near_pairs)
     pairs = 3.0 * members * count
     grad_x, row_loss = finish(unit_x, scale_x, [gx, *back_x], [sums[0], *back_sum], pairs)
-    (grad_y,) = finish(unit_y, scale_y, [g_own, back_near, back_far])
+    (grad_y,) = finish(unit_y, scale_y, [g_own, back_near, back_early, back_late])
     return (row_loss.reshape(count), grad_x, grad_y)
 
 

time: 31.3 us -> 35.9 us (1.15)
  the two profiles are of different devices: /device:TPU:1 before, /device:TPU:0 now
where the time goes in v2:
time: 35.9 us; the launch traced here: 35.7 us
  starting transfers between devices  20.4 us (57%)
  Pallas kernels  8.09 us (23%)
  waiting for transfers between devices  5.1 us (14%)
  between operations  2.05 us (6%)
    ppermute x6, starting transfers between devices, exchanged(): return lax.ppermute(x, axis, pairs + [(b, a) for a, b in pairs])  15.2 us
    pallas_call x4, Pallas kernels, call(): pl.pallas_call(body, out_shape=[pltpu.VMEM(o.shape, o.dtype) for o in out...  6.16 us
    ppermute x4, starting transfers between devices, shifted(): lax.ppermute(x, axis, [(i, (i + by) % length) for i in range(length)])  5.24 us
    ppermute x6, waiting for transfers between devices, exchanged(): return lax.ppermute(x, axis, pairs + [(b, a) for a, b in pairs])  3.46 us
    pallas_call x2, Pallas kernels, finish(): pl.pallas_call(functools.partial(last_body, len(grads), len(sums), pairs)...  1.93 us
    ppermute x4, waiting for transfers between devices, shifted(): lax.ppermute(x, axis, [(i, (i + by) % length) for i in range(length)])  1.64 us
  transfers between devices with their start and end apart: 10, of which 2 were waited for; matrix products, arithmetic and copies ran while one was open for 0% of the time, Pallas kernels for 15%

profile of v2, /device:TPU:0, one launch (start us, length us, event | category | flops | bytes accessed | tf_op | source)
XLA Modules:
  0.0 35.7 jit_solution(12213117599330166829)
XLA Ops:
  0.6 0.0 copy-start
  0.6 0.6 %collective-permute-start = (f32[128,768]{1,0:T(8,128)}, f32[128,768]{1,0:T(8,128)S(1)}, u32[]{:S(2)}, u32[]{:S(2)}) collective-permute-start(f32[128,768]{1,0:T(8,128)} %y_any.1), channel_id=1, source_target_pairs={{0,2},{4,6},{8,10},{12,14},{16,18},{20,22},{24,26},{28,30},{2,0},{... | collective-permute-start | bytes 1179656 | tf_op jit(solution)/shard_map/ppermute | solution.py:22
  1.2 2.6 %collective-permute-start.4 = (f32[128,768]{1,0:T(8,128)}, f32[128,768]{1,0:T(8,128)S(1)}, u32[]{:S(2)}, u32[]{:S(2)}) collective-permute-start(f32[128,768]{1,0:T(8,128)} %x_any.1), channel_id=1, source_target_pairs={{0,1},{1,0},{2,3},{3,2},{4,5},{5,4},{6,7},{7,6},{8,9},{9,8},{10,11... | collective-permute-start | bytes 1179656 | tf_op jit(solution)/shard_map/ppermute | solution.py:32
  3.8 0.7 %collective-permute-start.1 = (f32[128,768]{1,0:T(8,128)}, f32[128,768]{1,0:T(8,128)S(1)}, u32[]{:S(2)}, u32[]{:S(2)}) collective-permute-start(f32[128,768]{1,0:T(8,128)} %y_any.1), channel_id=1, source_target_pairs={{2,4},{10,12},{18,20},{26,28},{4,2},{12,10},{20,18},{28,26},{3,5},... | collective-permute-start | bytes 1179656 | tf_op jit(solution)/shard_map/ppermute | solution.py:22
  4.4 6.2 %collective-permute-start.2 = (f32[128,768]{1,0:T(8,128)}, f32[128,768]{1,0:T(8,128)S(1)}, u32[]{:S(2)}, u32[]{:S(2)}) collective-permute-start(f32[128,768]{1,0:T(8,128)} %y_any.1), channel_id=1, source_target_pairs={{6,8},{14,16},{22,24},{30,0},{8,6},{16,14},{24,22},{0,30},{7,9},{1... | collective-permute-start | bytes 1179656 | tf_op jit(solution)/shard_map/ppermute | solution.py:22
  10.7 0.0 copy-done
  10.7 0.6 %collective-permute-start.3 = (f32[1,128]{1,0:T(1,128)S(1)}, f32[1,128]{1,0:T(1,128)S(1)}, u32[]{:S(2)}, u32[]{:S(2)}) collective-permute-start(f32[1,128]{1,0:T(1,128)S(1)} %bitcast.2), channel_id=1, source_target_pairs={{0,1},{1,0},{2,3},{3,2},{4,5},{5,4},{6,7},{7,6},{8,9},{9,8},{10,11... | collective-permute-start | bytes 1544 | tf_op jit(solution)/shard_map/ppermute | solution.py:32
  12.6 0.0 collective-permute-done.near_ref
  12.6 3.2 %shard_map.76 = (f32[128,768]{1,0:T(8,128)S(1)}, f32[128,1]{1,0:T(8,128)S(1)}, f32[128,768]{1,0:T(8,128)S(1)}, f32[128,1]{1,0:T(8,128)S(1)}, bf16[256,768]{1,0:T...) custom-call(f32[1]{0:T(128)S(6)} %copy.8.lt, ...), custom_call_target="tpu_custom_call" | custom-call | tf_op jit(solution)/shard_map/pallas_call | solution.py:225
  15.8 0.0 collective-permute-done.3.refs_1_.refs_3_
  15.8 0.0 collective-permute-done.4.refs_0_
  15.8 1.0 %shard_map.77 = (bf16[512,768]{1,0:T(8,128)(2,1)S(1)}, f32[128,768]{1,0:T(8,128)S(1)}, f32[1,128]{1,0:T(1,128)S(1)}, f32[128,256]{1,0:T(8,128)S(1)}) custom-call(f32[1]{0:T(128)S(6)} %copy.8.lt, f32[1]{0:T(128)S(6)} %copy.9.bi, f32[128,768]{1,0:T(8,128)S(1)} %collective-permute-done.4.refs_0_, f32[1,128]{1,0:T(1,128)S(1)} %collective-permute-done.3.refs_1_.refs_3_, ...), custom_call_target="tpu_custom_call" | custom-call | tf_op jit(solution)/shard_map/pallas_call | solution.py:225
  16.8 0.0 collective-permute-done.1.refs_0_
  16.9 0.0 collective-permute-done.2.refs_1_
  16.9 1.3 %shard_map.78 = (f32[128,768]{1,0:T(8,128)S(1)}, f32[128,768]{1,0:T(8,128)S(1)}, f32[1,128]{1,0:T(1,128)S(1)}, f32[1,128]{1,0:T(1,128)S(1)}, bf16[256,768]{1,0:T(8,128)(2,1)S(1)}, /*index=5*/f32[128,128]{1,0:T(8,128)S(1)}) custom-call(f32[1]{0:T(128)S(6)} %copy.8.lt, f32[1]{0:T(128)S(6)} %copy.9.bi, f32[128,768]{1,0:T(8,128)S(1)} %collective-permute-done.1.refs_0_, ...), custom_call_target="tpu_custom_call" | custom-call | tf_op jit(solution)/shard_map/pallas_call | solution.py:225
  18.1 0.7 %shard_map.79 = (f32[128,768]{1,0:T(8,128)S(1)}, f32[128,768]{1,0:T(8,128)S(1)}, f32[128,768]{1,0:T(8,128)S(1)}) custom-call(f32[128,768]{1,0:T(8,128)S(1)} %get-tuple-element.29.gx_in, f32[256,768]{1,0:T(8,128)S(1)} %get-tuple-element.30.gy_in, f32[128,128]{1,0:T(8,128)S(1)} %get-tuple-element.37.slope_ref, bf16[256,768]{1,0:T(8,128)(2,1)S(1)} %get-tuple-element.38.fs_ref, ...), custom_call_target="tpu_custom_call" | custom-call | tf_op jit(solution)/shard_map/pallas_call | solution.py:225
  18.8 0.6 %collective-permute-start.7 = (f32[128,768]{1,0:T(8,128)S(1)}, f32[128,768]{1,0:T(8,128)S(1)}, u32[]{:S(2)}, u32[]{:S(2)}) collective-permute-start(f32[128,768]{1,0:T(8,128)S(1)} %get-tuple-element.49), channel_id=1, source_target_pairs={{0,2},{4,6},{8,10},{12,14},{16,18},{20,22},{24,26},{28,30},{2,0},{... | collective-permute-start | bytes 1179656 | tf_op jit(solution)/shard_map/ppermute | solution.py:22
  19.4 0.7 %collective-permute-start.8 = (f32[128,768]{1,0:T(8,128)S(1)}, f32[128,768]{1,0:T(8,128)S(1)}, u32[]{:S(2)}, u32[]{:S(2)}) collective-permute-start(f32[128,768]{1,0:T(8,128)S(1)} %get-tuple-element.50), channel_id=1, source_target_pairs={{2,4},{10,12},{18,20},{26,28},{4,2},{12,10},{20,18},{28,26},{3,5},... | collective-permute-start | bytes 1179656 | tf_op jit(solution)/shard_map/ppermute | solution.py:22
  20.1 6.4 %collective-permute-start.9 = (f32[128,768]{1,0:T(8,128)S(1)}, f32[128,768]{1,0:T(8,128)S(1)}, u32[]{:S(2)}, u32[]{:S(2)}) collective-permute-start(f32[128,768]{1,0:T(8,128)S(1)} %get-tuple-element.50), channel_id=1, source_target_pairs={{6,8},{14,16},{22,24},{30,0},{8,6},{16,14},{24,22},{0,30},{7,9},{1... | collective-permute-start | bytes 1179656 | tf_op jit(solution)/shard_map/ppermute | solution.py:22
  26.5 0.6 %collective-permute-start.5 = (f32[128,768]{1,0:T(8,128)S(1)}, f32[128,768]{1,0:T(8,128)S(1)}, u32[]{:S(2)}, u32[]{:S(2)}) collective-permute-start(f32[128,768]{1,0:T(8,128)S(1)} %get-tuple-element.41), channel_id=1, source_target_pairs={{0,1},{1,0},{2,3},{3,2},{4,5},{5,4},{6,7},{7,6},{8,9},{9,8},{10,11... | collective-permute-start | bytes 1179656 | tf_op jit(solution)/shard_map/ppermute | solution.py:32
  27.1 1.5 %collective-permute-start.6 = (f32[1,128]{1,0:T(1,128)S(1)}, f32[1,128]{1,0:T(1,128)S(1)}, u32[]{:S(2)}, u32[]{:S(2)}) collective-permute-start(f32[1,128]{1,0:T(1,128)S(1)} %get-tuple-element.43), channel_id=1, source_target_pairs={{0,1},{1,0},{2,3},{3,2},{4,5},{5,4},{6,7},{7,6},{8,9},{9,8},{10,11... | collective-permute-start | bytes 1544 | tf_op jit(solution)/shard_map/ppermute | solution.py:32
  28.6 0.0 collective-permute-done.7.refs_1_
  28.6 0.0 collective-permute-done.8.refs_2_
  28.6 3.4 %collective-permute-done.9.refs_3_ = f32[128,768]{1,0:T(8,128)S(1)} collective-permute-done((f32[128,768]{1,0:T(8,128)S(1)}, f32[128,768]{1,0:T(8,128)S(1)}, u32[]{:S(2)}, u32[]{:S(2)}) %collective-permute-start.9) | collective-permute-done | bytes 393248 | tf_op jit(solution)/shard_map/ppermute | solution.py:22
  32.1 1.0 %shard_map.81 = f32[128,768]{1,0:T(8,128)} custom-call(f32[128,768]{1,0:T(8,128)S(1)} %get-tuple-element.46.unit_ref, f32[128,1]{1,0:T(8,128)S(1)} %get-tuple-element.47.scale_ref, f32[128,768]{1,0:T(8,128)S(1)} %get-tuple-element.48.refs_0_, f32[128,768]{1,0:T(8,128)S(1)} %collective-permute-done.7.refs_1_, f32[128,768]{1,0:T(8,128)S(1)} %collective-permute-done.8.refs_2_, ...), custom_call_target="tpu_custom_call" | custom-call | tf_op jit(solution)/shard_map/pallas_call | solution.py:241
  33.1 1.6 %collective-permute-done.6.refs_3_ = f32[1,128]{1,0:T(1,128)S(1)} collective-permute-done((f32[1,128]{1,0:T(1,128)S(1)}, f32[1,128]{1,0:T(1,128)S(1)}, u32[]{:S(2)}, u32[]{:S(2)}) %collective-permute-start.6) | collective-permute-done | bytes 544 | tf_op jit(solution)/shard_map/ppermute | solution.py:32
  34.7 0.0 collective-permute-done.5.refs_1_
  34.7 0.9 %shard_map.80 = (f32[128,768]{1,0:T(8,128)}, f32[1,128]{1,0:T(1,128)}) custom-call(f32[128,768]{1,0:T(8,128)S(1)} %get-tuple-element.27.unit_ref, f32[128,1]{1,0:T(8,128)S(1)} %get-tuple-element.28.scale_ref, f32[128,768]{1,0:T(8,128)S(1)} %get-tuple-element.40.refs_0_, f32[128,768]{1,0:T(8,128)S(1)} %collective-permute-done.5.refs_1_, ...), custom_call_target="tpu_custom_call" | custom-call | tf_op jit(solution)/shard_map/pallas_call | solution.py:241
Async XLA Ops:
  0.6 10.0 %copy-start = (f32[128]{0:T(128)S(1)}, f32[128]{0:T(128)}, u32[]{:S(2)}) copy-start(f32[128]{0:T(128)} %param.9) | copy-start | bytes 1540
  0.6 11.9 %collective-permute-start = (f32[128,768]{1,0:T(8,128)}, f32[128,768]{1,0:T(8,128)S(1)}, u32[]{:S(2)}, u32[]{:S(2)}) collective-permute-start(f32[128,768]{1,0:T(8,128)} %y_any.1), channel_id=1, source_target_pairs={{0,2},{4,6},{8,10},{12,14},{16,18},{20,22},{24,26},{28,30},{2,0},{... | collective-permute-start | bytes 1179656 | tf_op jit(solution)/shard_map/ppermute | solution.py:22
  1.2 14.6 %collective-permute-start.4 = (f32[128,768]{1,0:T(8,128)}, f32[128,768]{1,0:T(8,128)S(1)}, u32[]{:S(2)}, u32[]{:S(2)}) collective-permute-start(f32[128,768]{1,0:T(8,128)} %x_any.1), channel_id=1, source_target_pairs={{0,1},{1,0},{2,3},{3,2},{4,5},{5,4},{6,7},{7,6},{8,9},{9,8},{10,11... | collective-permute-start | bytes 1179656 | tf_op jit(solution)/shard_map/ppermute | solution.py:32
  3.8 13.1 %collective-permute-start.1 = (f32[128,768]{1,0:T(8,128)}, f32[128,768]{1,0:T(8,128)S(1)}, u32[]{:S(2)}, u32[]{:S(2)}) collective-permute-start(f32[128,768]{1,0:T(8,128)} %y_any.1), channel_id=1, source_target_pairs={{2,4},{10,12},{18,20},{26,28},{4,2},{12,10},{20,18},{28,26},{3,5},... | collective-permute-start | bytes 1179656 | tf_op jit(solution)/shard_map/ppermute | solution.py:22
  4.4 12.4 %collective-permute-start.2 = (f32[128,768]{1,0:T(8,128)}, f32[128,768]{1,0:T(8,128)S(1)}, u32[]{:S(2)}, u32[]{:S(2)}) collective-permute-start(f32[128,768]{1,0:T(8,128)} %y_any.1), channel_id=1, source_target_pairs={{6,8},{14,16},{22,24},{30,0},{8,6},{16,14},{24,22},{0,30},{7,9},{1... | collective-permute-start | bytes 1179656 | tf_op jit(solution)/shard_map/ppermute | solution.py:22
  10.7 5.1 %collective-permute-start.3 = (f32[1,128]{1,0:T(1,128)S(1)}, f32[1,128]{1,0:T(1,128)S(1)}, u32[]{:S(2)}, u32[]{:S(2)}) collective-permute-start(f32[1,128]{1,0:T(1,128)S(1)} %bitcast.2), channel_id=1, source_target_pairs={{0,1},{1,0},{2,3},{3,2},{4,5},{5,4},{6,7},{7,6},{8,9},{9,8},{10,11... | collective-permute-start | bytes 1544 | tf_op jit(solution)/shard_map/ppermute | solution.py:32
  18.8 9.8 %collective-permute-start.7 = (f32[128,768]{1,0:T(8,128)S(1)}, f32[128,768]{1,0:T(8,128)S(1)}, u32[]{:S(2)}, u32[]{:S(2)}) collective-permute-start(f32[128,768]{1,0:T(8,128)S(1)} %get-tuple-element.49), channel_id=1, source_target_pairs={{0,2},{4,6},{8,10},{12,14},{16,18},{20,22},{24,26},{28,30},{2,0},{... | collective-permute-start | bytes 1179656 | tf_op jit(solution)/shard_map/ppermute | solution.py:22
  19.4 9.2 %collective-permute-start.8 = (f32[128,768]{1,0:T(8,128)S(1)}, f32[128,768]{1,0:T(8,128)S(1)}, u32[]{:S(2)}, u32[]{:S(2)}) collective-permute-start(f32[128,768]{1,0:T(8,128)S(1)} %get-tuple-element.50), channel_id=1, source_target_pairs={{2,4},{10,12},{18,20},{26,28},{4,2},{12,10},{20,18},{28,26},{3,5},... | collective-permute-start | bytes 1179656 | tf_op jit(solution)/shard_map/ppermute | solution.py:22
  20.1 12.0 %collective-permute-start.9 = (f32[128,768]{1,0:T(8,128)S(1)}, f32[128,768]{1,0:T(8,128)S(1)}, u32[]{:S(2)}, u32[]{:S(2)}) collective-permute-start(f32[128,768]{1,0:T(8,128)S(1)} %get-tuple-element.50), channel_id=1, source_target_pairs={{6,8},{14,16},{22,24},{30,0},{8,6},{16,14},{24,22},{0,30},{7,9},{1... | collective-permute-start | bytes 1179656 | tf_op jit(solution)/shard_map/ppermute | solution.py:22
  26.5 8.2 %collective-permute-start.5 = (f32[128,768]{1,0:T(8,128)S(1)}, f32[128,768]{1,0:T(8,128)S(1)}, u32[]{:S(2)}, u32[]{:S(2)}) collective-permute-start(f32[128,768]{1,0:T(8,128)S(1)} %get-tuple-element.41), channel_id=1, source_target_pairs={{0,1},{1,0},{2,3},{3,2},{4,5},{5,4},{6,7},{7,6},{8,9},{9,8},{10,11... | collective-permute-start | bytes 1179656 | tf_op jit(solution)/shard_map/ppermute | solution.py:32
  27.1 7.6 %collective-permute-start.6 = (f32[1,128]{1,0:T(1,128)S(1)}, f32[1,128]{1,0:T(1,128)S(1)}, u32[]{:S(2)}, u32[]{:S(2)}) collective-permute-start(f32[1,128]{1,0:T(1,128)S(1)} %get-tuple-element.43), channel_id=1, source_target_pairs={{0,1},{1,0},{2,3},{3,2},{4,5},{5,4},{6,7},{7,6},{8,9},{9,8},{10,11... | collective-permute-start | bytes 1544 | tf_op jit(solution)/shard_map/ppermute | solution.py:32

commit v3 on v2

--- a/solution.py
+++ b/solution.py
@@ -19,12 +19,9 @@
 
 
 def exchanged(x, axis, pairs):
-    return lax.ppermute(x, axis, pairs + [(b, a) for (a, b) in pairs])
-
-
-def far_pairs(length):
-    pairs = [(i, (i + 1) % length) for i in range(1, length, 2)]
-    return [pairs[0::2], pairs[1::2]]
+    paired = {i for pair in pairs for i in pair}
+    alone = [(i, i) for i in range(lax.axis_size(axis)) if i not in paired]
+    return lax.ppermute(x, axis, pairs + [(b, a) for (a, b) in pairs] + alone)
 
 
 def shifted(x, axis, by):
@@ -129,9 +126,9 @@
         gp_refs[s][...] = mm(stacked(slope), ys_ref, NN)
 
 
-def third_body(others, lt, bi, *refs):
+def third_body(others, lt, bi, at_end, *refs):
     members = others + 1
-    early_ref, late_ref, refs = *refs[:2], refs[2:]
+    far_ref, end_ref, refs = *refs[:2], refs[2:]
     w_refs, refs = refs[:members], refs[members:]
     all_ref, refs = refs[0], refs[1:]
     gp_in, refs = refs[:others], refs[others:]
@@ -141,8 +138,8 @@
     sum_refs, refs = refs[:members], refs[members:]
     fs_ref, slope_ref = refs
     temper = temper_of(lt)
-    count = early_ref.shape[0]
-    far = early_ref[...] + late_ref[...]
+    count = far_ref.shape[0]
+    far = jnp.where(at_end[0] == 1, end_ref[...], far_ref[...])
     fs_ref[...] = stacked(far)
     scale = scale_of(far)
     z = (temper * scale) * mm(fs_ref, all_ref, NT) + bi[0]
@@ -176,32 +173,40 @@
     gx_ref[...] = gx_in[...] + mm(stacked(slope_ref[...].T), fs_ref, NN)
 
 
-def last_body(terms, lines, pairs, unit_ref, scale_ref, *refs):
-    grads, refs = refs[:terms], refs[terms:]
-    sums, refs = refs[:lines], refs[lines:]
-    if lines:
-        out_ref, loss_ref, held, sem, line = refs
-    else:
-        out_ref, held, sem = refs
-    rows = unit_ref.shape[0] // CHUNKS
+def last_body(others, pairs, at_end, *refs):
+    (unit_x, scale_x, own_x), refs = refs[:3], refs[3:]
+    back_x, refs = refs[:others], refs[others:]
+    (unit_y, scale_y, own_y, near_y, far_y, end_y), refs = refs[:6], refs[6:]
+    sums, refs = refs[: others + 1], refs[others + 1 :]
+    x_out, y_out, loss_out, held, line, sem = refs
+    rows = unit_x.shape[0] // CHUNKS
     copies = []
-    if lines:
-        total = sums[0][...]
-        for r in sums[1:]:
-            total = total + r[...]
-        line[...] = total / pairs
-        copies.append(pltpu.make_async_copy(line, loss_ref, sem.at[CHUNKS]))
+
+    def send(source, target):
+        copies.append(pltpu.make_async_copy(source, target, sem.at[len(copies)]))
         copies[-1].start()
+
+    def through(k, here, unit, scale, grad, out_ref):
+        inner = jnp.sum(unit * grad, axis=1, keepdims=True)
+        held[k, here, :] = scale * (grad - unit * inner)
+        send(held.at[k, here, :], out_ref.at[here, :])
+
+    total = sums[0][...]
+    for r in sums[1:]:
+        total = total + r[...]
+    line[...] = total / pairs
+    send(line, loss_out)
     for c in range(CHUNKS):
         here = pl.ds(c * rows, rows)
-        grad = grads[0][here, :]
-        for r in grads[1:]:
+        grad = own_x[here, :]
+        for r in back_x:
             grad = grad + r[here, :]
-        unit = unit_ref[here, :]
-        inner = jnp.sum(unit * grad, axis=1, keepdims=True)
-        held[here, :] = scale_ref[here, :] * (grad - unit * inner)
-        copies.append(pltpu.make_async_copy(held.at[here, :], out_ref.at[here, :], sem.at[c]))
-        copies[-1].start()
+        through(0, here, unit_x[here, :], scale_x[here, :], grad, x_out)
+    for c in range(CHUNKS):
+        here = pl.ds(c * rows, rows)
+        grad = jnp.where(at_end[0] == 1, end_y[here, :], far_y[here, :])
+        grad = own_y[here, :] + near_y[here, :] + grad
+        through(1, here, unit_y[here, :], scale_y[here, :], grad, y_out)
     for copy in copies:
         copy.wait()
 
@@ -232,24 +237,21 @@
     )(*scalars, *in_hbm(args[:anywhere]), *in_vmem(args[anywhere:]))
 
 
-def finish(unit, scale, grads, sums=(), pairs=None):
-    full = shape(*unit.shape)
-    line = shape(1, unit.shape[0])
-    args = [unit, scale, *grads, *sums]
-    extra = [pltpu.VMEM(line.shape, F32)] if sums else []
-    outs = [full, line] if sums else [full]
+def finish(others, pairs, at_end, *args):
+    full = shape(*args[0].shape)
+    line = shape(1, full.shape[0])
     return pl.pallas_call(
-        functools.partial(last_body, len(grads), len(sums), pairs),
-        out_shape=outs,
-        in_specs=[VMEM] * len(args),
-        out_specs=[HBM] * len(outs),
+        functools.partial(last_body, others, pairs),
+        out_shape=[full, full, line],
+        in_specs=[SMEM] + [VMEM] * len(args),
+        out_specs=[HBM] * 3,
         scratch_shapes=[
-            pltpu.VMEM(full.shape, F32),
-            pltpu.SemaphoreType.DMA((CHUNKS + 1,)),
-            *extra,
+            pltpu.VMEM((2, *full.shape), F32),
+            pltpu.VMEM(line.shape, F32),
+            pltpu.SemaphoreType.DMA((2 * CHUNKS + 1,)),
         ],
         compiler_params=PARAMS,
-    )(*in_vmem(args))
+    )(at_end, *in_vmem(args))
 
 
 def body(images, texts, log_temp, bias, row_weight):
@@ -260,10 +262,13 @@
     scalars = (log_temp, bias)
     length = lax.axis_size("blk")
     near_pairs = [(i, i + 1) for i in range(0, length, 2)]
-    early, late = far_pairs(length)
-    far_early = exchanged(texts, "blk", early)
+    far_pairs = [(i, i + 1) for i in range(1, length - 1, 2)]
+    ends = [(length - 1, 0)]
+    place = lax.axis_index("blk")
+    at_end = jnp.where((place == 0) | (place == length - 1), 1, 0).astype(jnp.int32).reshape(1)
+    far = exchanged(texts, "blk", far_pairs)
     raws = [shifted(images, "grp", -s) for s in range(1, members)]
-    far_late = exchanged(texts, "blk", late)
+    far_end = exchanged(texts, "blk", ends)
     near = exchanged(texts, "blk", near_pairs)
     weights = [weight] + [shifted(weight, "grp", -s) for s in range(1, members)]
     full = shape(count, width)
@@ -308,9 +313,9 @@
     outs = call(
         functools.partial(third_body, others),
         [full] + [full] * others + [line] * members + [stack, shape(count, count)],
-        scalars,
-        far_early,
-        far_late,
+        (*scalars, at_end),
+        far,
+        far_end,
         *weights,
         everyone,
         *gp,
@@ -320,9 +325,9 @@
     g_far, outs = outs[0], outs[1:]
     gp, outs = outs[:others], outs[others:]
     sums, (fs, slope) = outs[:members], outs[members:]
-    back_early = exchanged(g_far, "blk", early)
+    back_far = exchanged(g_far, "blk", far_pairs)
     back_x = [shifted(gp[s - 1], "grp", s) for s in range(1, members)]
-    back_late = exchanged(g_far, "blk", late)
+    back_end = exchanged(g_far, "blk", ends)
     back_sum = [shifted(sums[s], "grp", s) for s in range(1, members)]
     gx, g_own, g_near = call(
         functools.partial(fourth_body, others),
@@ -336,9 +341,23 @@
         *slopes,
     )
     back_near = exchanged(g_near, "blk", near_pairs)
-    pairs = 3.0 * members * count
-    grad_x, row_loss = finish(unit_x, scale_x, [gx, *back_x], [sums[0], *back_sum], pairs)
-    (grad_y,) = finish(unit_y, scale_y, [g_own, back_near, back_early, back_late])
+    grad_x, grad_y, row_loss = finish(
+        others,
+        3.0 * members * count,
+        at_end,
+        unit_x,
+        scale_x,
+        gx,
+        *back_x,
+        unit_y,
+        scale_y,
+        g_own,
+        back_near,
+        back_far,
+        back_end,
+        sums[0],
+        *back_sum,
+    )
     return (row_loss.reshape(count), grad_x, grad_y)
 
 

time: 35.9 us -> 35.9 us (level)
  the two profiles are of different devices: /device:TPU:0 before, /device:TPU:1 now
where the time goes in v3:
time: 35.9 us; the launch traced here: 35.6 us
  starting transfers between devices  14 us (39%)
  waiting for transfers between devices  12.2 us (34%)
  Pallas kernels  7.39 us (21%)
  between operations  2.03 us (6%)
    ppermute x6, starting transfers between devices, exchanged(): return lax.ppermute(x, axis, pairs + [(b, a) for a, b in pairs] + alone)  8.6 us
    ppermute x6, waiting for transfers between devices, exchanged(): return lax.ppermute(x, axis, pairs + [(b, a) for a, b in pairs] + alone)  6.63 us
    pallas_call x4, Pallas kernels, call(): pl.pallas_call(body, out_shape=[pltpu.VMEM(o.shape, o.dtype) for o in out...  6.17 us
    ppermute x4, waiting for transfers between devices, shifted(): lax.ppermute(x, axis, [(i, (i + by) % length) for i in range(length)])  5.55 us
    ppermute x4, starting transfers between devices, shifted(): lax.ppermute(x, axis, [(i, (i + by) % length) for i in range(length)])  5.39 us
    pallas_call x1, Pallas kernels, finish(): pl.pallas_call(functools.partial(last_body, others, pairs), out_shape=[fu...  1.23 us
  transfers between devices with their start and end apart: 10, of which 3 were waited for; matrix products, arithmetic and copies ran while one was open for 0% of the time, Pallas kernels for 12%

profile of v3, /device:TPU:1, one launch (start us, length us, event | category | flops | bytes accessed | tf_op | source)
XLA Modules:
  0.0 35.6 jit_solution(17104938910212105073)
XLA Ops:
  0.6 0.0 copy-start
  0.6 0.1 collective-permute-start
  0.7 2.7 %collective-permute-start.4 = (f32[128,768]{1,0:T(8,128)}, f32[128,768]{1,0:T(8,128)S(1)}, u32[]{:S(2)}, u32[]{:S(2)}) collective-permute-start(f32[128,768]{1,0:T(8,128)} %x_any.1), channel_id=1, source_target_pairs={{0,1},{1,0},{2,3},{3,2},{4,5},{5,4},{6,7},{7,6},{8,9},{9,8},{10,11... | collective-permute-start | bytes 1179656 | tf_op jit(solution)/shard_map/ppermute | solution.py:29
  3.4 3.4 %collective-permute-start.1 = (f32[128,768]{1,0:T(8,128)}, f32[128,768]{1,0:T(8,128)S(1)}, u32[]{:S(2)}, u32[]{:S(2)}) collective-permute-start(f32[128,768]{1,0:T(8,128)} %y_any.1), channel_id=1, source_target_pairs={{2,4},{6,8},{10,12},{14,16},{18,20},{22,24},{26,28},{4,2},{8,6},{1... | collective-permute-start | bytes 1179656 | tf_op jit(solution)/shard_map/ppermute | solution.py:24
  6.8 1.7 %collective-permute-start.2 = (f32[128,768]{1,0:T(8,128)}, f32[128,768]{1,0:T(8,128)S(1)}, u32[]{:S(2)}, u32[]{:S(2)}) collective-permute-start(f32[128,768]{1,0:T(8,128)} %y_any.1), channel_id=1, source_target_pairs={{30,0},{0,30},{2,2},{4,4},{6,6},{8,8},{10,10},{12,12},{14,14},{16,... | collective-permute-start | bytes 1179656 | tf_op jit(solution)/shard_map/ppermute | solution.py:24
  8.5 0.0 copy-done
  8.5 0.3 collective-permute-start.3
  10.0 0.0 collective-permute-done.near_ref
  10.0 3.2 %shard_map.76 = (f32[128,768]{1,0:T(8,128)S(1)}, f32[128,1]{1,0:T(8,128)S(1)}, f32[128,768]{1,0:T(8,128)S(1)}, f32[128,1]{1,0:T(8,128)S(1)}, bf16[256,768]{1,0:T...) custom-call(f32[1]{0:T(128)S(6)} %copy.8.lt, ...), custom_call_target="tpu_custom_call" | custom-call | tf_op jit(solution)/shard_map/pallas_call | solution.py:230
  13.2 0.0 collective-permute-done.3.refs_1_.refs_3_
  13.2 0.0 collective-permute-done.4.refs_0_
  13.2 1.0 %shard_map.77 = (bf16[512,768]{1,0:T(8,128)(2,1)S(1)}, f32[128,768]{1,0:T(8,128)S(1)}, f32[1,128]{1,0:T(1,128)S(1)}, f32[128,256]{1,0:T(8,128)S(1)}) custom-call(f32[1]{0:T(128)S(6)} %copy.8.lt, f32[1]{0:T(128)S(6)} %copy.9.bi, f32[128,768]{1,0:T(8,128)S(1)} %collective-permute-done.4.refs_0_, f32[1,128]{1,0:T(1,128)S(1)} %collective-permute-done.3.refs_1_.refs_3_, ...), custom_call_target="tpu_custom_call" | custom-call | tf_op jit(solution)/shard_map/pallas_call | solution.py:230
  14.3 2.7 %collective-permute-done.1.refs_0_ = f32[128,768]{1,0:T(8,128)S(1)} collective-permute-done((f32[128,768]{1,0:T(8,128)}, f32[128,768]{1,0:T(8,128)S(1)}, u32[]{:S(2)}, u32[]{:S(2)}) %collective-permute-start.1) | collective-permute-done | bytes 393248 | tf_op jit(solution)/shard_map/ppermute | solution.py:24
  17.0 0.0 collective-permute-done.2.refs_1_
  17.0 1.3 %shard_map.78 = (f32[128,768]{1,0:T(8,128)S(1)}, f32[128,768]{1,0:T(8,128)S(1)}, f32[1,128]{1,0:T(1,128)S(1)}, f32[1,128]{1,0:T(1,128)S(1)}, bf16[256,768]{1,0:T(8,128)(2,1)S(1)}, /*index=5*/f32[128,128]{1,0:T(8,128)S(1)}) custom-call(f32[1]{0:T(128)S(6)} %copy.8.lt, f32[1]{0:T(128)S(6)} %copy.9.bi, s32[1]{0:T(128)} %bitcast.at_end, ...), custom_call_target="tpu_custom_call" | custom-call | tf_op jit(solution)/shard_map/pallas_call | solution.py:230
  18.3 0.7 %shard_map.79 = (f32[128,768]{1,0:T(8,128)S(1)}, f32[128,768]{1,0:T(8,128)S(1)}, f32[128,768]{1,0:T(8,128)S(1)}) custom-call(f32[128,768]{1,0:T(8,128)S(1)} %get-tuple-element.30.gx_in, f32[256,768]{1,0:T(8,128)S(1)} %get-tuple-element.31.gy_in, f32[128,128]{1,0:T(8,128)S(1)} %get-tuple-element.38.slope_ref, bf16[256,768]{1,0:T(8,128)(2,1)S(1)} %get-tuple-element.39.fs_ref, ...), custom_call_target="tpu_custom_call" | custom-call | tf_op jit(solution)/shard_map/pallas_call | solution.py:230
  19.0 0.9 %collective-permute-start.6 = (f32[128,768]{1,0:T(8,128)S(1)}, f32[128,768]{1,0:T(8,128)S(1)}, u32[]{:S(2)}, u32[]{:S(2)}) collective-permute-start(f32[128,768]{1,0:T(8,128)S(1)} %get-tuple-element.46), channel_id=1, source_target_pairs={{0,2},{4,6},{8,10},{12,14},{16,18},{20,22},{24,26},{28,30},{2,0},{... | collective-permute-start | bytes 1179656 | tf_op jit(solution)/shard_map/ppermute | solution.py:24
  19.9 1.2 %collective-permute-start.5 = (f32[128,768]{1,0:T(8,128)S(1)}, f32[128,768]{1,0:T(8,128)S(1)}, u32[]{:S(2)}, u32[]{:S(2)}) collective-permute-start(f32[128,768]{1,0:T(8,128)S(1)} %get-tuple-element.42), channel_id=1, source_target_pairs={{0,1},{1,0},{2,3},{3,2},{4,5},{5,4},{6,7},{7,6},{8,9},{9,8},{10,11... | collective-permute-start | bytes 1179656 | tf_op jit(solution)/shard_map/ppermute | solution.py:29
  21.1 1.9 %collective-permute-start.7 = (f32[128,768]{1,0:T(8,128)S(1)}, f32[128,768]{1,0:T(8,128)S(1)}, u32[]{:S(2)}, u32[]{:S(2)}) collective-permute-start(f32[128,768]{1,0:T(8,128)S(1)} %get-tuple-element.47), channel_id=1, source_target_pairs={{2,4},{6,8},{10,12},{14,16},{18,20},{22,24},{26,28},{4,2},{8,6},{1... | collective-permute-start | bytes 1179656 | tf_op jit(solution)/shard_map/ppermute | solution.py:24
  23.0 0.7 %collective-permute-start.8 = (f32[128,768]{1,0:T(8,128)S(1)}, f32[128,768]{1,0:T(8,128)S(1)}, u32[]{:S(2)}, u32[]{:S(2)}) collective-permute-start(f32[128,768]{1,0:T(8,128)S(1)} %get-tuple-element.47), channel_id=1, source_target_pairs={{30,0},{0,30},{2,2},{4,4},{6,6},{8,8},{10,10},{12,12},{14,14},{16,... | collective-permute-start | bytes 1179656 | tf_op jit(solution)/shard_map/ppermute | solution.py:24
  23.7 1.2 %collective-permute-start.9 = (f32[1,128]{1,0:T(1,128)S(1)}, f32[1,128]{1,0:T(1,128)S(1)}, u32[]{:S(2)}, u32[]{:S(2)}) collective-permute-start(f32[1,128]{1,0:T(1,128)S(1)} %get-tuple-element.49), channel_id=1, source_target_pairs={{0,1},{1,0},{2,3},{3,2},{4,5},{5,4},{6,7},{7,6},{8,9},{9,8},{10,11... | collective-permute-start | bytes 1544 | tf_op jit(solution)/shard_map/ppermute | solution.py:29
  24.9 5.5 %collective-permute-done.9.refs_11_ = f32[1,128]{1,0:T(1,128)S(1)} collective-permute-done((f32[1,128]{1,0:T(1,128)S(1)}, f32[1,128]{1,0:T(1,128)S(1)}, u32[]{:S(2)}, u32[]{:S(2)}) %collective-permute-start.9) | collective-permute-done | bytes 544 | tf_op jit(solution)/shard_map/ppermute | solution.py:29
  30.5 0.0 collective-permute-done.6.refs_7_
  30.5 0.0 collective-permute-done.5.refs_3_
  30.5 3.9 %collective-permute-done.7.refs_8_ = f32[128,768]{1,0:T(8,128)S(1)} collective-permute-done((f32[128,768]{1,0:T(8,128)S(1)}, f32[128,768]{1,0:T(8,128)S(1)}, u32[]{:S(2)}, u32[]{:S(2)}) %collective-permute-start.7) | collective-permute-done | bytes 393248 | tf_op jit(solution)/shard_map/ppermute | solution.py:24
  34.4 0.0 collective-permute-done.8.refs_9_
  34.4 1.2 %shard_map.80 = (f32[128,768]{1,0:T(8,128)}, f32[128,768]{1,0:T(8,128)}, f32[1,128]{1,0:T(1,128)}) custom-call(s32[1]{0:T(128)} %bitcast.at_end, f32[128,768]{1,0:T(8,128)S(1)} %get-tuple-element.28.refs_0_, f32[128,1]{1,0:T(8,128)S(1)} %get-tuple-element.29.refs_1_, f32[128,768]{1,0:T(8,128)S(1)} %get-tuple-element.41.refs_2_, ...), custom_call_target="tpu_custom_call" | custom-call | tf_op jit(solution)/shard_map/pallas_call | solution.py:243
Async XLA Ops:
  0.6 7.8 %copy-start = (f32[128]{0:T(128)S(1)}, f32[128]{0:T(128)}, u32[]{:S(2)}) copy-start(f32[128]{0:T(128)} %param.9) | copy-start | bytes 1540
  0.6 9.4 %collective-permute-start = (f32[128,768]{1,0:T(8,128)}, f32[128,768]{1,0:T(8,128)S(1)}, u32[]{:S(2)}, u32[]{:S(2)}) collective-permute-start(f32[128,768]{1,0:T(8,128)} %y_any.1), channel_id=1, source_target_pairs={{0,2},{4,6},{8,10},{12,14},{16,18},{20,22},{24,26},{28,30},{2,0},{... | collective-permute-start | bytes 1179656 | tf_op jit(solution)/shard_map/ppermute | solution.py:24
  0.7 12.5 %collective-permute-start.4 = (f32[128,768]{1,0:T(8,128)}, f32[128,768]{1,0:T(8,128)S(1)}, u32[]{:S(2)}, u32[]{:S(2)}) collective-permute-start(f32[128,768]{1,0:T(8,128)} %x_any.1), channel_id=1, source_target_pairs={{0,1},{1,0},{2,3},{3,2},{4,5},{5,4},{6,7},{7,6},{8,9},{9,8},{10,11... | collective-permute-start | bytes 1179656 | tf_op jit(solution)/shard_map/ppermute | solution.py:29
  3.4 13.6 %collective-permute-start.1 = (f32[128,768]{1,0:T(8,128)}, f32[128,768]{1,0:T(8,128)S(1)}, u32[]{:S(2)}, u32[]{:S(2)}) collective-permute-start(f32[128,768]{1,0:T(8,128)} %y_any.1), channel_id=1, source_target_pairs={{2,4},{6,8},{10,12},{14,16},{18,20},{22,24},{26,28},{4,2},{8,6},{1... | collective-permute-start | bytes 1179656 | tf_op jit(solution)/shard_map/ppermute | solution.py:24
  6.8 10.2 %collective-permute-start.2 = (f32[128,768]{1,0:T(8,128)}, f32[128,768]{1,0:T(8,128)S(1)}, u32[]{:S(2)}, u32[]{:S(2)}) collective-permute-start(f32[128,768]{1,0:T(8,128)} %y_any.1), channel_id=1, source_target_pairs={{30,0},{0,30},{2,2},{4,4},{6,6},{8,8},{10,10},{12,12},{14,14},{16,... | collective-permute-start | bytes 1179656 | tf_op jit(solution)/shard_map/ppermute | solution.py:24
  8.5 4.8 %collective-permute-start.3 = (f32[1,128]{1,0:T(1,128)S(1)}, f32[1,128]{1,0:T(1,128)S(1)}, u32[]{:S(2)}, u32[]{:S(2)}) collective-permute-start(f32[1,128]{1,0:T(1,128)S(1)} %bitcast.3), channel_id=1, source_target_pairs={{0,1},{1,0},{2,3},{3,2},{4,5},{5,4},{6,7},{7,6},{8,9},{9,8},{10,11... | collective-permute-start | bytes 1544 | tf_op jit(solution)/shard_map/ppermute | solution.py:29
  19.0 11.5 %collective-permute-start.6 = (f32[128,768]{1,0:T(8,128)S(1)}, f32[128,768]{1,0:T(8,128)S(1)}, u32[]{:S(2)}, u32[]{:S(2)}) collective-permute-start(f32[128,768]{1,0:T(8,128)S(1)} %get-tuple-element.46), channel_id=1, source_target_pairs={{0,2},{4,6},{8,10},{12,14},{16,18},{20,22},{24,26},{28,30},{2,0},{... | collective-permute-start | bytes 1179656 | tf_op jit(solution)/shard_map/ppermute | solution.py:24
  19.9 10.6 %collective-permute-start.5 = (f32[128,768]{1,0:T(8,128)S(1)}, f32[128,768]{1,0:T(8,128)S(1)}, u32[]{:S(2)}, u32[]{:S(2)}) collective-permute-start(f32[128,768]{1,0:T(8,128)S(1)} %get-tuple-element.42), channel_id=1, source_target_pairs={{0,1},{1,0},{2,3},{3,2},{4,5},{5,4},{6,7},{7,6},{8,9},{9,8},{10,11... | collective-permute-start | bytes 1179656 | tf_op jit(solution)/shard_map/ppermute | solution.py:29
  21.1 13.3 %collective-permute-start.7 = (f32[128,768]{1,0:T(8,128)S(1)}, f32[128,768]{1,0:T(8,128)S(1)}, u32[]{:S(2)}, u32[]{:S(2)}) collective-permute-start(f32[128,768]{1,0:T(8,128)S(1)} %get-tuple-element.47), channel_id=1, source_target_pairs={{2,4},{6,8},{10,12},{14,16},{18,20},{22,24},{26,28},{4,2},{8,6},{1... | collective-permute-start | bytes 1179656 | tf_op jit(solution)/shard_map/ppermute | solution.py:24
  23.0 11.4 %collective-permute-start.8 = (f32[128,768]{1,0:T(8,128)S(1)}, f32[128,768]{1,0:T(8,128)S(1)}, u32[]{:S(2)}, u32[]{:S(2)}) collective-permute-start(f32[128,768]{1,0:T(8,128)S(1)} %get-tuple-element.47), channel_id=1, source_target_pairs={{30,0},{0,30},{2,2},{4,4},{6,6},{8,8},{10,10},{12,12},{14,14},{16,... | collective-permute-start | bytes 1179656 | tf_op jit(solution)/shard_map/ppermute | solution.py:24
  23.7 6.8 %collective-permute-start.9 = (f32[1,128]{1,0:T(1,128)S(1)}, f32[1,128]{1,0:T(1,128)S(1)}, u32[]{:S(2)}, u32[]{:S(2)}) collective-permute-start(f32[1,128]{1,0:T(1,128)S(1)} %get-tuple-element.49), channel_id=1, source_target_pairs={{0,1},{1,0},{2,3},{3,2},{4,5},{5,4},{6,7},{7,6},{8,9},{9,8},{10,11... | collective-permute-start | bytes 1544 | tf_op jit(solution)/shard_map/ppermute | solution.py:29

commit v4 on v3

--- a/solution.py
+++ b/solution.py
@@ -19,9 +19,7 @@
 
 
 def exchanged(x, axis, pairs):
-    paired = {i for pair in pairs for i in pair}
-    alone = [(i, i) for i in range(lax.axis_size(axis)) if i not in paired]
-    return lax.ppermute(x, axis, pairs + [(b, a) for (a, b) in pairs] + alone)
+    return lax.ppermute(x, axis, pairs + [(b, a) for (a, b) in pairs])
 
 
 def shifted(x, axis, by):
@@ -69,19 +67,19 @@
     return rows == lax.broadcasted_iota(jnp.int32, (count, count), 1)
 
 
-def temper_of(lt):
-    return jnp.exp(jnp.full((1, 1), lt[0], F32))
+def scalars_of(tb_ref):
+    return tb_ref[0:1, 0:1], tb_ref[1:2, 0:1]
 
 
 def first_body(lt, bi, x_any, y_any, near_ref, w_ref, *refs):
-    x_ref, xc_ref, y_ref, yc_ref, xs_ref, ys_ref, gx_ref, gy_ref, sum_ref, sem = refs
+    tb_ref, x_ref, xc_ref, y_ref, yc_ref, xs_ref, ys_ref, gx_ref, gy_ref, sum_ref = refs[:10]
+    sem = refs[10]
     copies = [
         pltpu.make_async_copy(x_any, x_ref, sem.at[0]),
         pltpu.make_async_copy(y_any, y_ref, sem.at[1]),
     ]
     for copy in copies:
         copy.start()
-    temper = temper_of(lt)
     count = near_ref.shape[0]
     near = near_ref[...] * scale_of(near_ref[...])
     for copy, ref, scale_ref in zip(copies, (x_ref, y_ref), (xc_ref, yc_ref)):
@@ -90,22 +88,25 @@
         ref[...] = ref[...] * scale_ref[...]
     xs_ref[...] = stacked(x_ref[...])
     ys_ref[...] = stacked(jnp.concatenate([y_ref[...], near], axis=0))
+    tb_ref[0:1, :] = jnp.exp(jnp.full((1, count), lt[0], F32))
+    tb_ref[1:2, :] = jnp.full((1, count), bi[0], F32)
+    temper, bias = scalars_of(tb_ref)
     rows = lax.broadcasted_iota(jnp.int32, (2 * count, count), 0)
     cols = lax.broadcasted_iota(jnp.int32, (2 * count, count), 1)
-    z = temper * mm(ys_ref, xs_ref, NT) + bi[0]
+    z = temper * mm(ys_ref, xs_ref, NT) + bias
     loss, slope = gated(z, w_ref[...] * temper, rows == cols)
     sum_ref[...] = jnp.sum(loss, axis=0, keepdims=True)
     gx_ref[...] = mm(stacked(slope.T), ys_ref, NN)
     gy_ref[...] = mm(stacked(slope), xs_ref, NN)
 
 
-def second_body(others, lt, bi, *refs):
+def second_body(others, tb_ref, *refs):
     raw_refs, refs = refs[:others], refs[others:]
     w_refs, refs = refs[:others], refs[others:]
     xs_ref, ys_ref, all_ref, refs = *refs[:3], refs[3:]
     gp_refs, refs = refs[:others], refs[others:]
     sump_refs, slope_refs = refs[:others], refs[others:]
-    temper = temper_of(lt)
+    temper, bias = scalars_of(tb_ref)
     count = raw_refs[0].shape[0]
     deep = (others + 1) * count
     eye = square(count)
@@ -117,7 +118,7 @@
         here = (s + 1) * count
         all_ref[here : here + count] = px[:count]
         all_ref[deep + here : deep + here + count] = px[count:]
-        z = temper * mm(px, ys_ref, NT) + bi[0]
+        z = temper * mm(px, ys_ref, NT) + bias
         weight = jnp.sum(jnp.where(eye, w_refs[s][...], 0.0), axis=1, keepdims=True)
         loss, slope = gated(z, weight * temper)
         sums = jnp.sum(loss, axis=1, keepdims=True)
@@ -126,9 +127,9 @@
         gp_refs[s][...] = mm(stacked(slope), ys_ref, NN)
 
 
-def third_body(others, lt, bi, at_end, *refs):
+def third_body(others, tb_ref, *refs):
     members = others + 1
-    far_ref, end_ref, refs = *refs[:2], refs[2:]
+    far_ref, refs = refs[0], refs[1:]
     w_refs, refs = refs[:members], refs[members:]
     all_ref, refs = refs[0], refs[1:]
     gp_in, refs = refs[:others], refs[others:]
@@ -137,12 +138,12 @@
     gp_refs, refs = refs[:others], refs[others:]
     sum_refs, refs = refs[:members], refs[members:]
     fs_ref, slope_ref = refs
-    temper = temper_of(lt)
+    temper, bias = scalars_of(tb_ref)
     count = far_ref.shape[0]
-    far = jnp.where(at_end[0] == 1, end_ref[...], far_ref[...])
+    far = far_ref[...]
     fs_ref[...] = stacked(far)
     scale = scale_of(far)
-    z = (temper * scale) * mm(fs_ref, all_ref, NT) + bi[0]
+    z = (temper * scale) * mm(fs_ref, all_ref, NT) + bias
     weight = jnp.concatenate([w[...] for w in w_refs], axis=1) * temper
     loss, slope = gated(z, weight)
     gfar_ref[...] = mm(stacked(slope), all_ref, NN)
@@ -173,10 +174,10 @@
     gx_ref[...] = gx_in[...] + mm(stacked(slope_ref[...].T), fs_ref, NN)
 
 
-def last_body(others, pairs, at_end, *refs):
+def last_body(others, pairs, *refs):
     (unit_x, scale_x, own_x), refs = refs[:3], refs[3:]
     back_x, refs = refs[:others], refs[others:]
-    (unit_y, scale_y, own_y, near_y, far_y, end_y), refs = refs[:6], refs[6:]
+    (unit_y, scale_y, own_y, near_y, far_y), refs = refs[:5], refs[5:]
     sums, refs = refs[: others + 1], refs[others + 1 :]
     x_out, y_out, loss_out, held, line, sem = refs
     rows = unit_x.shape[0] // CHUNKS
@@ -204,8 +205,7 @@
         through(0, here, unit_x[here, :], scale_x[here, :], grad, x_out)
     for c in range(CHUNKS):
         here = pl.ds(c * rows, rows)
-        grad = jnp.where(at_end[0] == 1, end_y[here, :], far_y[here, :])
-        grad = own_y[here, :] + near_y[here, :] + grad
+        grad = own_y[here, :] + near_y[here, :] + far_y[here, :]
         through(1, here, unit_y[here, :], scale_y[here, :], grad, y_out)
     for copy in copies:
         copy.wait()
@@ -226,24 +226,25 @@
     return [pltpu.with_memory_space_constraint(a, pltpu.VMEM) for a in args]
 
 
-def call(body, outs, scalars, *args, scratch=(), anywhere=0):
+def call(body, outs, *args, scratch=(), scalars=0, anywhere=0):
+    numbers, args = args[:scalars], args[scalars:]
     return pl.pallas_call(
         body,
         out_shape=[pltpu.VMEM(o.shape, o.dtype) for o in outs],
-        in_specs=[SMEM] * len(scalars) + [HBM] * anywhere + [VMEM] * (len(args) - anywhere),
+        in_specs=[SMEM] * scalars + [HBM] * anywhere + [VMEM] * (len(args) - anywhere),
         out_specs=[VMEM] * len(outs),
         scratch_shapes=list(scratch),
         compiler_params=PARAMS,
-    )(*scalars, *in_hbm(args[:anywhere]), *in_vmem(args[anywhere:]))
-
-
-def finish(others, pairs, at_end, *args):
+    )(*numbers, *in_hbm(args[:anywhere]), *in_vmem(args[anywhere:]))
+
+
+def finish(others, pairs, *args):
     full = shape(*args[0].shape)
     line = shape(1, full.shape[0])
     return pl.pallas_call(
         functools.partial(last_body, others, pairs),
         out_shape=[full, full, line],
-        in_specs=[SMEM] + [VMEM] * len(args),
+        in_specs=[VMEM] * len(args),
         out_specs=[HBM] * 3,
         scratch_shapes=[
             pltpu.VMEM((2, *full.shape), F32),
@@ -251,7 +252,7 @@
             pltpu.SemaphoreType.DMA((2 * CHUNKS + 1,)),
         ],
         compiler_params=PARAMS,
-    )(at_end, *in_vmem(args))
+    )(*in_vmem(args))
 
 
 def body(images, texts, log_temp, bias, row_weight):
@@ -259,24 +260,20 @@
     others = members - 1
     count, width = images.shape
     weight = row_weight.reshape(1, count)
-    scalars = (log_temp, bias)
     length = lax.axis_size("blk")
     near_pairs = [(i, i + 1) for i in range(0, length, 2)]
-    far_pairs = [(i, i + 1) for i in range(1, length - 1, 2)]
-    ends = [(length - 1, 0)]
-    place = lax.axis_index("blk")
-    at_end = jnp.where((place == 0) | (place == length - 1), 1, 0).astype(jnp.int32).reshape(1)
+    far_pairs = [(i, (i + 1) % length) for i in range(1, length, 2)]
+    raws = [shifted(images, "grp", -s) for s in range(1, members)]
     far = exchanged(texts, "blk", far_pairs)
-    raws = [shifted(images, "grp", -s) for s in range(1, members)]
-    far_end = exchanged(texts, "blk", ends)
     near = exchanged(texts, "blk", near_pairs)
     weights = [weight] + [shifted(weight, "grp", -s) for s in range(1, members)]
     full = shape(count, width)
     line = shape(1, count)
     stack = shape(2 * count, width, kind=BF)
-    unit_x, scale_x, unit_y, scale_y, xs, ys, gx, gy, sums = call(
+    tb, unit_x, scale_x, unit_y, scale_y, xs, ys, gx, gy, sums = call(
         first_body,
         [
+            shape(2, count),
             full,
             shape(count, 1),
             full,
@@ -287,12 +284,14 @@
             shape(2 * count, width),
             line,
         ],
-        scalars,
+        log_temp,
+        bias,
         images,
         texts,
         near,
         weight,
         scratch=[pltpu.SemaphoreType.DMA((2,))],
+        scalars=2,
         anywhere=2,
     )
     outs = call(
@@ -301,7 +300,7 @@
         + [full] * others
         + [line] * others
         + [shape(count, 2 * count)] * others,
-        scalars,
+        tb,
         *raws,
         *weights[1:],
         xs,
@@ -313,9 +312,8 @@
     outs = call(
         functools.partial(third_body, others),
         [full] + [full] * others + [line] * members + [stack, shape(count, count)],
-        (*scalars, at_end),
+        tb,
         far,
-        far_end,
         *weights,
         everyone,
         *gp,
@@ -325,14 +323,12 @@
     g_far, outs = outs[0], outs[1:]
     gp, outs = outs[:others], outs[others:]
     sums, (fs, slope) = outs[:members], outs[members:]
+    back_x = [shifted(gp[s - 1], "grp", s) for s in range(1, members)]
     back_far = exchanged(g_far, "blk", far_pairs)
-    back_x = [shifted(gp[s - 1], "grp", s) for s in range(1, members)]
-    back_end = exchanged(g_far, "blk", ends)
     back_sum = [shifted(sums[s], "grp", s) for s in range(1, members)]
     gx, g_own, g_near = call(
         functools.partial(fourth_body, others),
         [full] * 3,
-        (),
         gx,
         gy,
         slope,
@@ -344,7 +340,6 @@
     grad_x, grad_y, row_loss = finish(
         others,
         3.0 * members * count,
-        at_end,
         unit_x,
         scale_x,
         gx,
@@ -354,7 +349,6 @@
         g_own,
         back_near,
         back_far,
-        back_end,
         sums[0],
         *back_sum,
     )

time: 35.9 us -> 31.2 us (0.87)
  starting transfers between devices: 14 us -> 7.88 us
  waiting for transfers between devices: 12.2 us -> 13.7 us
    ppermute x6 -> x4, starting transfers between devices: 8.6 us -> 3.12 us  [exchanged(): return lax.ppermute(x, axis, pairs + [(b, a) for a, b in pairs])]
    ppermute x4, waiting for transfers between devices: 5.55 us -> 10.4 us  [shifted(): lax.ppermute(x, axis, [(i, (i + by) % length) for i in range(length)])]
    ppermute x6 -> x4, waiting for transfers between devices: 6.63 us -> 3.31 us  [exchanged(): return lax.ppermute(x, axis, pairs + [(b, a) for a, b in pairs])]
    ppermute x4, starting transfers between devices: 5.39 us -> 4.76 us  [shifted(): lax.ppermute(x, axis, [(i, (i + by) % length) for i in range(length)])]
  transfers between devices with their start and end apart: 10 -> 8, of which waited for: 3 -> 4; matrix products, arithmetic and copies ran while one was open for 0% -> 0% of each run, Pallas kernels for 12% -> 14%
where the time goes in v4:
time: 31.2 us; the launch traced here: 31 us
  waiting for transfers between devices  13.7 us (44%)
  starting transfers between devices  7.88 us (25%)
  Pallas kernels  7.44 us (24%)
  between operations  1.98 us (6%)
    ppermute x4, waiting for transfers between devices, shifted(): lax.ppermute(x, axis, [(i, (i + by) % length) for i in range(length)])  10.4 us
    pallas_call x4, Pallas kernels, call(): pl.pallas_call(body, out_shape=[pltpu.VMEM(o.shape, o.dtype) for o in out...  6.23 us
    ppermute x4, starting transfers between devices, shifted(): lax.ppermute(x, axis, [(i, (i + by) % length) for i in range(length)])  4.76 us
    ppermute x4, waiting for transfers between devices, exchanged(): return lax.ppermute(x, axis, pairs + [(b, a) for a, b in pairs])  3.31 us
    ppermute x4, starting transfers between devices, exchanged(): return lax.ppermute(x, axis, pairs + [(b, a) for a, b in pairs])  3.12 us
    pallas_call x1, Pallas kernels, finish(): pl.pallas_call(functools.partial(last_body, others, pairs), out_shape=[fu...  1.21 us
  transfers between devices with their start and end apart: 8, of which 4 were waited for; matrix products, arithmetic and copies ran while one was open for 0% of the time, Pallas kernels for 14%

profile of v4, /device:TPU:1, one launch (start us, length us, event | category | flops | bytes accessed | tf_op | source)
XLA Modules:
  0.0 31.0 jit_solution(4376157302944495819)
XLA Ops:
  0.6 0.0 copy-start
  0.6 0.1 collective-permute-start
  0.7 2.7 %collective-permute-start.3 = (f32[128,768]{1,0:T(8,128)}, f32[128,768]{1,0:T(8,128)S(1)}, u32[]{:S(2)}, u32[]{:S(2)}) collective-permute-start(f32[128,768]{1,0:T(8,128)} %x_any.1), channel_id=1, source_target_pairs={{0,1},{1,0},{2,3},{3,2},{4,5},{5,4},{6,7},{7,6},{8,9},{9,8},{10,11... | collective-permute-start | bytes 1179656 | tf_op jit(solution)/shard_map/ppermute | solution.py:27
  3.4 1.5 %collective-permute-start.1 = (f32[128,768]{1,0:T(8,128)}, f32[128,768]{1,0:T(8,128)S(1)}, u32[]{:S(2)}, u32[]{:S(2)}) collective-permute-start(f32[128,768]{1,0:T(8,128)} %y_any.1), channel_id=1, source_target_pairs={{2,4},{6,8},{10,12},{14,16},{18,20},{22,24},{26,28},{30,0},{4,2},{... | collective-permute-start | bytes 1179656 | tf_op jit(solution)/shard_map/ppermute | solution.py:22
  4.9 0.0 copy-done
  4.9 0.3 collective-permute-start.2
  6.4 0.0 collective-permute-done.near_ref
  6.5 3.2 %shard_map.76 = (f32[2,128]{1,0:T(2,128)S(1)}, f32[128,768]{1,0:T(8,128)S(1)}, f32[128,1]{1,0:T(8,128)S(1)}, f32[128,768]{1,0:T(8,128)S(1)}, f32[128,1]{1,0:T(8,...) custom-call(f32[1]{0:T(128)S(6)} %copy.8.lt, ...), custom_call_target="tpu_custom_call" | custom-call | tf_op jit(solution)/shard_map/pallas_call | solution.py:231
  9.7 3.4 %collective-permute-done.2.refs_1_.refs_2_ = f32[1,128]{1,0:T(1,128)S(1)} collective-permute-done((f32[1,128]{1,0:T(1,128)S(1)}, f32[1,128]{1,0:T(1,128)S(1)}, u32[]{:S(2)}, u32[]{:S(2)}) %collective-permute-start.2) | collective-permute-done | bytes 544 | tf_op jit(solution)/shard_map/ppermute | solution.py:27
  13.0 0.0 collective-permute-done.3.refs_0_
  13.0 1.1 %shard_map.77 = (bf16[512,768]{1,0:T(8,128)(2,1)S(1)}, f32[128,768]{1,0:T(8,128)S(1)}, f32[1,128]{1,0:T(1,128)S(1)}, f32[128,256]{1,0:T(8,128)S(1)}) custom-call(f32[2,128]{1,0:T(2,128)S(1)} %get-tuple-element.33.tb_ref, f32[128,768]{1,0:T(8,128)S(1)} %collective-permute-done.3.refs_0_, f32[1,128]{1,0:T(1,128)S(1)} %collective-permute-done.2.refs_1_.refs_2_, ...), custom_call_target="tpu_custom_call" | custom-call | tf_op jit(solution)/shard_map/pallas_call | solution.py:231
  14.1 0.9 %collective-permute-done.1.refs_0_ = f32[128,768]{1,0:T(8,128)S(1)} collective-permute-done((f32[128,768]{1,0:T(8,128)}, f32[128,768]{1,0:T(8,128)S(1)}, u32[]{:S(2)}, u32[]{:S(2)}) %collective-permute-start.1) | collective-permute-done | bytes 393248 | tf_op jit(solution)/shard_map/ppermute | solution.py:22
  15.0 1.3 %shard_map.78 = (f32[128,768]{1,0:T(8,128)S(1)}, f32[128,768]{1,0:T(8,128)S(1)}, f32[1,128]{1,0:T(1,128)S(1)}, f32[1,128]{1,0:T(1,128)S(1)}, bf16[256,768]{1,0:T(8,128)(2,1)S(1)}, /*index=5*/f32[128,128]{1,0:T(8,128)S(1)}) custom-call(f32[2,128]{1,0:T(2,128)S(1)} %get-tuple-element.33.tb_ref, f32[128,768]{1,0:T(8,128)S(1)} %collective-permute-done.1.refs_0_, ...), custom_call_target="tpu_custom_call" | custom-call | tf_op jit(solution)/shard_map/pallas_call | solution.py:231
  16.3 0.7 %shard_map.79 = (f32[128,768]{1,0:T(8,128)S(1)}, f32[128,768]{1,0:T(8,128)S(1)}, f32[128,768]{1,0:T(8,128)S(1)}) custom-call(f32[128,768]{1,0:T(8,128)S(1)} %get-tuple-element.31.gx_in, f32[256,768]{1,0:T(8,128)S(1)} %get-tuple-element.32.gy_in, f32[128,128]{1,0:T(8,128)S(1)} %get-tuple-element.40.slope_ref, bf16[256,768]{1,0:T(8,128)(2,1)S(1)} %get-tuple-element.41.fs_ref, ...), custom_call_target="tpu_custom_call" | custom-call | tf_op jit(solution)/shard_map/pallas_call | solution.py:231
  17.0 0.1 collective-permute-start.5
  17.1 1.3 %collective-permute-start.4 = (f32[128,768]{1,0:T(8,128)S(1)}, f32[128,768]{1,0:T(8,128)S(1)}, u32[]{:S(2)}, u32[]{:S(2)}) collective-permute-start(f32[128,768]{1,0:T(8,128)S(1)} %get-tuple-element.44), channel_id=1, source_target_pairs={{0,1},{1,0},{2,3},{3,2},{4,5},{5,4},{6,7},{7,6},{8,9},{9,8},{10,11... | collective-permute-start | bytes 1179656 | tf_op jit(solution)/shard_map/ppermute | solution.py:27
  18.4 1.5 %collective-permute-start.6 = (f32[128,768]{1,0:T(8,128)S(1)}, f32[128,768]{1,0:T(8,128)S(1)}, u32[]{:S(2)}, u32[]{:S(2)}) collective-permute-start(f32[128,768]{1,0:T(8,128)S(1)} %get-tuple-element.49), channel_id=1, source_target_pairs={{2,4},{6,8},{10,12},{14,16},{18,20},{22,24},{26,28},{30,0},{4,2},{... | collective-permute-start | bytes 1179656 | tf_op jit(solution)/shard_map/ppermute | solution.py:22
  19.9 0.5 %collective-permute-start.7 = (f32[1,128]{1,0:T(1,128)S(1)}, f32[1,128]{1,0:T(1,128)S(1)}, u32[]{:S(2)}, u32[]{:S(2)}) collective-permute-start(f32[1,128]{1,0:T(1,128)S(1)} %get-tuple-element.51), channel_id=1, source_target_pairs={{0,1},{1,0},{2,3},{3,2},{4,5},{5,4},{6,7},{7,6},{8,9},{9,8},{10,11... | collective-permute-start | bytes 1544 | tf_op jit(solution)/shard_map/ppermute | solution.py:27
  20.4 7.0 %collective-permute-done.7.refs_10_ = f32[1,128]{1,0:T(1,128)S(1)} collective-permute-done((f32[1,128]{1,0:T(1,128)S(1)}, f32[1,128]{1,0:T(1,128)S(1)}, u32[]{:S(2)}, u32[]{:S(2)}) %collective-permute-start.7) | collective-permute-done | bytes 544 | tf_op jit(solution)/shard_map/ppermute | solution.py:27
  27.4 0.0 collective-permute-done.5.refs_7_
  27.4 0.0 collective-permute-done.4.refs_3_
  27.4 2.4 %collective-permute-done.6.refs_8_ = f32[128,768]{1,0:T(8,128)S(1)} collective-permute-done((f32[128,768]{1,0:T(8,128)S(1)}, f32[128,768]{1,0:T(8,128)S(1)}, u32[]{:S(2)}, u32[]{:S(2)}) %collective-permute-start.6) | collective-permute-done | bytes 393248 | tf_op jit(solution)/shard_map/ppermute | solution.py:22
  29.8 1.2 %shard_map.80 = (f32[128,768]{1,0:T(8,128)}, f32[128,768]{1,0:T(8,128)}, f32[1,128]{1,0:T(1,128)}) custom-call(f32[128,768]{1,0:T(8,128)S(1)} %get-tuple-element.29.refs_0_, f32[128,1]{1,0:T(8,128)S(1)} %get-tuple-element.30.refs_1_, f32[128,768]{1,0:T(8,128)S(1)} %get-tuple-element.43.refs_2_, f32[128,768]{1,0:T(8,128)S(1)} %collective-permute-done.4.refs_3_, ...), custom_call_target="tpu_custom_call" | custom-call | tf_op jit(solution)/shard_map/pallas_call | solution.py:244
Async XLA Ops:
  0.6 4.3 %copy-start = (f32[128]{0:T(128)S(1)}, f32[128]{0:T(128)}, u32[]{:S(2)}) copy-start(f32[128]{0:T(128)} %param.9) | copy-start | bytes 1540
  0.6 5.8 %collective-permute-start = (f32[128,768]{1,0:T(8,128)}, f32[128,768]{1,0:T(8,128)S(1)}, u32[]{:S(2)}, u32[]{:S(2)}) collective-permute-start(f32[128,768]{1,0:T(8,128)} %y_any.1), channel_id=1, source_target_pairs={{0,2},{4,6},{8,10},{12,14},{16,18},{20,22},{24,26},{28,30},{2,0},{... | collective-permute-start | bytes 1179656 | tf_op jit(solution)/shard_map/ppermute | solution.py:22
  0.7 12.3 %collective-permute-start.3 = (f32[128,768]{1,0:T(8,128)}, f32[128,768]{1,0:T(8,128)S(1)}, u32[]{:S(2)}, u32[]{:S(2)}) collective-permute-start(f32[128,768]{1,0:T(8,128)} %x_any.1), channel_id=1, source_target_pairs={{0,1},{1,0},{2,3},{3,2},{4,5},{5,4},{6,7},{7,6},{8,9},{9,8},{10,11... | collective-permute-start | bytes 1179656 | tf_op jit(solution)/shard_map/ppermute | solution.py:27
  3.4 11.6 %collective-permute-start.1 = (f32[128,768]{1,0:T(8,128)}, f32[128,768]{1,0:T(8,128)S(1)}, u32[]{:S(2)}, u32[]{:S(2)}) collective-permute-start(f32[128,768]{1,0:T(8,128)} %y_any.1), channel_id=1, source_target_pairs={{2,4},{6,8},{10,12},{14,16},{18,20},{22,24},{26,28},{30,0},{4,2},{... | collective-permute-start | bytes 1179656 | tf_op jit(solution)/shard_map/ppermute | solution.py:22
  4.9 8.1 %collective-permute-start.2 = (f32[1,128]{1,0:T(1,128)S(1)}, f32[1,128]{1,0:T(1,128)S(1)}, u32[]{:S(2)}, u32[]{:S(2)}) collective-permute-start(f32[1,128]{1,0:T(1,128)S(1)} %bitcast.2), channel_id=1, source_target_pairs={{0,1},{1,0},{2,3},{3,2},{4,5},{5,4},{6,7},{7,6},{8,9},{9,8},{10,11... | collective-permute-start | bytes 1544 | tf_op jit(solution)/shard_map/ppermute | solution.py:27
  17.0 10.4 %collective-permute-start.5 = (f32[128,768]{1,0:T(8,128)S(1)}, f32[128,768]{1,0:T(8,128)S(1)}, u32[]{:S(2)}, u32[]{:S(2)}) collective-permute-start(f32[128,768]{1,0:T(8,128)S(1)} %get-tuple-element.48), channel_id=1, source_target_pairs={{0,2},{4,6},{8,10},{12,14},{16,18},{20,22},{24,26},{28,30},{2,0},{... | collective-permute-start | bytes 1179656 | tf_op jit(solution)/shard_map/ppermute | solution.py:22
  17.1 10.3 %collective-permute-start.4 = (f32[128,768]{1,0:T(8,128)S(1)}, f32[128,768]{1,0:T(8,128)S(1)}, u32[]{:S(2)}, u32[]{:S(2)}) collective-permute-start(f32[128,768]{1,0:T(8,128)S(1)} %get-tuple-element.44), channel_id=1, source_target_pairs={{0,1},{1,0},{2,3},{3,2},{4,5},{5,4},{6,7},{7,6},{8,9},{9,8},{10,11... | collective-permute-start | bytes 1179656 | tf_op jit(solution)/shard_map/ppermute | solution.py:27
  18.4 11.4 %collective-permute-start.6 = (f32[128,768]{1,0:T(8,128)S(1)}, f32[128,768]{1,0:T(8,128)S(1)}, u32[]{:S(2)}, u32[]{:S(2)}) collective-permute-start(f32[128,768]{1,0:T(8,128)S(1)} %get-tuple-element.49), channel_id=1, source_target_pairs={{2,4},{6,8},{10,12},{14,16},{18,20},{22,24},{26,28},{30,0},{4,2},{... | collective-permute-start | bytes 1179656 | tf_op jit(solution)/shard_map/ppermute | solution.py:22
  19.9 7.5 %collective-permute-start.7 = (f32[1,128]{1,0:T(1,128)S(1)}, f32[1,128]{1,0:T(1,128)S(1)}, u32[]{:S(2)}, u32[]{:S(2)}) collective-permute-start(f32[1,128]{1,0:T(1,128)S(1)} %get-tuple-element.51), channel_id=1, source_target_pairs={{0,1},{1,0},{2,3},{3,2},{4,5},{5,4},{6,7},{7,6},{8,9},{9,8},{10,11... | collective-permute-start | bytes 1544 | tf_op jit(solution)/shard_map/ppermute | solution.py:27

commit v5 on v4

--- a/solution.py
+++ b/solution.py
@@ -103,7 +103,7 @@
 def second_body(others, tb_ref, *refs):
     raw_refs, refs = refs[:others], refs[others:]
     w_refs, refs = refs[:others], refs[others:]
-    xs_ref, ys_ref, all_ref, refs = *refs[:3], refs[3:]
+    xs_ref, ys_ref, gy_in, all_ref, gnear_ref, refs = *refs[:5], refs[5:]
     gp_refs, refs = refs[:others], refs[others:]
     sump_refs, slope_refs = refs[:others], refs[others:]
     temper, bias = scalars_of(tb_ref)
@@ -112,6 +112,7 @@
     eye = square(count)
     all_ref[:count] = xs_ref[:count]
     all_ref[deep : deep + count] = xs_ref[count:]
+    near = gy_in[count:]
     for s in range(others):
         raw = raw_refs[s][...]
         px = stacked(raw * scale_of(raw))
@@ -123,8 +124,10 @@
         loss, slope = gated(z, weight * temper)
         sums = jnp.sum(loss, axis=1, keepdims=True)
         sump_refs[s][...] = jnp.sum(jnp.where(eye, sums, 0.0), axis=0, keepdims=True)
-        slope_refs[s][...] = slope
+        slope_refs[s][...] = slope[:, :count]
+        near = near + mm(stacked(slope[:, count:].T), px, NN)
         gp_refs[s][...] = mm(stacked(slope), ys_ref, NN)
+    gnear_ref[...] = near
 
 
 def third_body(others, tb_ref, *refs):
@@ -159,18 +162,17 @@
 
 
 def fourth_body(others, gx_in, gy_in, slope_ref, fs_ref, all_ref, *refs):
-    slopes, (gx_ref, gown_ref, gnear_ref) = refs[:others], refs[others:]
+    slopes, (gx_ref, gown_ref) = refs[:others], refs[others:]
     count = gx_in.shape[0]
     deep = (others + 1) * count
-    gy = gy_in[...]
+    gy = gy_in[:count]
     for s in range(others):
         here = (s + 1) * count
         px = jnp.concatenate(
             [all_ref[here : here + count], all_ref[deep + here : deep + here + count]], axis=0
         )
         gy = gy + mm(stacked(slopes[s][...].T), px, NN)
-    gown_ref[...] = gy[:count]
-    gnear_ref[...] = gy[count:]
+    gown_ref[...] = gy
     gx_ref[...] = gx_in[...] + mm(stacked(slope_ref[...].T), fs_ref, NN)
 
 
@@ -187,26 +189,28 @@
         copies.append(pltpu.make_async_copy(source, target, sem.at[len(copies)]))
         copies[-1].start()
 
-    def through(k, here, unit, scale, grad, out_ref):
-        inner = jnp.sum(unit * grad, axis=1, keepdims=True)
-        held[k, here, :] = scale * (grad - unit * inner)
-        send(held.at[k, here, :], out_ref.at[here, :])
-
     total = sums[0][...]
     for r in sums[1:]:
         total = total + r[...]
     line[...] = total / pairs
     send(line, loss_out)
-    for c in range(CHUNKS):
-        here = pl.ds(c * rows, rows)
-        grad = own_x[here, :]
-        for r in back_x:
-            grad = grad + r[here, :]
-        through(0, here, unit_x[here, :], scale_x[here, :], grad, x_out)
-    for c in range(CHUNKS):
-        here = pl.ds(c * rows, rows)
-        grad = own_y[here, :] + near_y[here, :] + far_y[here, :]
-        through(1, here, unit_y[here, :], scale_y[here, :], grad, y_out)
+    sides = [
+        (unit_x, scale_x, [own_x, *back_x], x_out),
+        (unit_y, scale_y, [own_y, near_y, far_y], y_out),
+    ]
+    inners = []
+    for k, (unit, _, grads, _) in enumerate(sides):
+        grad = grads[0][...]
+        for r in grads[1:]:
+            grad = grad + r[...]
+        held[k] = grad
+        inners.append(jnp.sum(unit[...] * grad, axis=1, keepdims=True))
+    for k, (unit, scale, _, out_ref) in enumerate(sides):
+        for c in range(CHUNKS):
+            low, high = c * rows, (c + 1) * rows
+            inner = inners[k][low:high]
+            held[k, low:high] = scale[low:high] * (held[k, low:high] - unit[low:high] * inner)
+            send(held.at[k, pl.ds(low, rows), :], out_ref.at[pl.ds(low, rows), :])
     for copy in copies:
         copy.wait()
 
@@ -296,19 +300,21 @@
     )
     outs = call(
         functools.partial(second_body, others),
-        [shape(2 * members * count, width, kind=BF)]
+        [shape(2 * members * count, width, kind=BF), full]
         + [full] * others
         + [line] * others
-        + [shape(count, 2 * count)] * others,
+        + [shape(count, count)] * others,
         tb,
         *raws,
         *weights[1:],
         xs,
         ys,
-    )
-    everyone, outs = outs[0], outs[1:]
+        gy,
+    )
+    everyone, g_near, outs = outs[0], outs[1], outs[2:]
     gp, outs = outs[:others], outs[others:]
     sump, slopes = outs[:others], outs[others:]
+    back_near = exchanged(g_near, "blk", near_pairs)
     outs = call(
         functools.partial(third_body, others),
         [full] + [full] * others + [line] * members + [stack, shape(count, count)],
@@ -326,9 +332,9 @@
     back_x = [shifted(gp[s - 1], "grp", s) for s in range(1, members)]
     back_far = exchanged(g_far, "blk", far_pairs)
     back_sum = [shifted(sums[s], "grp", s) for s in range(1, members)]
-    gx, g_own, g_near = call(
+    gx, g_own = call(
         functools.partial(fourth_body, others),
-        [full] * 3,
+        [full] * 2,
         gx,
         gy,
         slope,
@@ -336,7 +342,6 @@
         everyone,
         *slopes,
     )
-    back_near = exchanged(g_near, "blk", near_pairs)
     grad_x, grad_y, row_loss = finish(
         others,
         3.0 * members * count,

time: 31.2 us -> 30.5 us (0.978)
  waiting for transfers between devices: 13.7 us -> 10.7 us
  starting transfers between devices: 7.88 us -> 10.1 us
    ppermute x4, starting transfers between devices: 3.12 us -> 6.24 us  [exchanged(): return lax.ppermute(x, axis, pairs + [(b, a) for a, b in pairs])]
    ppermute x4, waiting for transfers between devices: 10.4 us -> 7.9 us  [shifted(): lax.ppermute(x, axis, [(i, (i + by) % length) for i in range(length)])]
    ppermute x4, starting transfers between devices: 4.76 us -> 3.84 us  [shifted(): lax.ppermute(x, axis, [(i, (i + by) % length) for i in range(length)])]
    ppermute x4, waiting for transfers between devices: 3.31 us -> 2.75 us  [exchanged(): return lax.ppermute(x, axis, pairs + [(b, a) for a, b in pairs])]
  transfers between devices with their start and end apart: 8 -> 8, of which waited for: 4 -> 4; matrix products, arithmetic and copies ran while one was open for 0% -> 0% of each run, Pallas kernels for 14% -> 17%
where the time goes in v5:
time: 30.5 us; the launch traced here: 30.3 us
  waiting for transfers between devices  10.7 us (35%)
  starting transfers between devices  10.1 us (33%)
  Pallas kernels  7.6 us (25%)
  between operations  1.98 us (6%)
    ppermute x4, waiting for transfers between devices, shifted(): lax.ppermute(x, axis, [(i, (i + by) % length) for i in range(length)])  7.9 us
    pallas_call x4, Pallas kernels, call(): pl.pallas_call(body, out_shape=[pltpu.VMEM(o.shape, o.dtype) for o in out...  6.37 us
    ppermute x4, starting transfers between devices, exchanged(): return lax.ppermute(x, axis, pairs + [(b, a) for a, b in pairs])  6.24 us
    ppermute x4, starting transfers between devices, shifted(): lax.ppermute(x, axis, [(i, (i + by) % length) for i in range(length)])  3.84 us
    ppermute x4, waiting for transfers between devices, exchanged(): return lax.ppermute(x, axis, pairs + [(b, a) for a, b in pairs])  2.75 us
    pallas_call x1, Pallas kernels, finish(): pl.pallas_call(functools.partial(last_body, others, pairs), out_shape=[fu...  1.24 us
  transfers between devices with their start and end apart: 8, of which 4 were waited for; matrix products, arithmetic and copies ran while one was open for 0% of the time, Pallas kernels for 17%

profile of v5, /device:TPU:1, one launch (start us, length us, event | category | flops | bytes accessed | tf_op | source)
XLA Modules:
  0.0 30.3 jit_solution(8949312155549551622)
XLA Ops:
  0.6 0.0 copy-start
  0.6 0.1 collective-permute-start
  0.7 2.7 %collective-permute-start.3 = (f32[128,768]{1,0:T(8,128)}, f32[128,768]{1,0:T(8,128)S(1)}, u32[]{:S(2)}, u32[]{:S(2)}) collective-permute-start(f32[128,768]{1,0:T(8,128)} %x_any.1), channel_id=1, source_target_pairs={{0,1},{1,0},{2,3},{3,2},{4,5},{5,4},{6,7},{7,6},{8,9},{9,8},{10,11... | collective-permute-start | bytes 1179656 | tf_op jit(solution)/shard_map/ppermute | solution.py:27
  3.4 1.5 %collective-permute-start.1 = (f32[128,768]{1,0:T(8,128)}, f32[128,768]{1,0:T(8,128)S(1)}, u32[]{:S(2)}, u32[]{:S(2)}) collective-permute-start(f32[128,768]{1,0:T(8,128)} %y_any.1), channel_id=1, source_target_pairs={{2,4},{6,8},{10,12},{14,16},{18,20},{22,24},{26,28},{30,0},{4,2},{... | collective-permute-start | bytes 1179656 | tf_op jit(solution)/shard_map/ppermute | solution.py:22
  4.9 0.0 copy-done
  4.9 0.3 collective-permute-start.2
  6.4 0.0 collective-permute-done.near_ref
  6.5 3.2 %shard_map.76 = (f32[2,128]{1,0:T(2,128)S(1)}, f32[128,768]{1,0:T(8,128)S(1)}, f32[128,1]{1,0:T(8,128)S(1)}, f32[128,768]{1,0:T(8,128)S(1)}, f32[128,1]{1,0:T(8,...) custom-call(f32[1]{0:T(128)S(6)} %copy.8.lt, ...), custom_call_target="tpu_custom_call" | custom-call | tf_op jit(solution)/shard_map/pallas_call | solution.py:235
  9.7 3.4 %collective-permute-done.2.refs_1_.refs_2_ = f32[1,128]{1,0:T(1,128)S(1)} collective-permute-done((f32[1,128]{1,0:T(1,128)S(1)}, f32[1,128]{1,0:T(1,128)S(1)}, u32[]{:S(2)}, u32[]{:S(2)}) %collective-permute-start.2) | collective-permute-done | bytes 544 | tf_op jit(solution)/shard_map/ppermute | solution.py:27
  13.0 0.0 collective-permute-done.3.refs_0_
  13.0 1.4 %shard_map.77 = (bf16[512,768]{1,0:T(8,128)(2,1)S(1)}, f32[128,768]{1,0:T(8,128)S(1)}, f32[128,768]{1,0:T(8,128)S(1)}, f32[1,128]{1,0:T(1,128)S(1)}, f32[128,128]{1,0:T(8,128)S(1)}) custom-call(f32[2,128]{1,0:T(2,128)S(1)} %get-tuple-element.33.tb_ref, f32[128,768]{1,0:T(8,128)S(1)} %collective-permute-done.3.refs_0_, ...), custom_call_target="tpu_custom_call" | custom-call | tf_op jit(solution)/shard_map/pallas_call | solution.py:235
  14.4 0.6 %collective-permute-done.1.refs_0_ = f32[128,768]{1,0:T(8,128)S(1)} collective-permute-done((f32[128,768]{1,0:T(8,128)}, f32[128,768]{1,0:T(8,128)S(1)}, u32[]{:S(2)}, u32[]{:S(2)}) %collective-permute-start.1) | collective-permute-done | bytes 393248 | tf_op jit(solution)/shard_map/ppermute | solution.py:22
  15.0 1.3 %shard_map.78 = (f32[128,768]{1,0:T(8,128)S(1)}, f32[128,768]{1,0:T(8,128)S(1)}, f32[1,128]{1,0:T(1,128)S(1)}, f32[1,128]{1,0:T(1,128)S(1)}, bf16[256,768]{1,0:T(8,128)(2,1)S(1)}, /*index=5*/f32[128,128]{1,0:T(8,128)S(1)}) custom-call(f32[2,128]{1,0:T(2,128)S(1)} %get-tuple-element.33.tb_ref, f32[128,768]{1,0:T(8,128)S(1)} %collective-permute-done.1.refs_0_, ...), custom_call_target="tpu_custom_call" | custom-call | tf_op jit(solution)/shard_map/pallas_call | solution.py:235
  16.3 0.6 %collective-permute-start.4 = (f32[128,768]{1,0:T(8,128)S(1)}, f32[128,768]{1,0:T(8,128)S(1)}, u32[]{:S(2)}, u32[]{:S(2)}) collective-permute-start(f32[128,768]{1,0:T(8,128)S(1)} %get-tuple-element.44), channel_id=1, source_target_pairs={{0,1},{1,0},{2,3},{3,2},{4,5},{5,4},{6,7},{7,6},{8,9},{9,8},{10,11... | collective-permute-start | bytes 1179656 | tf_op jit(solution)/shard_map/ppermute | solution.py:27
  17.0 2.4 %collective-permute-start.6 = (f32[128,768]{1,0:T(8,128)S(1)}, f32[128,768]{1,0:T(8,128)S(1)}, u32[]{:S(2)}, u32[]{:S(2)}) collective-permute-start(f32[128,768]{1,0:T(8,128)S(1)} %get-tuple-element.49), channel_id=1, source_target_pairs={{2,4},{6,8},{10,12},{14,16},{18,20},{22,24},{26,28},{30,0},{4,2},{... | collective-permute-start | bytes 1179656 | tf_op jit(solution)/shard_map/ppermute | solution.py:22
  19.4 2.2 %collective-permute-start.5 = (f32[128,768]{1,0:T(8,128)S(1)}, f32[128,768]{1,0:T(8,128)S(1)}, u32[]{:S(2)}, u32[]{:S(2)}) collective-permute-start(f32[128,768]{1,0:T(8,128)S(1)} %get-tuple-element.48), channel_id=1, source_target_pairs={{0,2},{4,6},{8,10},{12,14},{16,18},{20,22},{24,26},{28,30},{2,0},{... | collective-permute-start | bytes 1179656 | tf_op jit(solution)/shard_map/ppermute | solution.py:22
  21.7 0.3 collective-permute-start.7
  21.9 0.5 %shard_map.79 = (f32[128,768]{1,0:T(8,128)S(1)}, f32[128,768]{1,0:T(8,128)S(1)}) custom-call(f32[128,768]{1,0:T(8,128)S(1)} %get-tuple-element.31.gx_in, f32[256,768]{1,0:T(8,128)S(1)} %get-tuple-element.32.refs_4_.gy_in, f32[128,128]{1,0:T(8,128)S(1)} %get-tuple-element.40.slope_ref, bf16[256,768]{1,0:T(8,128)(2,1)S(1)} %get-tuple-element.41.fs_ref, ...), custom_call_target="tpu_custom_call" | custom-call | tf_op jit(solution)/shard_map/pallas_call | solution.py:235
  22.4 4.5 %collective-permute-done.7.refs_10_ = f32[1,128]{1,0:T(1,128)S(1)} collective-permute-done((f32[1,128]{1,0:T(1,128)S(1)}, f32[1,128]{1,0:T(1,128)S(1)}, u32[]{:S(2)}, u32[]{:S(2)}) %collective-permute-start.7) | collective-permute-done | bytes 544 | tf_op jit(solution)/shard_map/ppermute | solution.py:27
  26.9 0.0 collective-permute-done.4.refs_3_
  27.0 2.1 %collective-permute-done.6.refs_8_ = f32[128,768]{1,0:T(8,128)S(1)} collective-permute-done((f32[128,768]{1,0:T(8,128)S(1)}, f32[128,768]{1,0:T(8,128)S(1)}, u32[]{:S(2)}, u32[]{:S(2)}) %collective-permute-start.6) | collective-permute-done | bytes 393248 | tf_op jit(solution)/shard_map/ppermute | solution.py:22
  29.1 0.0 collective-permute-done.5.refs_7_
  29.1 1.2 %shard_map.80 = (f32[128,768]{1,0:T(8,128)}, f32[128,768]{1,0:T(8,128)}, f32[1,128]{1,0:T(1,128)}) custom-call(f32[128,768]{1,0:T(8,128)S(1)} %get-tuple-element.29.refs_0_, f32[128,1]{1,0:T(8,128)S(1)} %get-tuple-element.30.refs_1_, f32[128,768]{1,0:T(8,128)S(1)} %get-tuple-element.43.refs_2_, f32[128,768]{1,0:T(8,128)S(1)} %collective-permute-done.4.refs_3_, ...), custom_call_target="tpu_custom_call" | custom-call | tf_op jit(solution)/shard_map/pallas_call | solution.py:248
Async XLA Ops:
  0.6 4.3 %copy-start = (f32[128]{0:T(128)S(1)}, f32[128]{0:T(128)}, u32[]{:S(2)}) copy-start(f32[128]{0:T(128)} %param.9) | copy-start | bytes 1540
  0.6 5.8 %collective-permute-start = (f32[128,768]{1,0:T(8,128)}, f32[128,768]{1,0:T(8,128)S(1)}, u32[]{:S(2)}, u32[]{:S(2)}) collective-permute-start(f32[128,768]{1,0:T(8,128)} %y_any.1), channel_id=1, source_target_pairs={{0,2},{4,6},{8,10},{12,14},{16,18},{20,22},{24,26},{28,30},{2,0},{... | collective-permute-start | bytes 1179656 | tf_op jit(solution)/shard_map/ppermute | solution.py:22
  0.7 12.3 %collective-permute-start.3 = (f32[128,768]{1,0:T(8,128)}, f32[128,768]{1,0:T(8,128)S(1)}, u32[]{:S(2)}, u32[]{:S(2)}) collective-permute-start(f32[128,768]{1,0:T(8,128)} %x_any.1), channel_id=1, source_target_pairs={{0,1},{1,0},{2,3},{3,2},{4,5},{5,4},{6,7},{7,6},{8,9},{9,8},{10,11... | collective-permute-start | bytes 1179656 | tf_op jit(solution)/shard_map/ppermute | solution.py:27
  3.4 11.6 %collective-permute-start.1 = (f32[128,768]{1,0:T(8,128)}, f32[128,768]{1,0:T(8,128)S(1)}, u32[]{:S(2)}, u32[]{:S(2)}) collective-permute-start(f32[128,768]{1,0:T(8,128)} %y_any.1), channel_id=1, source_target_pairs={{2,4},{6,8},{10,12},{14,16},{18,20},{22,24},{26,28},{30,0},{4,2},{... | collective-permute-start | bytes 1179656 | tf_op jit(solution)/shard_map/ppermute | solution.py:22
  4.9 8.1 %collective-permute-start.2 = (f32[1,128]{1,0:T(1,128)S(1)}, f32[1,128]{1,0:T(1,128)S(1)}, u32[]{:S(2)}, u32[]{:S(2)}) collective-permute-start(f32[1,128]{1,0:T(1,128)S(1)} %bitcast.2), channel_id=1, source_target_pairs={{0,1},{1,0},{2,3},{3,2},{4,5},{5,4},{6,7},{7,6},{8,9},{9,8},{10,11... | collective-permute-start | bytes 1544 | tf_op jit(solution)/shard_map/ppermute | solution.py:27
  16.3 10.6 %collective-permute-start.4 = (f32[128,768]{1,0:T(8,128)S(1)}, f32[128,768]{1,0:T(8,128)S(1)}, u32[]{:S(2)}, u32[]{:S(2)}) collective-permute-start(f32[128,768]{1,0:T(8,128)S(1)} %get-tuple-element.44), channel_id=1, source_target_pairs={{0,1},{1,0},{2,3},{3,2},{4,5},{5,4},{6,7},{7,6},{8,9},{9,8},{10,11... | collective-permute-start | bytes 1179656 | tf_op jit(solution)/shard_map/ppermute | solution.py:27
  17.0 12.1 %collective-permute-start.6 = (f32[128,768]{1,0:T(8,128)S(1)}, f32[128,768]{1,0:T(8,128)S(1)}, u32[]{:S(2)}, u32[]{:S(2)}) collective-permute-start(f32[128,768]{1,0:T(8,128)S(1)} %get-tuple-element.49), channel_id=1, source_target_pairs={{2,4},{6,8},{10,12},{14,16},{18,20},{22,24},{26,28},{30,0},{4,2},{... | collective-permute-start | bytes 1179656 | tf_op jit(solution)/shard_map/ppermute | solution.py:22
  19.4 9.7 %collective-permute-start.5 = (f32[128,768]{1,0:T(8,128)S(1)}, f32[128,768]{1,0:T(8,128)S(1)}, u32[]{:S(2)}, u32[]{:S(2)}) collective-permute-start(f32[128,768]{1,0:T(8,128)S(1)} %get-tuple-element.48), channel_id=1, source_target_pairs={{0,2},{4,6},{8,10},{12,14},{16,18},{20,22},{24,26},{28,30},{2,0},{... | collective-permute-start | bytes 1179656 | tf_op jit(solution)/shard_map/ppermute | solution.py:22
  21.7 5.3 %collective-permute-start.7 = (f32[1,128]{1,0:T(1,128)S(1)}, f32[1,128]{1,0:T(1,128)S(1)}, u32[]{:S(2)}, u32[]{:S(2)}) collective-permute-start(f32[1,128]{1,0:T(1,128)S(1)} %get-tuple-element.51), channel_id=1, source_target_pairs={{0,1},{1,0},{2,3},{3,2},{4,5},{5,4},{6,7},{7,6},{8,9},{9,8},{10,11... | collective-permute-start | bytes 1544 | tf_op jit(solution)/shard_map/ppermute | solution.py:27

commit v6 on v4

--- a/solution.py
+++ b/solution.py
@@ -20,6 +20,25 @@
 
 def exchanged(x, axis, pairs):
     return lax.ppermute(x, axis, pairs + [(b, a) for (a, b) in pairs])
+
+
+def mixed_pairs(length, members):
+    first, second = [], []
+    for b in range(length):
+        far = (b + 1) % length if b % 2 else (b - 1) % length
+        for g in range(members):
+            here = b * members + g
+            across = (here, far * members + g)
+            along = (here, b * members + (g + 1) % members)
+            direct = length % 4 == 0 and b % 4 in (1, 2)
+            first.append(across if direct else along)
+            second.append(along if direct else across)
+    return first, second
+
+
+def far_goes_first():
+    place = lax.axis_index("blk")
+    return (lax.axis_size("blk") % 4 == 0) & (lax.rem(place + 1, 4) >= 2)
 
 
 def shifted(x, axis, by):
@@ -134,10 +153,10 @@
     all_ref, refs = refs[0], refs[1:]
     gp_in, refs = refs[:others], refs[others:]
     sum_in, refs = refs[:members], refs[members:]
-    gfar_ref, refs = refs[0], refs[1:]
-    gp_refs, refs = refs[:others], refs[others:]
+    one_ref, two_ref, refs = *refs[:2], refs[2:]
+    gp_refs, refs = refs[: others - 1], refs[others - 1 :]
     sum_refs, refs = refs[:members], refs[members:]
-    fs_ref, slope_ref = refs
+    fs_ref, slope_ref, both_ref, turned_ref = refs
     temper, bias = scalars_of(tb_ref)
     count = far_ref.shape[0]
     far = far_ref[...]
@@ -146,7 +165,7 @@
     z = (temper * scale) * mm(fs_ref, all_ref, NT) + bias
     weight = jnp.concatenate([w[...] for w in w_refs], axis=1) * temper
     loss, slope = gated(z, weight)
-    gfar_ref[...] = mm(stacked(slope), all_ref, NN)
+    both_ref[...] = stacked(slope)
     slope = slope * scale
     sums = jnp.sum(loss, axis=0, keepdims=True)
     for s in range(members):
@@ -155,7 +174,17 @@
         if s == 0:
             slope_ref[...] = slope[:, part]
         else:
-            gp_refs[s - 1][...] = gp_in[s - 1][...] + mm(stacked(slope[:, part].T), fs_ref, NN)
+            turned_ref[s - 1] = stacked(slope[:, part].T)
+            if s > 1:
+                gp_refs[s - 2][...] = gp_in[s - 1][...] + mm(turned_ref[s - 1], fs_ref, NN)
+
+    def finish_into(far_out, next_out):
+        far_out[...] = mm(both_ref, all_ref, NN)
+        next_out[...] = gp_in[0][...] + mm(turned_ref[0], fs_ref, NN)
+
+    far_first = far_goes_first()
+    pl.when(far_first)(lambda: finish_into(one_ref, two_ref))
+    pl.when(jnp.logical_not(far_first))(lambda: finish_into(two_ref, one_ref))
 
 
 def fourth_body(others, gx_in, gy_in, slope_ref, fs_ref, all_ref, *refs):
@@ -176,39 +205,44 @@
 
 def last_body(others, pairs, *refs):
     (unit_x, scale_x, own_x), refs = refs[:3], refs[3:]
-    back_x, refs = refs[:others], refs[others:]
-    (unit_y, scale_y, own_y, near_y, far_y), refs = refs[:5], refs[5:]
+    back_x, refs = refs[: others - 1], refs[others - 1 :]
+    (unit_y, scale_y, own_y, near_y, one, two), refs = refs[:6], refs[6:]
     sums, refs = refs[: others + 1], refs[others + 1 :]
     x_out, y_out, loss_out, held, line, sem = refs
     rows = unit_x.shape[0] // CHUNKS
-    copies = []
-
-    def send(source, target):
-        copies.append(pltpu.make_async_copy(source, target, sem.at[len(copies)]))
-        copies[-1].start()
-
-    def through(k, here, unit, scale, grad, out_ref):
-        inner = jnp.sum(unit * grad, axis=1, keepdims=True)
-        held[k, here, :] = scale * (grad - unit * inner)
-        send(held.at[k, here, :], out_ref.at[here, :])
-
     total = sums[0][...]
     for r in sums[1:]:
         total = total + r[...]
     line[...] = total / pairs
-    send(line, loss_out)
-    for c in range(CHUNKS):
-        here = pl.ds(c * rows, rows)
-        grad = own_x[here, :]
-        for r in back_x:
-            grad = grad + r[here, :]
-        through(0, here, unit_x[here, :], scale_x[here, :], grad, x_out)
-    for c in range(CHUNKS):
-        here = pl.ds(c * rows, rows)
-        grad = own_y[here, :] + near_y[here, :] + far_y[here, :]
-        through(1, here, unit_y[here, :], scale_y[here, :], grad, y_out)
-    for copy in copies:
-        copy.wait()
+
+    def run(far_y, next_x):
+        copies = []
+
+        def send(source, target):
+            copies.append(pltpu.make_async_copy(source, target, sem.at[len(copies)]))
+            copies[-1].start()
+
+        send(line, loss_out)
+        sides = [
+            (unit_x, scale_x, [own_x, next_x, *back_x], x_out),
+            (unit_y, scale_y, [own_y, near_y, far_y], y_out),
+        ]
+        for k, (unit_ref, scale_ref, grads, out_ref) in enumerate(sides):
+            for c in range(CHUNKS):
+                here = pl.ds(c * rows, rows)
+                grad = grads[0][here, :]
+                for r in grads[1:]:
+                    grad = grad + r[here, :]
+                unit = unit_ref[here, :]
+                inner = jnp.sum(unit * grad, axis=1, keepdims=True)
+                held[k, here, :] = scale_ref[here, :] * (grad - unit * inner)
+                send(held.at[k, here, :], out_ref.at[here, :])
+        for copy in copies:
+            copy.wait()
+
+    far_first = far_goes_first()
+    pl.when(far_first)(lambda: run(one, two))
+    pl.when(jnp.logical_not(far_first))(lambda: run(two, one))
 
 
 def shape(*dims, kind=F32):
@@ -311,7 +345,10 @@
     sump, slopes = outs[:others], outs[others:]
     outs = call(
         functools.partial(third_body, others),
-        [full] + [full] * others + [line] * members + [stack, shape(count, count)],
+        [full, full]
+        + [full] * (others - 1)
+        + [line] * members
+        + [stack, shape(count, count)],
         tb,
         far,
         *weights,
@@ -319,12 +356,18 @@
         *gp,
         sums,
         *sump,
-    )
-    g_far, outs = outs[0], outs[1:]
-    gp, outs = outs[:others], outs[others:]
+        scratch=[
+            pltpu.VMEM((2 * count, members * count), BF),
+            pltpu.VMEM((others, 2 * count, count), BF),
+        ],
+    )
+    one, two, outs = outs[0], outs[1], outs[2:]
+    gp, outs = outs[: others - 1], outs[others - 1 :]
     sums, (fs, slope) = outs[:members], outs[members:]
-    back_x = [shifted(gp[s - 1], "grp", s) for s in range(1, members)]
-    back_far = exchanged(g_far, "blk", far_pairs)
+    first, second = mixed_pairs(length, members)
+    one = lax.ppermute(one, ("blk", "grp"), first)
+    two = lax.ppermute(two, ("blk", "grp"), second)
+    back_x = [shifted(gp[s - 2], "grp", s) for s in range(2, members)]
     back_sum = [shifted(sums[s], "grp", s) for s in range(1, members)]
     gx, g_own, g_near = call(
         functools.partial(fourth_body, others),
@@ -348,7 +391,8 @@
         scale_y,
         g_own,
         back_near,
-        back_far,
+        one,
+        two,
         sums[0],
         *back_sum,
     )

time: 31.2 us -> 30.2 us (0.968)
  waiting for transfers between devices: 13.7 us -> 13.2 us
    ppermute x0 -> x2, starting transfers between devices: none -> 2.49 us  [the longest x1 1.55 us: body(): one = lax.ppermute(one, ('blk', 'grp'), first)]
    ppermute x4 -> x3, waiting for transfers between devices: 3.31 us -> 0.93 us  [exchanged(): return lax.ppermute(x, axis, pairs + [(b, a) for a, b in pairs])]
    ppermute x4 -> x3, waiting for transfers between devices: 10.4 us -> 12.3 us  [shifted(): lax.ppermute(x, axis, [(i, (i + by) % length) for i in range(length)])]
    ppermute x4 -> x3, starting transfers between devices: 3.12 us -> 1.64 us  [exchanged(): return lax.ppermute(x, axis, pairs + [(b, a) for a, b in pairs])]
    ppermute x4 -> x3, starting transfers between devices: 4.76 us -> 3.47 us  [shifted(): lax.ppermute(x, axis, [(i, (i + by) % length) for i in range(length)])]
  transfers between devices with their start and end apart: 8 -> 8, of which waited for: 4 -> 3; matrix products, arithmetic and copies ran while one was open for 0% -> 0% of each run, Pallas kernels for 14% -> 14%
where the time goes in v6:
time: 30.2 us; the launch traced here: 30 us
  waiting for transfers between devices  13.2 us (44%)
  starting transfers between devices  7.59 us (25%)
  Pallas kernels  7.2 us (24%)
  between operations  1.99 us (7%)
    ppermute x3, waiting for transfers between devices, shifted(): lax.ppermute(x, axis, [(i, (i + by) % length) for i in range(length)])  12.3 us
    pallas_call x4, Pallas kernels, call(): pl.pallas_call(body, out_shape=[pltpu.VMEM(o.shape, o.dtype) for o in out...  5.97 us
    ppermute x3, starting transfers between devices, shifted(): lax.ppermute(x, axis, [(i, (i + by) % length) for i in range(length)])  3.47 us
    ppermute x3, starting transfers between devices, exchanged(): return lax.ppermute(x, axis, pairs + [(b, a) for a, b in pairs])  1.64 us
    ppermute x1, starting transfers between devices, body(): one = lax.ppermute(one, ('blk', 'grp'), first)  1.55 us
    pallas_call x1, Pallas kernels, finish(): pl.pallas_call(functools.partial(last_body, others, pairs), out_shape=[fu...  1.23 us
    ppermute x1, starting transfers between devices, body(): two = lax.ppermute(two, ('blk', 'grp'), second)  0.94 us
    ppermute x3, waiting for transfers between devices, exchanged(): return lax.ppermute(x, axis, pairs + [(b, a) for a, b in pairs])  0.93 us
  transfers between devices with their start and end apart: 8, of which 3 were waited for; matrix products, arithmetic and copies ran while one was open for 0% of the time, Pallas kernels for 14%

profile of v6, /device:TPU:1, one launch (start us, length us, event | category | flops | bytes accessed | tf_op | source)
XLA Modules:
  0.0 30.0 jit_solution(1317719535012828005)
XLA Ops:
  0.6 0.0 copy-start
  0.6 0.1 collective-permute-start
  0.7 2.7 %collective-permute-start.3 = (f32[128,768]{1,0:T(8,128)}, f32[128,768]{1,0:T(8,128)S(1)}, u32[]{:S(2)}, u32[]{:S(2)}) collective-permute-start(f32[128,768]{1,0:T(8,128)} %x_any.1), channel_id=1, source_target_pairs={{0,1},{1,0},{2,3},{3,2},{4,5},{5,4},{6,7},{7,6},{8,9},{9,8},{10,11... | collective-permute-start | bytes 1179656 | tf_op jit(solution)/shard_map/ppermute | solution.py:46
  3.4 1.5 %collective-permute-start.1 = (f32[128,768]{1,0:T(8,128)}, f32[128,768]{1,0:T(8,128)S(1)}, u32[]{:S(2)}, u32[]{:S(2)}) collective-permute-start(f32[128,768]{1,0:T(8,128)} %y_any.1), channel_id=1, source_target_pairs={{2,4},{6,8},{10,12},{14,16},{18,20},{22,24},{26,28},{30,0},{4,2},{... | collective-permute-start | bytes 1179656 | tf_op jit(solution)/shard_map/ppermute | solution.py:22
  4.9 0.0 copy-done
  4.9 0.3 collective-permute-start.2
  6.4 0.0 collective-permute-done.near_ref
  6.5 3.2 %shard_map.76 = (f32[2,128]{1,0:T(2,128)S(1)}, f32[128,768]{1,0:T(8,128)S(1)}, f32[128,1]{1,0:T(8,128)S(1)}, f32[128,768]{1,0:T(8,128)S(1)}, f32[128,1]{1,0:T(8,...) custom-call(f32[1]{0:T(128)S(6)} %copy.8.lt, ...), custom_call_target="tpu_custom_call" | custom-call | tf_op jit(solution)/shard_map/pallas_call | solution.py:265
  9.7 3.4 %collective-permute-done.2.refs_1_.refs_2_ = f32[1,128]{1,0:T(1,128)S(1)} collective-permute-done((f32[1,128]{1,0:T(1,128)S(1)}, f32[1,128]{1,0:T(1,128)S(1)}, u32[]{:S(2)}, u32[]{:S(2)}) %collective-permute-start.2) | collective-permute-done | bytes 544 | tf_op jit(solution)/shard_map/ppermute | solution.py:46
  13.0 0.0 collective-permute-done.3.refs_0_
  13.0 1.1 %shard_map.77 = (bf16[512,768]{1,0:T(8,128)(2,1)S(1)}, f32[128,768]{1,0:T(8,128)S(1)}, f32[1,128]{1,0:T(1,128)S(1)}, f32[128,256]{1,0:T(8,128)S(1)}) custom-call(f32[2,128]{1,0:T(2,128)S(1)} %get-tuple-element.33.tb_ref, f32[128,768]{1,0:T(8,128)S(1)} %collective-permute-done.3.refs_0_, f32[1,128]{1,0:T(1,128)S(1)} %collective-permute-done.2.refs_1_.refs_2_, ...), custom_call_target="tpu_custom_call" | custom-call | tf_op jit(solution)/shard_map/pallas_call | solution.py:265
  14.1 0.9 %collective-permute-done.1.refs_0_ = f32[128,768]{1,0:T(8,128)S(1)} collective-permute-done((f32[128,768]{1,0:T(8,128)}, f32[128,768]{1,0:T(8,128)S(1)}, u32[]{:S(2)}, u32[]{:S(2)}) %collective-permute-start.1) | collective-permute-done | bytes 393248 | tf_op jit(solution)/shard_map/ppermute | solution.py:22
  15.0 1.0 %shard_map.78 = (f32[128,768]{1,0:T(8,128)S(1)}, f32[128,768]{1,0:T(8,128)S(1)}, f32[1,128]{1,0:T(1,128)S(1)}, f32[1,128]{1,0:T(1,128)S(1)}, bf16[256,768]{1,0:T(8,128)(2,1)S(1)}, /*index=5*/f32[128,128]{1,0:T(8,128)S(1)}) custom-call(f32[2,128]{1,0:T(2,128)S(1)} %get-tuple-element.33.tb_ref, f32[128,768]{1,0:T(8,128)S(1)} %collective-permute-done.1.refs_0_, ...), custom_call_target="tpu_custom_call" | custom-call | tf_op jit(solution)/shard_map/pallas_call | solution.py:265
  16.1 0.7 %shard_map.79 = (f32[128,768]{1,0:T(8,128)S(1)}, f32[128,768]{1,0:T(8,128)S(1)}, f32[128,768]{1,0:T(8,128)S(1)}) custom-call(f32[128,768]{1,0:T(8,128)S(1)} %get-tuple-element.31.gx_in, f32[256,768]{1,0:T(8,128)S(1)} %get-tuple-element.32.gy_in, f32[128,128]{1,0:T(8,128)S(1)} %get-tuple-element.40.slope_ref, bf16[256,768]{1,0:T(8,128)(2,1)S(1)} %get-tuple-element.41.fs_ref, ...), custom_call_target="tpu_custom_call" | custom-call | tf_op jit(solution)/shard_map/pallas_call | solution.py:265
  16.8 0.1 collective-permute-start.4
  16.8 1.6 %collective-permute-start.5 = (f32[128,768]{1,0:T(8,128)S(1)}, f32[128,768]{1,0:T(8,128)S(1)}, u32[]{:S(2)}, u32[]{:S(2)}) collective-permute-start(f32[128,768]{1,0:T(8,128)S(1)} %get-tuple-element.48), channel_id=1, source_target_pairs={{0,1},{1,0},{2,4},{3,5},{4,2},{5,3},{6,7},{7,6},{8,9},{9,8},{10,12... | collective-permute-start | bytes 1179656 | tf_op jit(solution)/shard_map/ppermute | solution.py:368
  18.4 0.9 %collective-permute-start.6 = (f32[128,768]{1,0:T(8,128)S(1)}, f32[128,768]{1,0:T(8,128)S(1)}, u32[]{:S(2)}, u32[]{:S(2)}) collective-permute-start(f32[128,768]{1,0:T(8,128)S(1)} %get-tuple-element.49), channel_id=1, source_target_pairs={{0,30},{1,31},{2,3},{3,2},{4,5},{5,4},{6,8},{7,9},{8,6},{9,7},{10,... | collective-permute-start | bytes 1179656 | tf_op jit(solution)/shard_map/ppermute | solution.py:369
  19.3 0.5 %collective-permute-start.7 = (f32[1,128]{1,0:T(1,128)S(1)}, f32[1,128]{1,0:T(1,128)S(1)}, u32[]{:S(2)}, u32[]{:S(2)}) collective-permute-start(f32[1,128]{1,0:T(1,128)S(1)} %get-tuple-element.51), channel_id=1, source_target_pairs={{0,1},{1,0},{2,3},{3,2},{4,5},{5,4},{6,7},{7,6},{8,9},{9,8},{10,11... | collective-permute-start | bytes 1544 | tf_op jit(solution)/shard_map/ppermute | solution.py:46
  19.9 8.9 %collective-permute-done.7.refs_10_ = f32[1,128]{1,0:T(1,128)S(1)} collective-permute-done((f32[1,128]{1,0:T(1,128)S(1)}, f32[1,128]{1,0:T(1,128)S(1)}, u32[]{:S(2)}, u32[]{:S(2)}) %collective-permute-start.7) | collective-permute-done | bytes 544 | tf_op jit(solution)/shard_map/ppermute | solution.py:46
  28.7 0.0 collective-permute-done.4.refs_6_
  28.7 0.0 collective-permute-done.5.refs_7_
  28.7 0.0 collective-permute-done.6.refs_8_
  28.7 1.2 %shard_map.80 = (f32[128,768]{1,0:T(8,128)}, f32[128,768]{1,0:T(8,128)}, f32[1,128]{1,0:T(1,128)}) custom-call(f32[128,768]{1,0:T(8,128)S(1)} %get-tuple-element.29.refs_0_, f32[128,1]{1,0:T(8,128)S(1)} %get-tuple-element.30.refs_1_, f32[128,768]{1,0:T(8,128)S(1)} %get-tuple-element.43.refs_2_, f32[128,768]{1,0:T(8,128)S(1)} %get-tuple-element.44.refs_3_, ...), custom_call_target="tpu_custom_call" | custom-call | tf_op jit(solution)/shard_map/pallas_call | solution.py:278
Async XLA Ops:
  0.6 4.3 %copy-start = (f32[128]{0:T(128)S(1)}, f32[128]{0:T(128)}, u32[]{:S(2)}) copy-start(f32[128]{0:T(128)} %param.9) | copy-start | bytes 1540
  0.6 5.8 %collective-permute-start = (f32[128,768]{1,0:T(8,128)}, f32[128,768]{1,0:T(8,128)S(1)}, u32[]{:S(2)}, u32[]{:S(2)}) collective-permute-start(f32[128,768]{1,0:T(8,128)} %y_any.1), channel_id=1, source_target_pairs={{0,2},{4,6},{8,10},{12,14},{16,18},{20,22},{24,26},{28,30},{2,0},{... | collective-permute-start | bytes 1179656 | tf_op jit(solution)/shard_map/ppermute | solution.py:22
  0.7 12.3 %collective-permute-start.3 = (f32[128,768]{1,0:T(8,128)}, f32[128,768]{1,0:T(8,128)S(1)}, u32[]{:S(2)}, u32[]{:S(2)}) collective-permute-start(f32[128,768]{1,0:T(8,128)} %x_any.1), channel_id=1, source_target_pairs={{0,1},{1,0},{2,3},{3,2},{4,5},{5,4},{6,7},{7,6},{8,9},{9,8},{10,11... | collective-permute-start | bytes 1179656 | tf_op jit(solution)/shard_map/ppermute | solution.py:46
  3.4 11.6 %collective-permute-start.1 = (f32[128,768]{1,0:T(8,128)}, f32[128,768]{1,0:T(8,128)S(1)}, u32[]{:S(2)}, u32[]{:S(2)}) collective-permute-start(f32[128,768]{1,0:T(8,128)} %y_any.1), channel_id=1, source_target_pairs={{2,4},{6,8},{10,12},{14,16},{18,20},{22,24},{26,28},{30,0},{4,2},{... | collective-permute-start | bytes 1179656 | tf_op jit(solution)/shard_map/ppermute | solution.py:22
  4.9 8.1 %collective-permute-start.2 = (f32[1,128]{1,0:T(1,128)S(1)}, f32[1,128]{1,0:T(1,128)S(1)}, u32[]{:S(2)}, u32[]{:S(2)}) collective-permute-start(f32[1,128]{1,0:T(1,128)S(1)} %bitcast.2), channel_id=1, source_target_pairs={{0,1},{1,0},{2,3},{3,2},{4,5},{5,4},{6,7},{7,6},{8,9},{9,8},{10,11... | collective-permute-start | bytes 1544 | tf_op jit(solution)/shard_map/ppermute | solution.py:46
  16.8 12.0 %collective-permute-start.4 = (f32[128,768]{1,0:T(8,128)S(1)}, f32[128,768]{1,0:T(8,128)S(1)}, u32[]{:S(2)}, u32[]{:S(2)}) collective-permute-start(f32[128,768]{1,0:T(8,128)S(1)} %get-tuple-element.47), channel_id=1, source_target_pairs={{0,2},{4,6},{8,10},{12,14},{16,18},{20,22},{24,26},{28,30},{2,0},{... | collective-permute-start | bytes 1179656 | tf_op jit(solution)/shard_map/ppermute | solution.py:22
  16.8 11.9 %collective-permute-start.5 = (f32[128,768]{1,0:T(8,128)S(1)}, f32[128,768]{1,0:T(8,128)S(1)}, u32[]{:S(2)}, u32[]{:S(2)}) collective-permute-start(f32[128,768]{1,0:T(8,128)S(1)} %get-tuple-element.48), channel_id=1, source_target_pairs={{0,1},{1,0},{2,4},{3,5},{4,2},{5,3},{6,7},{7,6},{8,9},{9,8},{10,12... | collective-permute-start | bytes 1179656 | tf_op jit(solution)/shard_map/ppermute | solution.py:368
  18.4 10.4 %collective-permute-start.6 = (f32[128,768]{1,0:T(8,128)S(1)}, f32[128,768]{1,0:T(8,128)S(1)}, u32[]{:S(2)}, u32[]{:S(2)}) collective-permute-start(f32[128,768]{1,0:T(8,128)S(1)} %get-tuple-element.49), channel_id=1, source_target_pairs={{0,30},{1,31},{2,3},{3,2},{4,5},{5,4},{6,8},{7,9},{8,6},{9,7},{10,... | collective-permute-start | bytes 1179656 | tf_op jit(solution)/shard_map/ppermute | solution.py:369
  19.3 9.4 %collective-permute-start.7 = (f32[1,128]{1,0:T(1,128)S(1)}, f32[1,128]{1,0:T(1,128)S(1)}, u32[]{:S(2)}, u32[]{:S(2)}) collective-permute-start(f32[1,128]{1,0:T(1,128)S(1)} %get-tuple-element.51), channel_id=1, source_target_pairs={{0,1},{1,0},{2,3},{3,2},{4,5},{5,4},{6,7},{7,6},{8,9},{9,8},{10,11... | collective-permute-start | bytes 1544 | tf_op jit(solution)/shard_map/ppermute | solution.py:46

commit v7 on v6

--- a/solution.py
+++ b/solution.py
@@ -122,7 +122,7 @@
 def second_body(others, tb_ref, *refs):
     raw_refs, refs = refs[:others], refs[others:]
     w_refs, refs = refs[:others], refs[others:]
-    xs_ref, ys_ref, all_ref, refs = *refs[:3], refs[3:]
+    xs_ref, ys_ref, gy_in, all_ref, gnear_ref, refs = *refs[:5], refs[5:]
     gp_refs, refs = refs[:others], refs[others:]
     sump_refs, slope_refs = refs[:others], refs[others:]
     temper, bias = scalars_of(tb_ref)
@@ -131,6 +131,7 @@
     eye = square(count)
     all_ref[:count] = xs_ref[:count]
     all_ref[deep : deep + count] = xs_ref[count:]
+    near = gy_in[count:]
     for s in range(others):
         raw = raw_refs[s][...]
         px = stacked(raw * scale_of(raw))
@@ -142,8 +143,10 @@
         loss, slope = gated(z, weight * temper)
         sums = jnp.sum(loss, axis=1, keepdims=True)
         sump_refs[s][...] = jnp.sum(jnp.where(eye, sums, 0.0), axis=0, keepdims=True)
-        slope_refs[s][...] = slope
+        slope_refs[s][...] = slope[:, :count]
+        near = near + mm(stacked(slope[:, count:].T), px, NN)
         gp_refs[s][...] = mm(stacked(slope), ys_ref, NN)
+    gnear_ref[...] = near
 
 
 def third_body(others, tb_ref, *refs):
@@ -188,18 +191,17 @@
 
 
 def fourth_body(others, gx_in, gy_in, slope_ref, fs_ref, all_ref, *refs):
-    slopes, (gx_ref, gown_ref, gnear_ref) = refs[:others], refs[others:]
+    slopes, (gx_ref, gown_ref) = refs[:others], refs[others:]
     count = gx_in.shape[0]
     deep = (others + 1) * count
-    gy = gy_in[...]
+    gy = gy_in[:count]
     for s in range(others):
         here = (s + 1) * count
         px = jnp.concatenate(
             [all_ref[here : here + count], all_ref[deep + here : deep + here + count]], axis=0
         )
         gy = gy + mm(stacked(slopes[s][...].T), px, NN)
-    gown_ref[...] = gy[:count]
-    gnear_ref[...] = gy[count:]
+    gown_ref[...] = gy
     gx_ref[...] = gx_in[...] + mm(stacked(slope_ref[...].T), fs_ref, NN)
 
 
@@ -330,19 +332,21 @@
     )
     outs = call(
         functools.partial(second_body, others),
-        [shape(2 * members * count, width, kind=BF)]
+        [shape(2 * members * count, width, kind=BF), full]
         + [full] * others
         + [line] * others
-        + [shape(count, 2 * count)] * others,
+        + [shape(count, count)] * others,
         tb,
         *raws,
         *weights[1:],
         xs,
         ys,
-    )
-    everyone, outs = outs[0], outs[1:]
+        gy,
+    )
+    everyone, g_near, outs = outs[0], outs[1], outs[2:]
     gp, outs = outs[:others], outs[others:]
     sump, slopes = outs[:others], outs[others:]
+    back_near = exchanged(g_near, "blk", near_pairs)
     outs = call(
         functools.partial(third_body, others),
         [full, full]
@@ -369,9 +373,9 @@
     two = lax.ppermute(two, ("blk", "grp"), second)
     back_x = [shifted(gp[s - 2], "grp", s) for s in range(2, members)]
     back_sum = [shifted(sums[s], "grp", s) for s in range(1, members)]
-    gx, g_own, g_near = call(
+    gx, g_own = call(
         functools.partial(fourth_body, others),
-        [full] * 3,
+        [full] * 2,
         gx,
         gy,
         slope,
@@ -379,7 +383,6 @@
         everyone,
         *slopes,
     )
-    back_near = exchanged(g_near, "blk", near_pairs)
     grad_x, grad_y, row_loss = finish(
         others,
         3.0 * members * count,

time: 30.2 us -> 29.4 us (0.974)
  waiting for transfers between devices: 13.2 us -> 9.51 us
  starting transfers between devices: 7.59 us -> 10.1 us
    ppermute x3, waiting for transfers between devices: 12.3 us -> 8.88 us  [shifted(): lax.ppermute(x, axis, [(i, (i + by) % length) for i in range(length)])]
    ppermute x3, starting transfers between devices: 1.64 us -> 4.12 us  [exchanged(): return lax.ppermute(x, axis, pairs + [(b, a) for a, b in pairs])]
    ppermute x3, waiting for transfers between devices: 0.93 us -> 0.62 us  [exchanged(): return lax.ppermute(x, axis, pairs + [(b, a) for a, b in pairs])]
  transfers between devices with their start and end apart: 8 -> 8, of which waited for: 3 -> 3; matrix products, arithmetic and copies ran while one was open for 0% -> 0% of each run, Pallas kernels for 14% -> 18%
where the time goes in v7:
time: 29.4 us; the launch traced here: 29 us
  starting transfers between devices  10.1 us (34%)
  waiting for transfers between devices  9.51 us (32%)
  Pallas kernels  7.35 us (25%)
  between operations  1.98 us (7%)
    ppermute x3, waiting for transfers between devices, shifted(): lax.ppermute(x, axis, [(i, (i + by) % length) for i in range(length)])  8.88 us
    pallas_call x4, Pallas kernels, call(): pl.pallas_call(body, out_shape=[pltpu.VMEM(o.shape, o.dtype) for o in out...  6.12 us
    ppermute x3, starting transfers between devices, exchanged(): return lax.ppermute(x, axis, pairs + [(b, a) for a, b in pairs])  4.12 us
    ppermute x3, starting transfers between devices, shifted(): lax.ppermute(x, axis, [(i, (i + by) % length) for i in range(length)])  3.19 us
    ppermute x1, starting transfers between devices, body(): one = lax.ppermute(one, ('blk', 'grp'), first)  1.57 us
    pallas_call x1, Pallas kernels, finish(): pl.pallas_call(functools.partial(last_body, others, pairs), out_shape=[fu...  1.23 us
    ppermute x1, starting transfers between devices, body(): two = lax.ppermute(two, ('blk', 'grp'), second)  1.22 us
    ppermute x3, waiting for transfers between devices, exchanged(): return lax.ppermute(x, axis, pairs + [(b, a) for a, b in pairs])  0.62 us
  transfers between devices with their start and end apart: 8, of which 3 were waited for; matrix products, arithmetic and copies ran while one was open for 0% of the time, Pallas kernels for 18%

profile of v7, /device:TPU:1, one launch (start us, length us, event | category | flops | bytes accessed | tf_op | source)
XLA Modules:
  0.0 29.0 jit_solution(6735327835881031711)
XLA Ops:
  0.6 0.0 copy-start
  0.6 0.1 collective-permute-start
  0.7 2.7 %collective-permute-start.3 = (f32[128,768]{1,0:T(8,128)}, f32[128,768]{1,0:T(8,128)S(1)}, u32[]{:S(2)}, u32[]{:S(2)}) collective-permute-start(f32[128,768]{1,0:T(8,128)} %x_any.1), channel_id=1, source_target_pairs={{0,1},{1,0},{2,3},{3,2},{4,5},{5,4},{6,7},{7,6},{8,9},{9,8},{10,11... | collective-permute-start | bytes 1179656 | tf_op jit(solution)/shard_map/ppermute | solution.py:46
  3.4 1.5 %collective-permute-start.1 = (f32[128,768]{1,0:T(8,128)}, f32[128,768]{1,0:T(8,128)S(1)}, u32[]{:S(2)}, u32[]{:S(2)}) collective-permute-start(f32[128,768]{1,0:T(8,128)} %y_any.1), channel_id=1, source_target_pairs={{2,4},{6,8},{10,12},{14,16},{18,20},{22,24},{26,28},{30,0},{4,2},{... | collective-permute-start | bytes 1179656 | tf_op jit(solution)/shard_map/ppermute | solution.py:22
  4.9 0.0 copy-done
  4.9 0.3 collective-permute-start.2
  6.4 0.0 collective-permute-done.near_ref
  6.5 3.2 %shard_map.76 = (f32[2,128]{1,0:T(2,128)S(1)}, f32[128,768]{1,0:T(8,128)S(1)}, f32[128,1]{1,0:T(8,128)S(1)}, f32[128,768]{1,0:T(8,128)S(1)}, f32[128,1]{1,0:T(8,...) custom-call(f32[1]{0:T(128)S(6)} %copy.8.lt, ...), custom_call_target="tpu_custom_call" | custom-call | tf_op jit(solution)/shard_map/pallas_call | solution.py:267
  9.7 3.4 %collective-permute-done.2.refs_1_.refs_2_ = f32[1,128]{1,0:T(1,128)S(1)} collective-permute-done((f32[1,128]{1,0:T(1,128)S(1)}, f32[1,128]{1,0:T(1,128)S(1)}, u32[]{:S(2)}, u32[]{:S(2)}) %collective-permute-start.2) | collective-permute-done | bytes 544 | tf_op jit(solution)/shard_map/ppermute | solution.py:46
  13.0 0.0 collective-permute-done.3.refs_0_
  13.0 1.4 %shard_map.77 = (bf16[512,768]{1,0:T(8,128)(2,1)S(1)}, f32[128,768]{1,0:T(8,128)S(1)}, f32[128,768]{1,0:T(8,128)S(1)}, f32[1,128]{1,0:T(1,128)S(1)}, f32[128,128]{1,0:T(8,128)S(1)}) custom-call(f32[2,128]{1,0:T(2,128)S(1)} %get-tuple-element.33.tb_ref, f32[128,768]{1,0:T(8,128)S(1)} %collective-permute-done.3.refs_0_, ...), custom_call_target="tpu_custom_call" | custom-call | tf_op jit(solution)/shard_map/pallas_call | solution.py:267
  14.4 0.6 %collective-permute-done.1.refs_0_ = f32[128,768]{1,0:T(8,128)S(1)} collective-permute-done((f32[128,768]{1,0:T(8,128)}, f32[128,768]{1,0:T(8,128)S(1)}, u32[]{:S(2)}, u32[]{:S(2)}) %collective-permute-start.1) | collective-permute-done | bytes 393248 | tf_op jit(solution)/shard_map/ppermute | solution.py:22
  15.0 1.0 %shard_map.78 = (f32[128,768]{1,0:T(8,128)S(1)}, f32[128,768]{1,0:T(8,128)S(1)}, f32[1,128]{1,0:T(1,128)S(1)}, f32[1,128]{1,0:T(1,128)S(1)}, bf16[256,768]{1,0:T(8,128)(2,1)S(1)}, /*index=5*/f32[128,128]{1,0:T(8,128)S(1)}) custom-call(f32[2,128]{1,0:T(2,128)S(1)} %get-tuple-element.33.tb_ref, f32[128,768]{1,0:T(8,128)S(1)} %collective-permute-done.1.refs_0_, ...), custom_call_target="tpu_custom_call" | custom-call | tf_op jit(solution)/shard_map/pallas_call | solution.py:267
  16.1 1.6 %collective-permute-start.5 = (f32[128,768]{1,0:T(8,128)S(1)}, f32[128,768]{1,0:T(8,128)S(1)}, u32[]{:S(2)}, u32[]{:S(2)}) collective-permute-start(f32[128,768]{1,0:T(8,128)S(1)} %get-tuple-element.48), channel_id=1, source_target_pairs={{0,1},{1,0},{2,4},{3,5},{4,2},{5,3},{6,7},{7,6},{8,9},{9,8},{10,12... | collective-permute-start | bytes 1179656 | tf_op jit(solution)/shard_map/ppermute | solution.py:372
  17.7 1.2 %collective-permute-start.6 = (f32[128,768]{1,0:T(8,128)S(1)}, f32[128,768]{1,0:T(8,128)S(1)}, u32[]{:S(2)}, u32[]{:S(2)}) collective-permute-start(f32[128,768]{1,0:T(8,128)S(1)} %get-tuple-element.49), channel_id=1, source_target_pairs={{0,30},{1,31},{2,3},{3,2},{4,5},{5,4},{6,8},{7,9},{8,6},{9,7},{10,... | collective-permute-start | bytes 1179656 | tf_op jit(solution)/shard_map/ppermute | solution.py:373
  18.9 2.6 %collective-permute-start.4 = (f32[128,768]{1,0:T(8,128)S(1)}, f32[128,768]{1,0:T(8,128)S(1)}, u32[]{:S(2)}, u32[]{:S(2)}) collective-permute-start(f32[128,768]{1,0:T(8,128)S(1)} %get-tuple-element.47), channel_id=1, source_target_pairs={{0,2},{4,6},{8,10},{12,14},{16,18},{20,22},{24,26},{28,30},{2,0},{... | collective-permute-start | bytes 1179656 | tf_op jit(solution)/shard_map/ppermute | solution.py:22
  21.4 0.3 collective-permute-start.7
  21.7 0.5 %shard_map.79 = (f32[128,768]{1,0:T(8,128)S(1)}, f32[128,768]{1,0:T(8,128)S(1)}) custom-call(f32[128,768]{1,0:T(8,128)S(1)} %get-tuple-element.31.gx_in, f32[256,768]{1,0:T(8,128)S(1)} %get-tuple-element.32.refs_4_.gy_in, f32[128,128]{1,0:T(8,128)S(1)} %get-tuple-element.40.slope_ref, bf16[256,768]{1,0:T(8,128)(2,1)S(1)} %get-tuple-element.41.fs_ref, ...), custom_call_target="tpu_custom_call" | custom-call | tf_op jit(solution)/shard_map/pallas_call | solution.py:267
  22.2 5.5 %collective-permute-done.7.refs_10_ = f32[1,128]{1,0:T(1,128)S(1)} collective-permute-done((f32[1,128]{1,0:T(1,128)S(1)}, f32[1,128]{1,0:T(1,128)S(1)}, u32[]{:S(2)}, u32[]{:S(2)}) %collective-permute-start.7) | collective-permute-done | bytes 544 | tf_op jit(solution)/shard_map/ppermute | solution.py:46
  27.7 0.0 collective-permute-done.5.refs_7_
  27.7 0.0 collective-permute-done.6.refs_8_
  27.7 0.0 collective-permute-done.4.refs_6_
  27.7 1.2 %shard_map.80 = (f32[128,768]{1,0:T(8,128)}, f32[128,768]{1,0:T(8,128)}, f32[1,128]{1,0:T(1,128)}) custom-call(f32[128,768]{1,0:T(8,128)S(1)} %get-tuple-element.29.refs_0_, f32[128,1]{1,0:T(8,128)S(1)} %get-tuple-element.30.refs_1_, f32[128,768]{1,0:T(8,128)S(1)} %get-tuple-element.43.refs_2_, f32[128,768]{1,0:T(8,128)S(1)} %get-tuple-element.44.refs_3_, ...), custom_call_target="tpu_custom_call" | custom-call | tf_op jit(solution)/shard_map/pallas_call | solution.py:280
Async XLA Ops:
  0.6 4.3 %copy-start = (f32[128]{0:T(128)S(1)}, f32[128]{0:T(128)}, u32[]{:S(2)}) copy-start(f32[128]{0:T(128)} %param.9) | copy-start | bytes 1540
  0.6 5.8 %collective-permute-start = (f32[128,768]{1,0:T(8,128)}, f32[128,768]{1,0:T(8,128)S(1)}, u32[]{:S(2)}, u32[]{:S(2)}) collective-permute-start(f32[128,768]{1,0:T(8,128)} %y_any.1), channel_id=1, source_target_pairs={{0,2},{4,6},{8,10},{12,14},{16,18},{20,22},{24,26},{28,30},{2,0},{... | collective-permute-start | bytes 1179656 | tf_op jit(solution)/shard_map/ppermute | solution.py:22
  0.7 12.3 %collective-permute-start.3 = (f32[128,768]{1,0:T(8,128)}, f32[128,768]{1,0:T(8,128)S(1)}, u32[]{:S(2)}, u32[]{:S(2)}) collective-permute-start(f32[128,768]{1,0:T(8,128)} %x_any.1), channel_id=1, source_target_pairs={{0,1},{1,0},{2,3},{3,2},{4,5},{5,4},{6,7},{7,6},{8,9},{9,8},{10,11... | collective-permute-start | bytes 1179656 | tf_op jit(solution)/shard_map/ppermute | solution.py:46
  3.4 11.6 %collective-permute-start.1 = (f32[128,768]{1,0:T(8,128)}, f32[128,768]{1,0:T(8,128)S(1)}, u32[]{:S(2)}, u32[]{:S(2)}) collective-permute-start(f32[128,768]{1,0:T(8,128)} %y_any.1), channel_id=1, source_target_pairs={{2,4},{6,8},{10,12},{14,16},{18,20},{22,24},{26,28},{30,0},{4,2},{... | collective-permute-start | bytes 1179656 | tf_op jit(solution)/shard_map/ppermute | solution.py:22
  4.9 8.1 %collective-permute-start.2 = (f32[1,128]{1,0:T(1,128)S(1)}, f32[1,128]{1,0:T(1,128)S(1)}, u32[]{:S(2)}, u32[]{:S(2)}) collective-permute-start(f32[1,128]{1,0:T(1,128)S(1)} %bitcast.2), channel_id=1, source_target_pairs={{0,1},{1,0},{2,3},{3,2},{4,5},{5,4},{6,7},{7,6},{8,9},{9,8},{10,11... | collective-permute-start | bytes 1544 | tf_op jit(solution)/shard_map/ppermute | solution.py:46
  16.1 11.6 %collective-permute-start.5 = (f32[128,768]{1,0:T(8,128)S(1)}, f32[128,768]{1,0:T(8,128)S(1)}, u32[]{:S(2)}, u32[]{:S(2)}) collective-permute-start(f32[128,768]{1,0:T(8,128)S(1)} %get-tuple-element.48), channel_id=1, source_target_pairs={{0,1},{1,0},{2,4},{3,5},{4,2},{5,3},{6,7},{7,6},{8,9},{9,8},{10,12... | collective-permute-start | bytes 1179656 | tf_op jit(solution)/shard_map/ppermute | solution.py:372
  17.7 10.1 %collective-permute-start.6 = (f32[128,768]{1,0:T(8,128)S(1)}, f32[128,768]{1,0:T(8,128)S(1)}, u32[]{:S(2)}, u32[]{:S(2)}) collective-permute-start(f32[128,768]{1,0:T(8,128)S(1)} %get-tuple-element.49), channel_id=1, source_target_pairs={{0,30},{1,31},{2,3},{3,2},{4,5},{5,4},{6,8},{7,9},{8,6},{9,7},{10,... | collective-permute-start | bytes 1179656 | tf_op jit(solution)/shard_map/ppermute | solution.py:373
  18.9 8.8 %collective-permute-start.4 = (f32[128,768]{1,0:T(8,128)S(1)}, f32[128,768]{1,0:T(8,128)S(1)}, u32[]{:S(2)}, u32[]{:S(2)}) collective-permute-start(f32[128,768]{1,0:T(8,128)S(1)} %get-tuple-element.47), channel_id=1, source_target_pairs={{0,2},{4,6},{8,10},{12,14},{16,18},{20,22},{24,26},{28,30},{2,0},{... | collective-permute-start | bytes 1179656 | tf_op jit(solution)/shard_map/ppermute | solution.py:22
  21.4 6.3 %collective-permute-start.7 = (f32[1,128]{1,0:T(1,128)S(1)}, f32[1,128]{1,0:T(1,128)S(1)}, u32[]{:S(2)}, u32[]{:S(2)}) collective-permute-start(f32[1,128]{1,0:T(1,128)S(1)} %get-tuple-element.51), channel_id=1, source_target_pairs={{0,1},{1,0},{2,3},{3,2},{4,5},{5,4},{6,7},{7,6},{8,9},{9,8},{10,11... | collective-permute-start | bytes 1544 | tf_op jit(solution)/shard_map/ppermute | solution.py:46

commit v8 on v6

--- a/solution.py
+++ b/solution.py
@@ -150,13 +150,11 @@
     members = others + 1
     far_ref, refs = refs[0], refs[1:]
     w_refs, refs = refs[:members], refs[members:]
-    all_ref, refs = refs[0], refs[1:]
-    gp_in, refs = refs[:others], refs[others:]
+    all_ref, gp_in, refs = *refs[:2], refs[2:]
     sum_in, refs = refs[:members], refs[members:]
-    one_ref, two_ref, refs = *refs[:2], refs[2:]
-    gp_refs, refs = refs[: others - 1], refs[others - 1 :]
+    one_ref, refs = refs[0], refs[1:]
     sum_refs, refs = refs[:members], refs[members:]
-    fs_ref, slope_ref, both_ref, turned_ref = refs
+    fs_ref, both_ref, slope_ref = refs
     temper, bias = scalars_of(tb_ref)
     count = far_ref.shape[0]
     far = far_ref[...]
@@ -171,20 +169,34 @@
     for s in range(members):
         part = slice(s * count, (s + 1) * count)
         sum_refs[s][...] = sum_in[s][...] + sums[:, part]
-        if s == 0:
-            slope_ref[...] = slope[:, part]
-        else:
-            turned_ref[s - 1] = stacked(slope[:, part].T)
-            if s > 1:
-                gp_refs[s - 2][...] = gp_in[s - 1][...] + mm(turned_ref[s - 1], fs_ref, NN)
-
-    def finish_into(far_out, next_out):
-        far_out[...] = mm(both_ref, all_ref, NN)
-        next_out[...] = gp_in[0][...] + mm(turned_ref[0], fs_ref, NN)
-
-    far_first = far_goes_first()
-    pl.when(far_first)(lambda: finish_into(one_ref, two_ref))
-    pl.when(jnp.logical_not(far_first))(lambda: finish_into(two_ref, one_ref))
+        slope_ref[s] = slope[:, part]
+
+    @pl.when(far_goes_first())
+    def _():
+        one_ref[...] = mm(both_ref, all_ref, NN)
+
+    @pl.when(jnp.logical_not(far_goes_first()))
+    def _():
+        one_ref[...] = gp_in[...] + mm(stacked(slope_ref[1].T), fs_ref, NN)
+
+
+def rest_body(others, *refs):
+    gp_in, (fs_ref, both_ref, slope_ref, all_ref, two_ref), gp_refs = (
+        refs[:others],
+        refs[others : others + 5],
+        refs[others + 5 :],
+    )
+
+    @pl.when(far_goes_first())
+    def _():
+        two_ref[...] = gp_in[0][...] + mm(stacked(slope_ref[1].T), fs_ref, NN)
+
+    @pl.when(jnp.logical_not(far_goes_first()))
+    def _():
+        two_ref[...] = mm(both_ref, all_ref, NN)
+
+    for s in range(2, others + 1):
+        gp_refs[s - 2][...] = gp_in[s - 1][...] + mm(stacked(slope_ref[s].T), fs_ref, NN)
 
 
 def fourth_body(others, gx_in, gy_in, slope_ref, fs_ref, all_ref, *refs):
@@ -200,7 +212,7 @@
         gy = gy + mm(stacked(slopes[s][...].T), px, NN)
     gown_ref[...] = gy[:count]
     gnear_ref[...] = gy[count:]
-    gx_ref[...] = gx_in[...] + mm(stacked(slope_ref[...].T), fs_ref, NN)
+    gx_ref[...] = gx_in[...] + mm(stacked(slope_ref[0].T), fs_ref, NN)
 
 
 def last_body(others, pairs, *refs):
@@ -345,27 +357,34 @@
     sump, slopes = outs[:others], outs[others:]
     outs = call(
         functools.partial(third_body, others),
-        [full, full]
-        + [full] * (others - 1)
+        [full]
         + [line] * members
-        + [stack, shape(count, count)],
+        + [
+            stack,
+            shape(2 * count, members * count, kind=BF),
+            shape(members, count, count),
+        ],
         tb,
         far,
         *weights,
         everyone,
-        *gp,
+        gp[0],
         sums,
         *sump,
-        scratch=[
-            pltpu.VMEM((2 * count, members * count), BF),
-            pltpu.VMEM((others, 2 * count, count), BF),
-        ],
-    )
-    one, two, outs = outs[0], outs[1], outs[2:]
-    gp, outs = outs[: others - 1], outs[others - 1 :]
-    sums, (fs, slope) = outs[:members], outs[members:]
+    )
+    one, outs = outs[0], outs[1:]
+    sums, (fs, both, slope) = outs[:members], outs[members:]
     first, second = mixed_pairs(length, members)
     one = lax.ppermute(one, ("blk", "grp"), first)
+    two, *gp = call(
+        functools.partial(rest_body, others),
+        [full] * others,
+        *gp,
+        fs,
+        both,
+        slope,
+        everyone,
+    )
     two = lax.ppermute(two, ("blk", "grp"), second)
     back_x = [shifted(gp[s - 2], "grp", s) for s in range(2, members)]
     back_sum = [shifted(sums[s], "grp", s) for s in range(1, members)]

time: 30.2 us -> 31 us (1.026)
  starting transfers between devices: 7.59 us -> 9.6 us
  waiting for transfers between devices: 13.2 us -> 11.9 us
    ppermute x3, waiting for transfers between devices: 12.3 us -> 4.89 us  [shifted(): lax.ppermute(x, axis, [(i, (i + by) % length) for i in range(length)])]
    ppermute x1, waiting for transfers between devices: 0.01 us -> 6.05 us  [body(): one = lax.ppermute(one, ('blk', 'grp'), first)]
    ppermute x3, starting transfers between devices: 1.64 us -> 5.11 us  [exchanged(): return lax.ppermute(x, axis, pairs + [(b, a) for a, b in pairs])]
    ppermute x1, starting transfers between devices: 1.55 us -> 0.01 us  [body(): one = lax.ppermute(one, ('blk', 'grp'), first)]
    ppermute x3, starting transfers between devices: 3.47 us -> 4.14 us  [shifted(): lax.ppermute(x, axis, [(i, (i + by) % length) for i in range(length)])]
    ppermute x1, starting transfers between devices: 0.94 us -> 0.34 us  [body(): two = lax.ppermute(two, ('blk', 'grp'), second)]
    pallas_call x4 -> x5, Pallas kernels: 5.97 us -> 6.16 us  [call(): pl.pallas_call(body, out_shape=[pltpu.VMEM(o.shape, o.dtype) for o in out...]
  transfers between devices with their start and end apart: 8 -> 8, of which waited for: 3 -> 4; matrix products, arithmetic and copies ran while one was open for 0% -> 0% of each run, Pallas kernels for 14% -> 16%
where the time goes in v8:
time: 31 us; the launch traced here: 30.8 us
  waiting for transfers between devices  11.9 us (38%)
  starting transfers between devices  9.6 us (31%)
  Pallas kernels  7.38 us (24%)
  between operations  1.99 us (6%)
    pallas_call x5, Pallas kernels, call(): pl.pallas_call(body, out_shape=[pltpu.VMEM(o.shape, o.dtype) for o in out...  6.16 us
    ppermute x1, waiting for transfers between devices, body(): one = lax.ppermute(one, ('blk', 'grp'), first)  6.05 us
    ppermute x3, starting transfers between devices, exchanged(): return lax.ppermute(x, axis, pairs + [(b, a) for a, b in pairs])  5.11 us
    ppermute x3, waiting for transfers between devices, shifted(): lax.ppermute(x, axis, [(i, (i + by) % length) for i in range(length)])  4.89 us
    ppermute x3, starting transfers between devices, shifted(): lax.ppermute(x, axis, [(i, (i + by) % length) for i in range(length)])  4.14 us
    pallas_call x1, Pallas kernels, finish(): pl.pallas_call(functools.partial(last_body, others, pairs), out_shape=[fu...  1.21 us
    ppermute x3, waiting for transfers between devices, exchanged(): return lax.ppermute(x, axis, pairs + [(b, a) for a, b in pairs])  0.93 us
  transfers between devices with their start and end apart: 8, of which 4 were waited for; matrix products, arithmetic and copies ran while one was open for 0% of the time, Pallas kernels for 16%

profile of v8, /device:TPU:1, one launch (start us, length us, event | category | flops | bytes accessed | tf_op | source)
XLA Modules:
  0.0 30.8 jit_solution(6891234936515447117)
XLA Ops:
  0.6 0.0 copy-start
  0.6 0.1 collective-permute-start
  0.7 2.7 %collective-permute-start.3 = (f32[128,768]{1,0:T(8,128)}, f32[128,768]{1,0:T(8,128)S(1)}, u32[]{:S(2)}, u32[]{:S(2)}) collective-permute-start(f32[128,768]{1,0:T(8,128)} %x_any.1), channel_id=1, source_target_pairs={{0,1},{1,0},{2,3},{3,2},{4,5},{5,4},{6,7},{7,6},{8,9},{9,8},{10,11... | collective-permute-start | bytes 1179656 | tf_op jit(solution)/shard_map/ppermute | solution.py:46
  3.4 1.5 %collective-permute-start.1 = (f32[128,768]{1,0:T(8,128)}, f32[128,768]{1,0:T(8,128)S(1)}, u32[]{:S(2)}, u32[]{:S(2)}) collective-permute-start(f32[128,768]{1,0:T(8,128)} %y_any.1), channel_id=1, source_target_pairs={{2,4},{6,8},{10,12},{14,16},{18,20},{22,24},{26,28},{30,0},{4,2},{... | collective-permute-start | bytes 1179656 | tf_op jit(solution)/shard_map/ppermute | solution.py:22
  4.9 0.0 copy-done
  4.9 0.3 collective-permute-start.2
  6.4 0.0 collective-permute-done.near_ref
  6.5 3.2 %shard_map.76 = (f32[2,128]{1,0:T(2,128)S(1)}, f32[128,768]{1,0:T(8,128)S(1)}, f32[128,1]{1,0:T(8,128)S(1)}, f32[128,768]{1,0:T(8,128)S(1)}, f32[128,1]{1,0:T(8,...) custom-call(f32[1]{0:T(128)S(6)} %copy.8.lt, ...), custom_call_target="tpu_custom_call" | custom-call | tf_op jit(solution)/shard_map/pallas_call | solution.py:277
  9.7 3.4 %collective-permute-done.2.refs_1_.refs_2_ = f32[1,128]{1,0:T(1,128)S(1)} collective-permute-done((f32[1,128]{1,0:T(1,128)S(1)}, f32[1,128]{1,0:T(1,128)S(1)}, u32[]{:S(2)}, u32[]{:S(2)}) %collective-permute-start.2) | collective-permute-done | bytes 544 | tf_op jit(solution)/shard_map/ppermute | solution.py:46
  13.0 0.0 collective-permute-done.3.refs_0_
  13.0 1.1 %shard_map.77 = (bf16[512,768]{1,0:T(8,128)(2,1)S(1)}, f32[128,768]{1,0:T(8,128)S(1)}, f32[1,128]{1,0:T(1,128)S(1)}, f32[128,256]{1,0:T(8,128)S(1)}) custom-call(f32[2,128]{1,0:T(2,128)S(1)} %get-tuple-element.33.tb_ref, f32[128,768]{1,0:T(8,128)S(1)} %collective-permute-done.3.refs_0_, f32[1,128]{1,0:T(1,128)S(1)} %collective-permute-done.2.refs_1_.refs_2_, ...), custom_call_target="tpu_custom_call" | custom-call | tf_op jit(solution)/shard_map/pallas_call | solution.py:277
  14.1 0.9 %collective-permute-done.1.refs_0_ = f32[128,768]{1,0:T(8,128)S(1)} collective-permute-done((f32[128,768]{1,0:T(8,128)}, f32[128,768]{1,0:T(8,128)S(1)}, u32[]{:S(2)}, u32[]{:S(2)}) %collective-permute-start.1) | collective-permute-done | bytes 393248 | tf_op jit(solution)/shard_map/ppermute | solution.py:22
  15.0 0.8 %shard_map.78 = (f32[128,768]{1,0:T(8,128)S(1)}, f32[1,128]{1,0:T(1,128)S(1)}, f32[1,128]{1,0:T(1,128)S(1)}, bf16[256,768]{1,0:T(8,128)(2,1)S(1)}, bf16[256,256]...) custom-call(f32[2,128]{1,0:T(2,128)S(1)} %get-tuple-element.33.tb_ref, f32[128,768]{1,0:T(8,128)S(1)} %collective-permute-done.1.refs_0_, ...), custom_call_target="tpu_custom_call" | custom-call | tf_op jit(solution)/shard_map/pallas_call | solution.py:277
  15.9 0.4 %shard_map.80 = f32[128,768]{1,0:T(8,128)S(1)} custom-call(f32[128,768]{1,0:T(8,128)S(1)} %get-tuple-element.37.refs_4_.refs_0_, bf16[256,768]{1,0:T(8,128)(2,1)S(1)} %get-tuple-element.41.fs_ref.refs_1_, bf16[256,256]{1,0:T(8,128)(2,1)S(1)} %get-tuple-element.49.refs_2_, f32[2,128,128]{2,1,0:T(8,128)S(1)} %get-tuple-element.40.slope_ref.refs_3_, ...), custom_call_target="tpu_custom_call" | custom-call | tf_op jit(solution)/shard_map/pallas_call | solution.py:277
  16.3 0.3 %collective-permute-start.6 = (f32[128,768]{1,0:T(8,128)S(1)}, f32[128,768]{1,0:T(8,128)S(1)}, u32[]{:S(2)}, u32[]{:S(2)}) collective-permute-start(f32[128,768]{1,0:T(8,128)S(1)} %shard_map.80), channel_id=1, source_target_pairs={{0,30},{1,31},{2,3},{3,2},{4,5},{5,4},{6,8},{7,9},{8,6},{9,7},{10,... | collective-permute-start | bytes 1179656 | tf_op jit(solution)/shard_map/ppermute | solution.py:388
  16.6 0.7 %shard_map.79 = (f32[128,768]{1,0:T(8,128)S(1)}, f32[128,768]{1,0:T(8,128)S(1)}, f32[128,768]{1,0:T(8,128)S(1)}) custom-call(f32[128,768]{1,0:T(8,128)S(1)} %get-tuple-element.31.gx_in, f32[256,768]{1,0:T(8,128)S(1)} %get-tuple-element.32.gy_in, f32[2,128,128]{2,1,0:T(8,128)S(1)} %get-tuple-element.40.slope_ref.refs_3_, ...), custom_call_target="tpu_custom_call" | custom-call | tf_op jit(solution)/shard_map/pallas_call | solution.py:277
  17.3 3.5 %collective-permute-start.4 = (f32[128,768]{1,0:T(8,128)S(1)}, f32[128,768]{1,0:T(8,128)S(1)}, u32[]{:S(2)}, u32[]{:S(2)}) collective-permute-start(f32[128,768]{1,0:T(8,128)S(1)} %get-tuple-element.47), channel_id=1, source_target_pairs={{0,2},{4,6},{8,10},{12,14},{16,18},{20,22},{24,26},{28,30},{2,0},{... | collective-permute-start | bytes 1179656 | tf_op jit(solution)/shard_map/ppermute | solution.py:22
  20.8 0.0 collective-permute-start.5
  20.8 1.2 %collective-permute-start.7 = (f32[1,128]{1,0:T(1,128)S(1)}, f32[1,128]{1,0:T(1,128)S(1)}, u32[]{:S(2)}, u32[]{:S(2)}) collective-permute-start(f32[1,128]{1,0:T(1,128)S(1)} %get-tuple-element.51), channel_id=1, source_target_pairs={{0,1},{1,0},{2,3},{3,2},{4,5},{5,4},{6,7},{7,6},{8,9},{9,8},{10,11... | collective-permute-start | bytes 1544 | tf_op jit(solution)/shard_map/ppermute | solution.py:46
  22.0 1.5 %collective-permute-done.7.refs_10_ = f32[1,128]{1,0:T(1,128)S(1)} collective-permute-done((f32[1,128]{1,0:T(1,128)S(1)}, f32[1,128]{1,0:T(1,128)S(1)}, u32[]{:S(2)}, u32[]{:S(2)}) %collective-permute-start.7) | collective-permute-done | bytes 544 | tf_op jit(solution)/shard_map/ppermute | solution.py:46
  23.6 0.0 collective-permute-done.6.refs_8_
  23.6 0.0 collective-permute-done.4.refs_6_
  23.6 6.0 %collective-permute-done.5.refs_7_ = f32[128,768]{1,0:T(8,128)S(1)} collective-permute-done((f32[128,768]{1,0:T(8,128)S(1)}, f32[128,768]{1,0:T(8,128)S(1)}, u32[]{:S(2)}, u32[]{:S(2)}) %collective-permute-start.5) | collective-permute-done | bytes 393248 | tf_op jit(solution)/shard_map/ppermute | solution.py:378
  29.6 1.2 %shard_map.81 = (f32[128,768]{1,0:T(8,128)}, f32[128,768]{1,0:T(8,128)}, f32[1,128]{1,0:T(1,128)}) custom-call(f32[128,768]{1,0:T(8,128)S(1)} %get-tuple-element.29.refs_0_, f32[128,1]{1,0:T(8,128)S(1)} %get-tuple-element.30.refs_1_, f32[128,768]{1,0:T(8,128)S(1)} %get-tuple-element.43.refs_2_, f32[128,768]{1,0:T(8,128)S(1)} %get-tuple-element.44.refs_3_, ...), custom_call_target="tpu_custom_call" | custom-call | tf_op jit(solution)/shard_map/pallas_call | solution.py:290
Async XLA Ops:
  0.6 4.3 %copy-start = (f32[128]{0:T(128)S(1)}, f32[128]{0:T(128)}, u32[]{:S(2)}) copy-start(f32[128]{0:T(128)} %param.9) | copy-start | bytes 1540
  0.6 5.8 %collective-permute-start = (f32[128,768]{1,0:T(8,128)}, f32[128,768]{1,0:T(8,128)S(1)}, u32[]{:S(2)}, u32[]{:S(2)}) collective-permute-start(f32[128,768]{1,0:T(8,128)} %y_any.1), channel_id=1, source_target_pairs={{0,2},{4,6},{8,10},{12,14},{16,18},{20,22},{24,26},{28,30},{2,0},{... | collective-permute-start | bytes 1179656 | tf_op jit(solution)/shard_map/ppermute | solution.py:22
  0.7 12.3 %collective-permute-start.3 = (f32[128,768]{1,0:T(8,128)}, f32[128,768]{1,0:T(8,128)S(1)}, u32[]{:S(2)}, u32[]{:S(2)}) collective-permute-start(f32[128,768]{1,0:T(8,128)} %x_any.1), channel_id=1, source_target_pairs={{0,1},{1,0},{2,3},{3,2},{4,5},{5,4},{6,7},{7,6},{8,9},{9,8},{10,11... | collective-permute-start | bytes 1179656 | tf_op jit(solution)/shard_map/ppermute | solution.py:46
  3.4 11.6 %collective-permute-start.1 = (f32[128,768]{1,0:T(8,128)}, f32[128,768]{1,0:T(8,128)S(1)}, u32[]{:S(2)}, u32[]{:S(2)}) collective-permute-start(f32[128,768]{1,0:T(8,128)} %y_any.1), channel_id=1, source_target_pairs={{2,4},{6,8},{10,12},{14,16},{18,20},{22,24},{26,28},{30,0},{4,2},{... | collective-permute-start | bytes 1179656 | tf_op jit(solution)/shard_map/ppermute | solution.py:22
  4.9 8.1 %collective-permute-start.2 = (f32[1,128]{1,0:T(1,128)S(1)}, f32[1,128]{1,0:T(1,128)S(1)}, u32[]{:S(2)}, u32[]{:S(2)}) collective-permute-start(f32[1,128]{1,0:T(1,128)S(1)} %bitcast.2), channel_id=1, source_target_pairs={{0,1},{1,0},{2,3},{3,2},{4,5},{5,4},{6,7},{7,6},{8,9},{9,8},{10,11... | collective-permute-start | bytes 1544 | tf_op jit(solution)/shard_map/ppermute | solution.py:46
  16.3 7.3 %collective-permute-start.6 = (f32[128,768]{1,0:T(8,128)S(1)}, f32[128,768]{1,0:T(8,128)S(1)}, u32[]{:S(2)}, u32[]{:S(2)}) collective-permute-start(f32[128,768]{1,0:T(8,128)S(1)} %shard_map.80), channel_id=1, source_target_pairs={{0,30},{1,31},{2,3},{3,2},{4,5},{5,4},{6,8},{7,9},{8,6},{9,7},{10,... | collective-permute-start | bytes 1179656 | tf_op jit(solution)/shard_map/ppermute | solution.py:388
  17.3 6.3 %collective-permute-start.4 = (f32[128,768]{1,0:T(8,128)S(1)}, f32[128,768]{1,0:T(8,128)S(1)}, u32[]{:S(2)}, u32[]{:S(2)}) collective-permute-start(f32[128,768]{1,0:T(8,128)S(1)} %get-tuple-element.47), channel_id=1, source_target_pairs={{0,2},{4,6},{8,10},{12,14},{16,18},{20,22},{24,26},{28,30},{2,0},{... | collective-permute-start | bytes 1179656 | tf_op jit(solution)/shard_map/ppermute | solution.py:22
  20.8 8.8 %collective-permute-start.5 = (f32[128,768]{1,0:T(8,128)S(1)}, f32[128,768]{1,0:T(8,128)S(1)}, u32[]{:S(2)}, u32[]{:S(2)}) collective-permute-start(f32[128,768]{1,0:T(8,128)S(1)} %get-tuple-element.48), channel_id=1, source_target_pairs={{0,1},{1,0},{2,4},{3,5},{4,2},{5,3},{6,7},{7,6},{8,9},{9,8},{10,12... | collective-permute-start | bytes 1179656 | tf_op jit(solution)/shard_map/ppermute | solution.py:378
  20.8 2.7 %collective-permute-start.7 = (f32[1,128]{1,0:T(1,128)S(1)}, f32[1,128]{1,0:T(1,128)S(1)}, u32[]{:S(2)}, u32[]{:S(2)}) collective-permute-start(f32[1,128]{1,0:T(1,128)S(1)} %get-tuple-element.51), channel_id=1, source_target_pairs={{0,1},{1,0},{2,3},{3,2},{4,5},{5,4},{6,7},{7,6},{8,9},{9,8},{10,11... | collective-permute-start | bytes 1544 | tf_op jit(solution)/shard_map/ppermute | solution.py:46

commit v9 on v8

--- a/solution.py
+++ b/solution.py
@@ -30,7 +30,8 @@
             here = b * members + g
             across = (here, far * members + g)
             along = (here, b * members + (g + 1) % members)
-            direct = length % 4 == 0 and b % 4 in (1, 2)
+            end = b in (0, length - 1)
+            direct = length % 4 == 0 and (end or (b % 4 in (1, 2) and 2 < b < length - 3))
             first.append(across if direct else along)
             second.append(along if direct else across)
     return first, second
@@ -38,7 +39,10 @@
 
 def far_goes_first():
     place = lax.axis_index("blk")
-    return (lax.axis_size("blk") % 4 == 0) & (lax.rem(place + 1, 4) >= 2)
+    length = lax.axis_size("blk")
+    end = (place == 0) | (place == length - 1)
+    inner = (place > 2) & (place < length - 3) & (lax.rem(place + 1, 4) >= 2)
+    return (length % 4 == 0) & (end | inner)
 
 
 def shifted(x, axis, by):

time: 31 us -> 30.3 us (0.977)
  the two profiles are of different devices: /device:TPU:1 before, /device:TPU:0 now
where the time goes in v9:
time: 30.3 us; the launch traced here: 30.2 us
  starting transfers between devices  14.5 us (48%)
  Pallas kernels  7.38 us (24%)
  waiting for transfers between devices  6.27 us (21%)
  between operations  1.99 us (7%)
    pallas_call x5, Pallas kernels, call(): pl.pallas_call(body, out_shape=[pltpu.VMEM(o.shape, o.dtype) for o in out...  6.17 us
    ppermute x3, starting transfers between devices, exchanged(): return lax.ppermute(x, axis, pairs + [(b, a) for a, b in pairs])  5.36 us
    ppermute x3, starting transfers between devices, shifted(): lax.ppermute(x, axis, [(i, (i + by) % length) for i in range(length)])  4.06 us
    ppermute x3, waiting for transfers between devices, shifted(): lax.ppermute(x, axis, [(i, (i + by) % length) for i in range(length)])  3.52 us
    ppermute x1, starting transfers between devices, body(): one = lax.ppermute(one, ('blk', 'grp'), first)  3.3 us
    ppermute x1, waiting for transfers between devices, body(): one = lax.ppermute(one, ('blk', 'grp'), first)  2.74 us
    ppermute x1, starting transfers between devices, body(): two = lax.ppermute(two, ('blk', 'grp'), second)  1.8 us
    pallas_call x1, Pallas kernels, finish(): pl.pallas_call(functools.partial(last_body, others, pairs), out_shape=[fu...  1.21 us
  transfers between devices with their start and end apart: 8, of which 3 were waited for; matrix products, arithmetic and copies ran while one was open for 0% of the time, Pallas kernels for 16%

profile of v9, /device:TPU:0, one launch (start us, length us, event | category | flops | bytes accessed | tf_op | source)
XLA Modules:
  0.0 30.2 jit_solution(14623627878392053336)
XLA Ops:
  0.6 0.0 copy-start
  0.6 0.6 %collective-permute-start = (f32[128,768]{1,0:T(8,128)}, f32[128,768]{1,0:T(8,128)S(1)}, u32[]{:S(2)}, u32[]{:S(2)}) collective-permute-start(f32[128,768]{1,0:T(8,128)} %y_any.1), channel_id=1, source_target_pairs={{0,2},{4,6},{8,10},{12,14},{16,18},{20,22},{24,26},{28,30},{2,0},{... | collective-permute-start | bytes 1179656 | tf_op jit(solution)/shard_map/ppermute | solution.py:22
  1.2 2.6 %collective-permute-start.3 = (f32[128,768]{1,0:T(8,128)}, f32[128,768]{1,0:T(8,128)S(1)}, u32[]{:S(2)}, u32[]{:S(2)}) collective-permute-start(f32[128,768]{1,0:T(8,128)} %x_any.1), channel_id=1, source_target_pairs={{0,1},{1,0},{2,3},{3,2},{4,5},{5,4},{6,7},{7,6},{8,9},{9,8},{10,11... | collective-permute-start | bytes 1179656 | tf_op jit(solution)/shard_map/ppermute | solution.py:50
  3.8 4.3 %collective-permute-start.1 = (f32[128,768]{1,0:T(8,128)}, f32[128,768]{1,0:T(8,128)S(1)}, u32[]{:S(2)}, u32[]{:S(2)}) collective-permute-start(f32[128,768]{1,0:T(8,128)} %y_any.1), channel_id=1, source_target_pairs={{2,4},{6,8},{10,12},{14,16},{18,20},{22,24},{26,28},{30,0},{4,2},{... | collective-permute-start | bytes 1179656 | tf_op jit(solution)/shard_map/ppermute | solution.py:22
  8.1 0.0 copy-done
  8.1 0.5 %collective-permute-start.2 = (f32[1,128]{1,0:T(1,128)S(1)}, f32[1,128]{1,0:T(1,128)S(1)}, u32[]{:S(2)}, u32[]{:S(2)}) collective-permute-start(f32[1,128]{1,0:T(1,128)S(1)} %bitcast.2), channel_id=1, source_target_pairs={{0,1},{1,0},{2,3},{3,2},{4,5},{5,4},{6,7},{7,6},{8,9},{9,8},{10,11... | collective-permute-start | bytes 1544 | tf_op jit(solution)/shard_map/ppermute | solution.py:50
  9.9 0.0 collective-permute-done.near_ref
  9.9 3.2 %shard_map.76 = (f32[2,128]{1,0:T(2,128)S(1)}, f32[128,768]{1,0:T(8,128)S(1)}, f32[128,1]{1,0:T(8,128)S(1)}, f32[128,768]{1,0:T(8,128)S(1)}, f32[128,1]{1,0:T(8,...) custom-call(f32[1]{0:T(128)S(6)} %copy.8.lt, ...), custom_call_target="tpu_custom_call" | custom-call | tf_op jit(solution)/shard_map/pallas_call | solution.py:281
  13.1 0.6 %collective-permute-done.2.refs_1_.refs_2_ = f32[1,128]{1,0:T(1,128)S(1)} collective-permute-done((f32[1,128]{1,0:T(1,128)S(1)}, f32[1,128]{1,0:T(1,128)S(1)}, u32[]{:S(2)}, u32[]{:S(2)}) %collective-permute-start.2) | collective-permute-done | bytes 544 | tf_op jit(solution)/shard_map/ppermute | solution.py:50
  13.8 0.0 collective-permute-done.3.refs_0_
  13.8 1.1 %shard_map.77 = (bf16[512,768]{1,0:T(8,128)(2,1)S(1)}, f32[128,768]{1,0:T(8,128)S(1)}, f32[1,128]{1,0:T(1,128)S(1)}, f32[128,256]{1,0:T(8,128)S(1)}) custom-call(f32[2,128]{1,0:T(2,128)S(1)} %get-tuple-element.33.tb_ref, f32[128,768]{1,0:T(8,128)S(1)} %collective-permute-done.3.refs_0_, f32[1,128]{1,0:T(1,128)S(1)} %collective-permute-done.2.refs_1_.refs_2_, ...), custom_call_target="tpu_custom_call" | custom-call | tf_op jit(solution)/shard_map/pallas_call | solution.py:281
  14.8 0.0 collective-permute-done.1.refs_0_
  14.9 0.9 %shard_map.78 = (f32[128,768]{1,0:T(8,128)S(1)}, f32[1,128]{1,0:T(1,128)S(1)}, f32[1,128]{1,0:T(1,128)S(1)}, bf16[256,768]{1,0:T(8,128)(2,1)S(1)}, bf16[256,256]...) custom-call(f32[2,128]{1,0:T(2,128)S(1)} %get-tuple-element.33.tb_ref, f32[128,768]{1,0:T(8,128)S(1)} %collective-permute-done.1.refs_0_, ...), custom_call_target="tpu_custom_call" | custom-call | tf_op jit(solution)/shard_map/pallas_call | solution.py:281
  15.7 0.4 %shard_map.80 = f32[128,768]{1,0:T(8,128)S(1)} custom-call(f32[128,768]{1,0:T(8,128)S(1)} %get-tuple-element.37.refs_4_.refs_0_, bf16[256,768]{1,0:T(8,128)(2,1)S(1)} %get-tuple-element.41.fs_ref.refs_1_, bf16[256,256]{1,0:T(8,128)(2,1)S(1)} %get-tuple-element.49.refs_2_, f32[2,128,128]{2,1,0:T(8,128)S(1)} %get-tuple-element.40.slope_ref.refs_3_, ...), custom_call_target="tpu_custom_call" | custom-call | tf_op jit(solution)/shard_map/pallas_call | solution.py:281
  16.1 1.8 %collective-permute-start.6 = (f32[128,768]{1,0:T(8,128)S(1)}, f32[128,768]{1,0:T(8,128)S(1)}, u32[]{:S(2)}, u32[]{:S(2)}) collective-permute-start(f32[128,768]{1,0:T(8,128)S(1)} %shard_map.80), channel_id=1, source_target_pairs={{0,1},{1,0},{2,4},{3,5},{4,2},{5,3},{6,8},{7,9},{8,6},{9,7},{10,11... | collective-permute-start | bytes 1179656 | tf_op jit(solution)/shard_map/ppermute | solution.py:392
  17.9 0.7 %shard_map.79 = (f32[128,768]{1,0:T(8,128)S(1)}, f32[128,768]{1,0:T(8,128)S(1)}, f32[128,768]{1,0:T(8,128)S(1)}) custom-call(f32[128,768]{1,0:T(8,128)S(1)} %get-tuple-element.31.gx_in, f32[256,768]{1,0:T(8,128)S(1)} %get-tuple-element.32.gy_in, f32[2,128,128]{2,1,0:T(8,128)S(1)} %get-tuple-element.40.slope_ref.refs_3_, ...), custom_call_target="tpu_custom_call" | custom-call | tf_op jit(solution)/shard_map/pallas_call | solution.py:281
  18.6 0.5 %collective-permute-start.4 = (f32[128,768]{1,0:T(8,128)S(1)}, f32[128,768]{1,0:T(8,128)S(1)}, u32[]{:S(2)}, u32[]{:S(2)}) collective-permute-start(f32[128,768]{1,0:T(8,128)S(1)} %get-tuple-element.47), channel_id=1, source_target_pairs={{0,2},{4,6},{8,10},{12,14},{16,18},{20,22},{24,26},{28,30},{2,0},{... | collective-permute-start | bytes 1179656 | tf_op jit(solution)/shard_map/ppermute | solution.py:22
  19.1 3.3 %collective-permute-start.5 = (f32[128,768]{1,0:T(8,128)S(1)}, f32[128,768]{1,0:T(8,128)S(1)}, u32[]{:S(2)}, u32[]{:S(2)}) collective-permute-start(f32[128,768]{1,0:T(8,128)S(1)} %get-tuple-element.48), channel_id=1, source_target_pairs={{0,30},{1,31},{2,3},{3,2},{4,5},{5,4},{6,7},{7,6},{8,9},{9,8},{10,... | collective-permute-start | bytes 1179656 | tf_op jit(solution)/shard_map/ppermute | solution.py:382
  22.4 1.0 %collective-permute-start.7 = (f32[1,128]{1,0:T(1,128)S(1)}, f32[1,128]{1,0:T(1,128)S(1)}, u32[]{:S(2)}, u32[]{:S(2)}) collective-permute-start(f32[1,128]{1,0:T(1,128)S(1)} %get-tuple-element.51), channel_id=1, source_target_pairs={{0,1},{1,0},{2,3},{3,2},{4,5},{5,4},{6,7},{7,6},{8,9},{9,8},{10,11... | collective-permute-start | bytes 1544 | tf_op jit(solution)/shard_map/ppermute | solution.py:50
  23.3 2.9 %collective-permute-done.7.refs_10_ = f32[1,128]{1,0:T(1,128)S(1)} collective-permute-done((f32[1,128]{1,0:T(1,128)S(1)}, f32[1,128]{1,0:T(1,128)S(1)}, u32[]{:S(2)}, u32[]{:S(2)}) %collective-permute-start.7) | collective-permute-done | bytes 544 | tf_op jit(solution)/shard_map/ppermute | solution.py:50
  26.2 0.0 collective-permute-done.6.refs_8_
  26.2 0.0 collective-permute-done.4.refs_6_
  26.2 2.7 %collective-permute-done.5.refs_7_ = f32[128,768]{1,0:T(8,128)S(1)} collective-permute-done((f32[128,768]{1,0:T(8,128)S(1)}, f32[128,768]{1,0:T(8,128)S(1)}, u32[]{:S(2)}, u32[]{:S(2)}) %collective-permute-start.5) | collective-permute-done | bytes 393248 | tf_op jit(solution)/shard_map/ppermute | solution.py:382
  29.0 1.2 %shard_map.81 = (f32[128,768]{1,0:T(8,128)}, f32[128,768]{1,0:T(8,128)}, f32[1,128]{1,0:T(1,128)}) custom-call(f32[128,768]{1,0:T(8,128)S(1)} %get-tuple-element.29.refs_0_, f32[128,1]{1,0:T(8,128)S(1)} %get-tuple-element.30.refs_1_, f32[128,768]{1,0:T(8,128)S(1)} %get-tuple-element.43.refs_2_, f32[128,768]{1,0:T(8,128)S(1)} %get-tuple-element.44.refs_3_, ...), custom_call_target="tpu_custom_call" | custom-call | tf_op jit(solution)/shard_map/pallas_call | solution.py:294
Async XLA Ops:
  0.6 7.4 %copy-start = (f32[128]{0:T(128)S(1)}, f32[128]{0:T(128)}, u32[]{:S(2)}) copy-start(f32[128]{0:T(128)} %param.9) | copy-start | bytes 1540
  0.6 9.3 %collective-permute-start = (f32[128,768]{1,0:T(8,128)}, f32[128,768]{1,0:T(8,128)S(1)}, u32[]{:S(2)}, u32[]{:S(2)}) collective-permute-start(f32[128,768]{1,0:T(8,128)} %y_any.1), channel_id=1, source_target_pairs={{0,2},{4,6},{8,10},{12,14},{16,18},{20,22},{24,26},{28,30},{2,0},{... | collective-permute-start | bytes 1179656 | tf_op jit(solution)/shard_map/ppermute | solution.py:22
  1.2 12.6 %collective-permute-start.3 = (f32[128,768]{1,0:T(8,128)}, f32[128,768]{1,0:T(8,128)S(1)}, u32[]{:S(2)}, u32[]{:S(2)}) collective-permute-start(f32[128,768]{1,0:T(8,128)} %x_any.1), channel_id=1, source_target_pairs={{0,1},{1,0},{2,3},{3,2},{4,5},{5,4},{6,7},{7,6},{8,9},{9,8},{10,11... | collective-permute-start | bytes 1179656 | tf_op jit(solution)/shard_map/ppermute | solution.py:50
  3.8 11.1 %collective-permute-start.1 = (f32[128,768]{1,0:T(8,128)}, f32[128,768]{1,0:T(8,128)S(1)}, u32[]{:S(2)}, u32[]{:S(2)}) collective-permute-start(f32[128,768]{1,0:T(8,128)} %y_any.1), channel_id=1, source_target_pairs={{2,4},{6,8},{10,12},{14,16},{18,20},{22,24},{26,28},{30,0},{4,2},{... | collective-permute-start | bytes 1179656 | tf_op jit(solution)/shard_map/ppermute | solution.py:22
  8.1 5.7 %collective-permute-start.2 = (f32[1,128]{1,0:T(1,128)S(1)}, f32[1,128]{1,0:T(1,128)S(1)}, u32[]{:S(2)}, u32[]{:S(2)}) collective-permute-start(f32[1,128]{1,0:T(1,128)S(1)} %bitcast.2), channel_id=1, source_target_pairs={{0,1},{1,0},{2,3},{3,2},{4,5},{5,4},{6,7},{7,6},{8,9},{9,8},{10,11... | collective-permute-start | bytes 1544 | tf_op jit(solution)/shard_map/ppermute | solution.py:50
  16.1 10.1 %collective-permute-start.6 = (f32[128,768]{1,0:T(8,128)S(1)}, f32[128,768]{1,0:T(8,128)S(1)}, u32[]{:S(2)}, u32[]{:S(2)}) collective-permute-start(f32[128,768]{1,0:T(8,128)S(1)} %shard_map.80), channel_id=1, source_target_pairs={{0,1},{1,0},{2,4},{3,5},{4,2},{5,3},{6,8},{7,9},{8,6},{9,7},{10,11... | collective-permute-start | bytes 1179656 | tf_op jit(solution)/shard_map/ppermute | solution.py:392
  18.6 7.7 %collective-permute-start.4 = (f32[128,768]{1,0:T(8,128)S(1)}, f32[128,768]{1,0:T(8,128)S(1)}, u32[]{:S(2)}, u32[]{:S(2)}) collective-permute-start(f32[128,768]{1,0:T(8,128)S(1)} %get-tuple-element.47), channel_id=1, source_target_pairs={{0,2},{4,6},{8,10},{12,14},{16,18},{20,22},{24,26},{28,30},{2,0},{... | collective-permute-start | bytes 1179656 | tf_op jit(solution)/shard_map/ppermute | solution.py:22
  19.1 9.9 %collective-permute-start.5 = (f32[128,768]{1,0:T(8,128)S(1)}, f32[128,768]{1,0:T(8,128)S(1)}, u32[]{:S(2)}, u32[]{:S(2)}) collective-permute-start(f32[128,768]{1,0:T(8,128)S(1)} %get-tuple-element.48), channel_id=1, source_target_pairs={{0,30},{1,31},{2,3},{3,2},{4,5},{5,4},{6,7},{7,6},{8,9},{9,8},{10,... | collective-permute-start | bytes 1179656 | tf_op jit(solution)/shard_map/ppermute | solution.py:382
  22.4 3.9 %collective-permute-start.7 = (f32[1,128]{1,0:T(1,128)S(1)}, f32[1,128]{1,0:T(1,128)S(1)}, u32[]{:S(2)}, u32[]{:S(2)}) collective-permute-start(f32[1,128]{1,0:T(1,128)S(1)} %get-tuple-element.51), channel_id=1, source_target_pairs={{0,1},{1,0},{2,3},{3,2},{4,5},{5,4},{6,7},{7,6},{8,9},{9,8},{10,11... | collective-permute-start | bytes 1544 | tf_op jit(solution)/shard_map/ppermute | solution.py:50

commit v10 on v8

--- a/solution.py
+++ b/solution.py
@@ -124,7 +124,7 @@
     w_refs, refs = refs[:others], refs[others:]
     xs_ref, ys_ref, all_ref, refs = *refs[:3], refs[3:]
     gp_refs, refs = refs[:others], refs[others:]
-    sump_refs, slope_refs = refs[:others], refs[others:]
+    sump_refs, slope_refs, row_refs = refs[:others], refs[others : 2 * others], refs[2 * others :]
     temper, bias = scalars_of(tb_ref)
     count = raw_refs[0].shape[0]
     deep = (others + 1) * count
@@ -133,16 +133,18 @@
     all_ref[deep : deep + count] = xs_ref[count:]
     for s in range(others):
         raw = raw_refs[s][...]
-        px = stacked(raw * scale_of(raw))
+        px = stacked(raw)
+        scale = scale_of(raw)
+        row_refs[s][...] = jnp.sum(jnp.where(eye, scale, 0.0), axis=0, keepdims=True)
         here = (s + 1) * count
         all_ref[here : here + count] = px[:count]
         all_ref[deep + here : deep + here + count] = px[count:]
-        z = temper * mm(px, ys_ref, NT) + bias
+        z = (temper * scale) * mm(px, ys_ref, NT) + bias
         weight = jnp.sum(jnp.where(eye, w_refs[s][...], 0.0), axis=1, keepdims=True)
         loss, slope = gated(z, weight * temper)
         sums = jnp.sum(loss, axis=1, keepdims=True)
         sump_refs[s][...] = jnp.sum(jnp.where(eye, sums, 0.0), axis=0, keepdims=True)
-        slope_refs[s][...] = slope
+        slope_refs[s][...] = slope * scale
         gp_refs[s][...] = mm(stacked(slope), ys_ref, NN)
 
 
@@ -152,6 +154,7 @@
     w_refs, refs = refs[:members], refs[members:]
     all_ref, gp_in, refs = *refs[:2], refs[2:]
     sum_in, refs = refs[:members], refs[members:]
+    row_refs, refs = refs[:others], refs[others:]
     one_ref, refs = refs[0], refs[1:]
     sum_refs, refs = refs[:members], refs[members:]
     fs_ref, both_ref, slope_ref = refs
@@ -160,10 +163,11 @@
     far = far_ref[...]
     fs_ref[...] = stacked(far)
     scale = scale_of(far)
-    z = (temper * scale) * mm(fs_ref, all_ref, NT) + bias
+    along = jnp.concatenate([jnp.ones((1, count), F32), *[r[...] for r in row_refs]], axis=1)
+    z = (temper * scale) * (along * mm(fs_ref, all_ref, NT)) + bias
     weight = jnp.concatenate([w[...] for w in w_refs], axis=1) * temper
     loss, slope = gated(z, weight)
-    both_ref[...] = stacked(slope)
+    both_ref[...] = stacked(slope * along)
     slope = slope * scale
     sums = jnp.sum(loss, axis=0, keepdims=True)
     for s in range(members):
@@ -227,34 +231,36 @@
         total = total + r[...]
     line[...] = total / pairs
 
-    def run(far_y, next_x):
-        copies = []
-
-        def send(source, target):
-            copies.append(pltpu.make_async_copy(source, target, sem.at[len(copies)]))
-            copies[-1].start()
-
-        send(line, loss_out)
-        sides = [
-            (unit_x, scale_x, [own_x, next_x, *back_x], x_out),
-            (unit_y, scale_y, [own_y, near_y, far_y], y_out),
-        ]
-        for k, (unit_ref, scale_ref, grads, out_ref) in enumerate(sides):
-            for c in range(CHUNKS):
-                here = pl.ds(c * rows, rows)
-                grad = grads[0][here, :]
-                for r in grads[1:]:
-                    grad = grad + r[here, :]
-                unit = unit_ref[here, :]
-                inner = jnp.sum(unit * grad, axis=1, keepdims=True)
-                held[k, here, :] = scale_ref[here, :] * (grad - unit * inner)
-                send(held.at[k, here, :], out_ref.at[here, :])
-        for copy in copies:
-            copy.wait()
+    copies = [pltpu.make_async_copy(line, loss_out, sem.at[0])]
+    copies[0].start()
+
+    def side(k, unit_ref, scale_ref, grads, out_ref):
+        for c in range(CHUNKS):
+            here = pl.ds(c * rows, rows)
+            grad = grads[0][here, :]
+            for r in grads[1:]:
+                grad = grad + r[here, :]
+            unit = unit_ref[here, :]
+            inner = jnp.sum(unit * grad, axis=1, keepdims=True)
+            held[k, here, :] = scale_ref[here, :] * (grad - unit * inner)
+            piece(k, c, out_ref).start()
+
+    def piece(k, c, out_ref):
+        here = pl.ds(c * rows, rows)
+        return pltpu.make_async_copy(
+            held.at[k, here, :], out_ref.at[here, :], sem.at[1 + k * CHUNKS + c]
+        )
 
     far_first = far_goes_first()
-    pl.when(far_first)(lambda: run(one, two))
-    pl.when(jnp.logical_not(far_first))(lambda: run(two, one))
+    near_first = jnp.logical_not(far_first)
+    sides = ((0, unit_x, scale_x, x_out), (1, unit_y, scale_y, y_out))
+    mine = ([own_x, *back_x], [own_y, near_y])
+    for (k, unit, scale, out), terms, early, late in zip(sides, mine, (two, one), (one, two)):
+        pl.when(far_first)(functools.partial(side, k, unit, scale, [*terms, early], out))
+        pl.when(near_first)(functools.partial(side, k, unit, scale, [*terms, late], out))
+    copies += [piece(k, c, out) for k, _, _, out in sides for c in range(CHUNKS)]
+    for copy in copies:
+        copy.wait()
 
 
 def shape(*dims, kind=F32):
@@ -345,7 +351,8 @@
         [shape(2 * members * count, width, kind=BF)]
         + [full] * others
         + [line] * others
-        + [shape(count, 2 * count)] * others,
+        + [shape(count, 2 * count)] * others
+        + [line] * others,
         tb,
         *raws,
         *weights[1:],
@@ -354,7 +361,7 @@
     )
     everyone, outs = outs[0], outs[1:]
     gp, outs = outs[:others], outs[others:]
-    sump, slopes = outs[:others], outs[others:]
+    sump, slopes, rows = outs[:others], outs[others : 2 * others], outs[2 * others :]
     outs = call(
         functools.partial(third_body, others),
         [full]
@@ -371,6 +378,7 @@
         gp[0],
         sums,
         *sump,
+        *rows,
     )
     one, outs = outs[0], outs[1:]
     sums, (fs, both, slope) = outs[:members], outs[members:]

time: 31 us -> 30.9 us (level)
  no operation moved by 1% of the time
where the time goes in v10:
time: 30.9 us; the launch traced here: 30.8 us
  waiting for transfers between devices  11.9 us (39%)
  starting transfers between devices  9.56 us (31%)
  Pallas kernels  7.33 us (24%)
  between operations  1.99 us (6%)
    pallas_call x5, Pallas kernels, call(): pl.pallas_call(body, out_shape=[pltpu.VMEM(o.shape, o.dtype) for o in out...  6.13 us
    ppermute x1, waiting for transfers between devices, body(): one = lax.ppermute(one, ('blk', 'grp'), first)  6.05 us
    ppermute x3, starting transfers between devices, exchanged(): return lax.ppermute(x, axis, pairs + [(b, a) for a, b in pairs])  5.11 us
    ppermute x3, waiting for transfers between devices, shifted(): lax.ppermute(x, axis, [(i, (i + by) % length) for i in range(length)])  4.89 us
    ppermute x3, starting transfers between devices, shifted(): lax.ppermute(x, axis, [(i, (i + by) % length) for i in range(length)])  4.14 us
    pallas_call x1, Pallas kernels, finish(): pl.pallas_call(functools.partial(last_body, others, pairs), out_shape=[fu...  1.2 us
    ppermute x3, waiting for transfers between devices, exchanged(): return lax.ppermute(x, axis, pairs + [(b, a) for a, b in pairs])  0.96 us
  transfers between devices with their start and end apart: 8, of which 4 were waited for; matrix products, arithmetic and copies ran while one was open for 0% of the time, Pallas kernels for 16%

profile of v10, /device:TPU:1, one launch (start us, length us, event | category | flops | bytes accessed | tf_op | source)
XLA Modules:
  0.0 30.8 jit_solution(3696382010824551376)
XLA Ops:
  0.6 0.0 copy-start
  0.6 0.1 collective-permute-start
  0.7 2.7 %collective-permute-start.3 = (f32[128,768]{1,0:T(8,128)}, f32[128,768]{1,0:T(8,128)S(1)}, u32[]{:S(2)}, u32[]{:S(2)}) collective-permute-start(f32[128,768]{1,0:T(8,128)} %x_any.1), channel_id=1, source_target_pairs={{0,1},{1,0},{2,3},{3,2},{4,5},{5,4},{6,7},{7,6},{8,9},{9,8},{10,11... | collective-permute-start | bytes 1179656 | tf_op jit(solution)/shard_map/ppermute | solution.py:46
  3.4 1.5 %collective-permute-start.1 = (f32[128,768]{1,0:T(8,128)}, f32[128,768]{1,0:T(8,128)S(1)}, u32[]{:S(2)}, u32[]{:S(2)}) collective-permute-start(f32[128,768]{1,0:T(8,128)} %y_any.1), channel_id=1, source_target_pairs={{2,4},{6,8},{10,12},{14,16},{18,20},{22,24},{26,28},{30,0},{4,2},{... | collective-permute-start | bytes 1179656 | tf_op jit(solution)/shard_map/ppermute | solution.py:22
  4.9 0.0 copy-done
  4.9 0.3 collective-permute-start.2
  6.4 0.0 collective-permute-done.near_ref
  6.5 3.2 %shard_map.76 = (f32[2,128]{1,0:T(2,128)S(1)}, f32[128,768]{1,0:T(8,128)S(1)}, f32[128,1]{1,0:T(8,128)S(1)}, f32[128,768]{1,0:T(8,128)S(1)}, f32[128,1]{1,0:T(8,...) custom-call(f32[1]{0:T(128)S(6)} %copy.8.lt, ...), custom_call_target="tpu_custom_call" | custom-call | tf_op jit(solution)/shard_map/pallas_call | solution.py:283
  9.7 3.4 %collective-permute-done.2.refs_1_.refs_2_ = f32[1,128]{1,0:T(1,128)S(1)} collective-permute-done((f32[1,128]{1,0:T(1,128)S(1)}, f32[1,128]{1,0:T(1,128)S(1)}, u32[]{:S(2)}, u32[]{:S(2)}) %collective-permute-start.2) | collective-permute-done | bytes 544 | tf_op jit(solution)/shard_map/ppermute | solution.py:46
  13.0 0.0 collective-permute-done.3.refs_0_
  13.0 1.0 %shard_map.77 = (bf16[512,768]{1,0:T(8,128)(2,1)S(1)}, f32[128,768]{1,0:T(8,128)S(1)}, f32[1,128]{1,0:T(1,128)S(1)}, f32[128,256]{1,0:T(8,128)S(1)}, f32[1,128]{1,0:T(1,128)S(1)}) custom-call(f32[2,128]{1,0:T(2,128)S(1)} %get-tuple-element.34.tb_ref, f32[128,768]{1,0:T(8,128)S(1)} %collective-permute-done.3.refs_0_, ...), custom_call_target="tpu_custom_call" | custom-call | tf_op jit(solution)/shard_map/pallas_call | solution.py:283
  14.1 1.0 %collective-permute-done.1.refs_0_ = f32[128,768]{1,0:T(8,128)S(1)} collective-permute-done((f32[128,768]{1,0:T(8,128)}, f32[128,768]{1,0:T(8,128)S(1)}, u32[]{:S(2)}, u32[]{:S(2)}) %collective-permute-start.1) | collective-permute-done | bytes 393248 | tf_op jit(solution)/shard_map/ppermute | solution.py:22
  15.0 0.8 %shard_map.78 = (f32[128,768]{1,0:T(8,128)S(1)}, f32[1,128]{1,0:T(1,128)S(1)}, f32[1,128]{1,0:T(1,128)S(1)}, bf16[256,768]{1,0:T(8,128)(2,1)S(1)}, bf16[256,256]...) custom-call(f32[2,128]{1,0:T(2,128)S(1)} %get-tuple-element.34.tb_ref, f32[128,768]{1,0:T(8,128)S(1)} %collective-permute-done.1.refs_0_, ...), custom_call_target="tpu_custom_call" | custom-call | tf_op jit(solution)/shard_map/pallas_call | solution.py:283
  15.9 0.4 %shard_map.80 = f32[128,768]{1,0:T(8,128)S(1)} custom-call(f32[128,768]{1,0:T(8,128)S(1)} %get-tuple-element.38.refs_4_.refs_0_, bf16[256,768]{1,0:T(8,128)(2,1)S(1)} %get-tuple-element.43.fs_ref.refs_1_, bf16[256,256]{1,0:T(8,128)(2,1)S(1)} %get-tuple-element.51.refs_2_, f32[2,128,128]{2,1,0:T(8,128)S(1)} %get-tuple-element.42.slope_ref.refs_3_, ...), custom_call_target="tpu_custom_call" | custom-call | tf_op jit(solution)/shard_map/pallas_call | solution.py:283
  16.3 0.3 %collective-permute-start.6 = (f32[128,768]{1,0:T(8,128)S(1)}, f32[128,768]{1,0:T(8,128)S(1)}, u32[]{:S(2)}, u32[]{:S(2)}) collective-permute-start(f32[128,768]{1,0:T(8,128)S(1)} %shard_map.80), channel_id=1, source_target_pairs={{0,30},{1,31},{2,3},{3,2},{4,5},{5,4},{6,8},{7,9},{8,6},{9,7},{10,... | collective-permute-start | bytes 1179656 | tf_op jit(solution)/shard_map/ppermute | solution.py:396
  16.6 0.7 %shard_map.79 = (f32[128,768]{1,0:T(8,128)S(1)}, f32[128,768]{1,0:T(8,128)S(1)}, f32[128,768]{1,0:T(8,128)S(1)}) custom-call(f32[128,768]{1,0:T(8,128)S(1)} %get-tuple-element.32.gx_in, f32[256,768]{1,0:T(8,128)S(1)} %get-tuple-element.33.gy_in, f32[2,128,128]{2,1,0:T(8,128)S(1)} %get-tuple-element.42.slope_ref.refs_3_, ...), custom_call_target="tpu_custom_call" | custom-call | tf_op jit(solution)/shard_map/pallas_call | solution.py:283
  17.3 3.5 %collective-permute-start.4 = (f32[128,768]{1,0:T(8,128)S(1)}, f32[128,768]{1,0:T(8,128)S(1)}, u32[]{:S(2)}, u32[]{:S(2)}) collective-permute-start(f32[128,768]{1,0:T(8,128)S(1)} %get-tuple-element.49), channel_id=1, source_target_pairs={{0,2},{4,6},{8,10},{12,14},{16,18},{20,22},{24,26},{28,30},{2,0},{... | collective-permute-start | bytes 1179656 | tf_op jit(solution)/shard_map/ppermute | solution.py:22
  20.8 0.0 collective-permute-start.5
  20.8 1.2 %collective-permute-start.7 = (f32[1,128]{1,0:T(1,128)S(1)}, f32[1,128]{1,0:T(1,128)S(1)}, u32[]{:S(2)}, u32[]{:S(2)}) collective-permute-start(f32[1,128]{1,0:T(1,128)S(1)} %get-tuple-element.53), channel_id=1, source_target_pairs={{0,1},{1,0},{2,3},{3,2},{4,5},{5,4},{6,7},{7,6},{8,9},{9,8},{10,11... | collective-permute-start | bytes 1544 | tf_op jit(solution)/shard_map/ppermute | solution.py:46
  22.0 1.5 %collective-permute-done.7.refs_10_ = f32[1,128]{1,0:T(1,128)S(1)} collective-permute-done((f32[1,128]{1,0:T(1,128)S(1)}, f32[1,128]{1,0:T(1,128)S(1)}, u32[]{:S(2)}, u32[]{:S(2)}) %collective-permute-start.7) | collective-permute-done | bytes 544 | tf_op jit(solution)/shard_map/ppermute | solution.py:46
  23.5 0.0 collective-permute-done.6.refs_8_
  23.5 0.0 collective-permute-done.4.refs_6_
  23.5 6.0 %collective-permute-done.5.refs_7_ = f32[128,768]{1,0:T(8,128)S(1)} collective-permute-done((f32[128,768]{1,0:T(8,128)S(1)}, f32[128,768]{1,0:T(8,128)S(1)}, u32[]{:S(2)}, u32[]{:S(2)}) %collective-permute-start.5) | collective-permute-done | bytes 393248 | tf_op jit(solution)/shard_map/ppermute | solution.py:386
  29.6 1.2 %shard_map.81 = (f32[128,768]{1,0:T(8,128)}, f32[128,768]{1,0:T(8,128)}, f32[1,128]{1,0:T(1,128)}) custom-call(f32[128,768]{1,0:T(8,128)S(1)} %get-tuple-element.30.refs_0_, f32[128,1]{1,0:T(8,128)S(1)} %get-tuple-element.31.refs_1_, f32[128,768]{1,0:T(8,128)S(1)} %get-tuple-element.45.refs_2_, f32[128,768]{1,0:T(8,128)S(1)} %get-tuple-element.46.refs_3_, ...), custom_call_target="tpu_custom_call" | custom-call | tf_op jit(solution)/shard_map/pallas_call | solution.py:296
Async XLA Ops:
  0.6 4.3 %copy-start = (f32[128]{0:T(128)S(1)}, f32[128]{0:T(128)}, u32[]{:S(2)}) copy-start(f32[128]{0:T(128)} %param.9) | copy-start | bytes 1540
  0.6 5.8 %collective-permute-start = (f32[128,768]{1,0:T(8,128)}, f32[128,768]{1,0:T(8,128)S(1)}, u32[]{:S(2)}, u32[]{:S(2)}) collective-permute-start(f32[128,768]{1,0:T(8,128)} %y_any.1), channel_id=1, source_target_pairs={{0,2},{4,6},{8,10},{12,14},{16,18},{20,22},{24,26},{28,30},{2,0},{... | collective-permute-start | bytes 1179656 | tf_op jit(solution)/shard_map/ppermute | solution.py:22
  0.7 12.3 %collective-permute-start.3 = (f32[128,768]{1,0:T(8,128)}, f32[128,768]{1,0:T(8,128)S(1)}, u32[]{:S(2)}, u32[]{:S(2)}) collective-permute-start(f32[128,768]{1,0:T(8,128)} %x_any.1), channel_id=1, source_target_pairs={{0,1},{1,0},{2,3},{3,2},{4,5},{5,4},{6,7},{7,6},{8,9},{9,8},{10,11... | collective-permute-start | bytes 1179656 | tf_op jit(solution)/shard_map/ppermute | solution.py:46
  3.4 11.6 %collective-permute-start.1 = (f32[128,768]{1,0:T(8,128)}, f32[128,768]{1,0:T(8,128)S(1)}, u32[]{:S(2)}, u32[]{:S(2)}) collective-permute-start(f32[128,768]{1,0:T(8,128)} %y_any.1), channel_id=1, source_target_pairs={{2,4},{6,8},{10,12},{14,16},{18,20},{22,24},{26,28},{30,0},{4,2},{... | collective-permute-start | bytes 1179656 | tf_op jit(solution)/shard_map/ppermute | solution.py:22
  4.9 8.1 %collective-permute-start.2 = (f32[1,128]{1,0:T(1,128)S(1)}, f32[1,128]{1,0:T(1,128)S(1)}, u32[]{:S(2)}, u32[]{:S(2)}) collective-permute-start(f32[1,128]{1,0:T(1,128)S(1)} %bitcast.2), channel_id=1, source_target_pairs={{0,1},{1,0},{2,3},{3,2},{4,5},{5,4},{6,7},{7,6},{8,9},{9,8},{10,11... | collective-permute-start | bytes 1544 | tf_op jit(solution)/shard_map/ppermute | solution.py:46
  16.3 7.2 %collective-permute-start.6 = (f32[128,768]{1,0:T(8,128)S(1)}, f32[128,768]{1,0:T(8,128)S(1)}, u32[]{:S(2)}, u32[]{:S(2)}) collective-permute-start(f32[128,768]{1,0:T(8,128)S(1)} %shard_map.80), channel_id=1, source_target_pairs={{0,30},{1,31},{2,3},{3,2},{4,5},{5,4},{6,8},{7,9},{8,6},{9,7},{10,... | collective-permute-start | bytes 1179656 | tf_op jit(solution)/shard_map/ppermute | solution.py:396
  17.3 6.3 %collective-permute-start.4 = (f32[128,768]{1,0:T(8,128)S(1)}, f32[128,768]{1,0:T(8,128)S(1)}, u32[]{:S(2)}, u32[]{:S(2)}) collective-permute-start(f32[128,768]{1,0:T(8,128)S(1)} %get-tuple-element.49), channel_id=1, source_target_pairs={{0,2},{4,6},{8,10},{12,14},{16,18},{20,22},{24,26},{28,30},{2,0},{... | collective-permute-start | bytes 1179656 | tf_op jit(solution)/shard_map/ppermute | solution.py:22
  20.8 8.8 %collective-permute-start.5 = (f32[128,768]{1,0:T(8,128)S(1)}, f32[128,768]{1,0:T(8,128)S(1)}, u32[]{:S(2)}, u32[]{:S(2)}) collective-permute-start(f32[128,768]{1,0:T(8,128)S(1)} %get-tuple-element.50), channel_id=1, source_target_pairs={{0,1},{1,0},{2,4},{3,5},{4,2},{5,3},{6,7},{7,6},{8,9},{9,8},{10,12... | collective-permute-start | bytes 1179656 | tf_op jit(solution)/shard_map/ppermute | solution.py:386
  20.8 2.7 %collective-permute-start.7 = (f32[1,128]{1,0:T(1,128)S(1)}, f32[1,128]{1,0:T(1,128)S(1)}, u32[]{:S(2)}, u32[]{:S(2)}) collective-permute-start(f32[1,128]{1,0:T(1,128)S(1)} %get-tuple-element.53), channel_id=1, source_target_pairs={{0,1},{1,0},{2,3},{3,2},{4,5},{5,4},{6,7},{7,6},{8,9},{9,8},{10,11... | collective-permute-start | bytes 1544 | tf_op jit(solution)/shard_map/ppermute | solution.py:46

commit v11 on v6

--- a/solution.py
+++ b/solution.py
@@ -124,7 +124,7 @@
     w_refs, refs = refs[:others], refs[others:]
     xs_ref, ys_ref, all_ref, refs = *refs[:3], refs[3:]
     gp_refs, refs = refs[:others], refs[others:]
-    sump_refs, slope_refs = refs[:others], refs[others:]
+    sump_refs, slope_refs, row_refs = refs[:others], refs[others : 2 * others], refs[2 * others :]
     temper, bias = scalars_of(tb_ref)
     count = raw_refs[0].shape[0]
     deep = (others + 1) * count
@@ -133,16 +133,18 @@
     all_ref[deep : deep + count] = xs_ref[count:]
     for s in range(others):
         raw = raw_refs[s][...]
-        px = stacked(raw * scale_of(raw))
+        px = stacked(raw)
+        scale = scale_of(raw)
+        row_refs[s][...] = jnp.sum(jnp.where(eye, scale, 0.0), axis=0, keepdims=True)
         here = (s + 1) * count
         all_ref[here : here + count] = px[:count]
         all_ref[deep + here : deep + here + count] = px[count:]
-        z = temper * mm(px, ys_ref, NT) + bias
+        z = (temper * scale) * mm(px, ys_ref, NT) + bias
         weight = jnp.sum(jnp.where(eye, w_refs[s][...], 0.0), axis=1, keepdims=True)
         loss, slope = gated(z, weight * temper)
         sums = jnp.sum(loss, axis=1, keepdims=True)
         sump_refs[s][...] = jnp.sum(jnp.where(eye, sums, 0.0), axis=0, keepdims=True)
-        slope_refs[s][...] = slope
+        slope_refs[s][...] = slope * scale
         gp_refs[s][...] = mm(stacked(slope), ys_ref, NN)
 
 
@@ -153,6 +155,7 @@
     all_ref, refs = refs[0], refs[1:]
     gp_in, refs = refs[:others], refs[others:]
     sum_in, refs = refs[:members], refs[members:]
+    row_refs, refs = refs[:others], refs[others:]
     one_ref, two_ref, refs = *refs[:2], refs[2:]
     gp_refs, refs = refs[: others - 1], refs[others - 1 :]
     sum_refs, refs = refs[:members], refs[members:]
@@ -162,10 +165,11 @@
     far = far_ref[...]
     fs_ref[...] = stacked(far)
     scale = scale_of(far)
-    z = (temper * scale) * mm(fs_ref, all_ref, NT) + bias
+    along = jnp.concatenate([jnp.ones((1, count), F32), *[r[...] for r in row_refs]], axis=1)
+    z = (temper * scale) * (along * mm(fs_ref, all_ref, NT)) + bias
     weight = jnp.concatenate([w[...] for w in w_refs], axis=1) * temper
     loss, slope = gated(z, weight)
-    both_ref[...] = stacked(slope)
+    both_ref[...] = stacked(slope * along)
     slope = slope * scale
     sums = jnp.sum(loss, axis=0, keepdims=True)
     for s in range(members):
@@ -333,7 +337,8 @@
         [shape(2 * members * count, width, kind=BF)]
         + [full] * others
         + [line] * others
-        + [shape(count, 2 * count)] * others,
+        + [shape(count, 2 * count)] * others
+        + [line] * others,
         tb,
         *raws,
         *weights[1:],
@@ -342,7 +347,7 @@
     )
     everyone, outs = outs[0], outs[1:]
     gp, outs = outs[:others], outs[others:]
-    sump, slopes = outs[:others], outs[others:]
+    sump, slopes, rows = outs[:others], outs[others : 2 * others], outs[2 * others :]
     outs = call(
         functools.partial(third_body, others),
         [full, full]
@@ -356,6 +361,7 @@
         *gp,
         sums,
         *sump,
+        *rows,
         scratch=[
             pltpu.VMEM((2 * count, members * count), BF),
             pltpu.VMEM((others, 2 * count, count), BF),

time: 30.2 us -> 30.2 us (level)
  no operation moved by 1% of the time
where the time goes in v11:
time: 30.2 us; the launch traced here: 30 us
  waiting for transfers between devices  13.2 us (44%)
  starting transfers between devices  7.59 us (25%)
  Pallas kernels  7.17 us (24%)
  between operations  1.99 us (7%)
    ppermute x3, waiting for transfers between devices, shifted(): lax.ppermute(x, axis, [(i, (i + by) % length) for i in range(length)])  12.3 us
    pallas_call x4, Pallas kernels, call(): pl.pallas_call(body, out_shape=[pltpu.VMEM(o.shape, o.dtype) for o in out...  5.94 us
    ppermute x3, starting transfers between devices, shifted(): lax.ppermute(x, axis, [(i, (i + by) % length) for i in range(length)])  3.5 us
    ppermute x3, starting transfers between devices, exchanged(): return lax.ppermute(x, axis, pairs + [(b, a) for a, b in pairs])  1.64 us
    ppermute x1, starting transfers between devices, body(): one = lax.ppermute(one, ('blk', 'grp'), first)  1.54 us
    pallas_call x1, Pallas kernels, finish(): pl.pallas_call(functools.partial(last_body, others, pairs), out_shape=[fu...  1.23 us
    ppermute x3, waiting for transfers between devices, exchanged(): return lax.ppermute(x, axis, pairs + [(b, a) for a, b in pairs])  0.97 us
    ppermute x1, starting transfers between devices, body(): two = lax.ppermute(two, ('blk', 'grp'), second)  0.91 us
  transfers between devices with their start and end apart: 8, of which 3 were waited for; matrix products, arithmetic and copies ran while one was open for 0% of the time, Pallas kernels for 14%

profile of v11, /device:TPU:1, one launch (start us, length us, event | category | flops | bytes accessed | tf_op | source)
XLA Modules:
  0.0 30.0 jit_solution(3618326394095599388)
XLA Ops:
  0.6 0.0 copy-start
  0.6 0.1 collective-permute-start
  0.7 2.7 %collective-permute-start.3 = (f32[128,768]{1,0:T(8,128)}, f32[128,768]{1,0:T(8,128)S(1)}, u32[]{:S(2)}, u32[]{:S(2)}) collective-permute-start(f32[128,768]{1,0:T(8,128)} %x_any.1), channel_id=1, source_target_pairs={{0,1},{1,0},{2,3},{3,2},{4,5},{5,4},{6,7},{7,6},{8,9},{9,8},{10,11... | collective-permute-start | bytes 1179656 | tf_op jit(solution)/shard_map/ppermute | solution.py:46
  3.4 1.5 %collective-permute-start.1 = (f32[128,768]{1,0:T(8,128)}, f32[128,768]{1,0:T(8,128)S(1)}, u32[]{:S(2)}, u32[]{:S(2)}) collective-permute-start(f32[128,768]{1,0:T(8,128)} %y_any.1), channel_id=1, source_target_pairs={{2,4},{6,8},{10,12},{14,16},{18,20},{22,24},{26,28},{30,0},{4,2},{... | collective-permute-start | bytes 1179656 | tf_op jit(solution)/shard_map/ppermute | solution.py:22
  4.9 0.0 copy-done
  4.9 0.3 collective-permute-start.2
  6.4 0.0 collective-permute-done.near_ref
  6.5 3.2 %shard_map.76 = (f32[2,128]{1,0:T(2,128)S(1)}, f32[128,768]{1,0:T(8,128)S(1)}, f32[128,1]{1,0:T(8,128)S(1)}, f32[128,768]{1,0:T(8,128)S(1)}, f32[128,1]{1,0:T(8,...) custom-call(f32[1]{0:T(128)S(6)} %copy.8.lt, ...), custom_call_target="tpu_custom_call" | custom-call | tf_op jit(solution)/shard_map/pallas_call | solution.py:269
  9.7 3.4 %collective-permute-done.2.refs_1_.refs_2_ = f32[1,128]{1,0:T(1,128)S(1)} collective-permute-done((f32[1,128]{1,0:T(1,128)S(1)}, f32[1,128]{1,0:T(1,128)S(1)}, u32[]{:S(2)}, u32[]{:S(2)}) %collective-permute-start.2) | collective-permute-done | bytes 544 | tf_op jit(solution)/shard_map/ppermute | solution.py:46
  13.0 0.0 collective-permute-done.3.refs_0_
  13.0 1.0 %shard_map.77 = (bf16[512,768]{1,0:T(8,128)(2,1)S(1)}, f32[128,768]{1,0:T(8,128)S(1)}, f32[1,128]{1,0:T(1,128)S(1)}, f32[128,256]{1,0:T(8,128)S(1)}, f32[1,128]{1,0:T(1,128)S(1)}) custom-call(f32[2,128]{1,0:T(2,128)S(1)} %get-tuple-element.34.tb_ref, f32[128,768]{1,0:T(8,128)S(1)} %collective-permute-done.3.refs_0_, ...), custom_call_target="tpu_custom_call" | custom-call | tf_op jit(solution)/shard_map/pallas_call | solution.py:269
  14.1 1.0 %collective-permute-done.1.refs_0_ = f32[128,768]{1,0:T(8,128)S(1)} collective-permute-done((f32[128,768]{1,0:T(8,128)}, f32[128,768]{1,0:T(8,128)S(1)}, u32[]{:S(2)}, u32[]{:S(2)}) %collective-permute-start.1) | collective-permute-done | bytes 393248 | tf_op jit(solution)/shard_map/ppermute | solution.py:22
  15.0 1.0 %shard_map.78 = (f32[128,768]{1,0:T(8,128)S(1)}, f32[128,768]{1,0:T(8,128)S(1)}, f32[1,128]{1,0:T(1,128)S(1)}, f32[1,128]{1,0:T(1,128)S(1)}, bf16[256,768]{1,0:T(8,128)(2,1)S(1)}, /*index=5*/f32[128,128]{1,0:T(8,128)S(1)}) custom-call(f32[2,128]{1,0:T(2,128)S(1)} %get-tuple-element.34.tb_ref, f32[128,768]{1,0:T(8,128)S(1)} %collective-permute-done.1.refs_0_, ...), custom_call_target="tpu_custom_call" | custom-call | tf_op jit(solution)/shard_map/pallas_call | solution.py:269
  16.1 0.7 %shard_map.79 = (f32[128,768]{1,0:T(8,128)S(1)}, f32[128,768]{1,0:T(8,128)S(1)}, f32[128,768]{1,0:T(8,128)S(1)}) custom-call(f32[128,768]{1,0:T(8,128)S(1)} %get-tuple-element.32.gx_in, f32[256,768]{1,0:T(8,128)S(1)} %get-tuple-element.33.gy_in, f32[128,128]{1,0:T(8,128)S(1)} %get-tuple-element.42.slope_ref, bf16[256,768]{1,0:T(8,128)(2,1)S(1)} %get-tuple-element.43.fs_ref, ...), custom_call_target="tpu_custom_call" | custom-call | tf_op jit(solution)/shard_map/pallas_call | solution.py:269
  16.8 0.1 collective-permute-start.4
  16.8 1.5 %collective-permute-start.5 = (f32[128,768]{1,0:T(8,128)S(1)}, f32[128,768]{1,0:T(8,128)S(1)}, u32[]{:S(2)}, u32[]{:S(2)}) collective-permute-start(f32[128,768]{1,0:T(8,128)S(1)} %get-tuple-element.50), channel_id=1, source_target_pairs={{0,1},{1,0},{2,4},{3,5},{4,2},{5,3},{6,7},{7,6},{8,9},{9,8},{10,12... | collective-permute-start | bytes 1179656 | tf_op jit(solution)/shard_map/ppermute | solution.py:374
  18.4 0.9 %collective-permute-start.6 = (f32[128,768]{1,0:T(8,128)S(1)}, f32[128,768]{1,0:T(8,128)S(1)}, u32[]{:S(2)}, u32[]{:S(2)}) collective-permute-start(f32[128,768]{1,0:T(8,128)S(1)} %get-tuple-element.51), channel_id=1, source_target_pairs={{0,30},{1,31},{2,3},{3,2},{4,5},{5,4},{6,8},{7,9},{8,6},{9,7},{10,... | collective-permute-start | bytes 1179656 | tf_op jit(solution)/shard_map/ppermute | solution.py:375
  19.3 0.6 %collective-permute-start.7 = (f32[1,128]{1,0:T(1,128)S(1)}, f32[1,128]{1,0:T(1,128)S(1)}, u32[]{:S(2)}, u32[]{:S(2)}) collective-permute-start(f32[1,128]{1,0:T(1,128)S(1)} %get-tuple-element.53), channel_id=1, source_target_pairs={{0,1},{1,0},{2,3},{3,2},{4,5},{5,4},{6,7},{7,6},{8,9},{9,8},{10,11... | collective-permute-start | bytes 1544 | tf_op jit(solution)/shard_map/ppermute | solution.py:46
  19.9 8.9 %collective-permute-done.7.refs_10_ = f32[1,128]{1,0:T(1,128)S(1)} collective-permute-done((f32[1,128]{1,0:T(1,128)S(1)}, f32[1,128]{1,0:T(1,128)S(1)}, u32[]{:S(2)}, u32[]{:S(2)}) %collective-permute-start.7) | collective-permute-done | bytes 544 | tf_op jit(solution)/shard_map/ppermute | solution.py:46
  28.7 0.0 collective-permute-done.4.refs_6_
  28.7 0.0 collective-permute-done.5.refs_7_
  28.7 0.0 collective-permute-done.6.refs_8_
  28.8 1.2 %shard_map.80 = (f32[128,768]{1,0:T(8,128)}, f32[128,768]{1,0:T(8,128)}, f32[1,128]{1,0:T(1,128)}) custom-call(f32[128,768]{1,0:T(8,128)S(1)} %get-tuple-element.30.refs_0_, f32[128,1]{1,0:T(8,128)S(1)} %get-tuple-element.31.refs_1_, f32[128,768]{1,0:T(8,128)S(1)} %get-tuple-element.45.refs_2_, f32[128,768]{1,0:T(8,128)S(1)} %get-tuple-element.46.refs_3_, ...), custom_call_target="tpu_custom_call" | custom-call | tf_op jit(solution)/shard_map/pallas_call | solution.py:282
Async XLA Ops:
  0.6 4.3 %copy-start = (f32[128]{0:T(128)S(1)}, f32[128]{0:T(128)}, u32[]{:S(2)}) copy-start(f32[128]{0:T(128)} %param.9) | copy-start | bytes 1540
  0.6 5.8 %collective-permute-start = (f32[128,768]{1,0:T(8,128)}, f32[128,768]{1,0:T(8,128)S(1)}, u32[]{:S(2)}, u32[]{:S(2)}) collective-permute-start(f32[128,768]{1,0:T(8,128)} %y_any.1), channel_id=1, source_target_pairs={{0,2},{4,6},{8,10},{12,14},{16,18},{20,22},{24,26},{28,30},{2,0},{... | collective-permute-start | bytes 1179656 | tf_op jit(solution)/shard_map/ppermute | solution.py:22
  0.7 12.3 %collective-permute-start.3 = (f32[128,768]{1,0:T(8,128)}, f32[128,768]{1,0:T(8,128)S(1)}, u32[]{:S(2)}, u32[]{:S(2)}) collective-permute-start(f32[128,768]{1,0:T(8,128)} %x_any.1), channel_id=1, source_target_pairs={{0,1},{1,0},{2,3},{3,2},{4,5},{5,4},{6,7},{7,6},{8,9},{9,8},{10,11... | collective-permute-start | bytes 1179656 | tf_op jit(solution)/shard_map/ppermute | solution.py:46
  3.4 11.6 %collective-permute-start.1 = (f32[128,768]{1,0:T(8,128)}, f32[128,768]{1,0:T(8,128)S(1)}, u32[]{:S(2)}, u32[]{:S(2)}) collective-permute-start(f32[128,768]{1,0:T(8,128)} %y_any.1), channel_id=1, source_target_pairs={{2,4},{6,8},{10,12},{14,16},{18,20},{22,24},{26,28},{30,0},{4,2},{... | collective-permute-start | bytes 1179656 | tf_op jit(solution)/shard_map/ppermute | solution.py:22
  4.9 8.1 %collective-permute-start.2 = (f32[1,128]{1,0:T(1,128)S(1)}, f32[1,128]{1,0:T(1,128)S(1)}, u32[]{:S(2)}, u32[]{:S(2)}) collective-permute-start(f32[1,128]{1,0:T(1,128)S(1)} %bitcast.2), channel_id=1, source_target_pairs={{0,1},{1,0},{2,3},{3,2},{4,5},{5,4},{6,7},{7,6},{8,9},{9,8},{10,11... | collective-permute-start | bytes 1544 | tf_op jit(solution)/shard_map/ppermute | solution.py:46
  16.8 12.0 %collective-permute-start.4 = (f32[128,768]{1,0:T(8,128)S(1)}, f32[128,768]{1,0:T(8,128)S(1)}, u32[]{:S(2)}, u32[]{:S(2)}) collective-permute-start(f32[128,768]{1,0:T(8,128)S(1)} %get-tuple-element.49), channel_id=1, source_target_pairs={{0,2},{4,6},{8,10},{12,14},{16,18},{20,22},{24,26},{28,30},{2,0},{... | collective-permute-start | bytes 1179656 | tf_op jit(solution)/shard_map/ppermute | solution.py:22
  16.8 11.9 %collective-permute-start.5 = (f32[128,768]{1,0:T(8,128)S(1)}, f32[128,768]{1,0:T(8,128)S(1)}, u32[]{:S(2)}, u32[]{:S(2)}) collective-permute-start(f32[128,768]{1,0:T(8,128)S(1)} %get-tuple-element.50), channel_id=1, source_target_pairs={{0,1},{1,0},{2,4},{3,5},{4,2},{5,3},{6,7},{7,6},{8,9},{9,8},{10,12... | collective-permute-start | bytes 1179656 | tf_op jit(solution)/shard_map/ppermute | solution.py:374
  18.4 10.4 %collective-permute-start.6 = (f32[128,768]{1,0:T(8,128)S(1)}, f32[128,768]{1,0:T(8,128)S(1)}, u32[]{:S(2)}, u32[]{:S(2)}) collective-permute-start(f32[128,768]{1,0:T(8,128)S(1)} %get-tuple-element.51), channel_id=1, source_target_pairs={{0,30},{1,31},{2,3},{3,2},{4,5},{5,4},{6,8},{7,9},{8,6},{9,7},{10,... | collective-permute-start | bytes 1179656 | tf_op jit(solution)/shard_map/ppermute | solution.py:375
  19.3 9.4 %collective-permute-start.7 = (f32[1,128]{1,0:T(1,128)S(1)}, f32[1,128]{1,0:T(1,128)S(1)}, u32[]{:S(2)}, u32[]{:S(2)}) collective-permute-start(f32[1,128]{1,0:T(1,128)S(1)} %get-tuple-element.53), channel_id=1, source_target_pairs={{0,1},{1,0},{2,3},{3,2},{4,5},{5,4},{6,7},{7,6},{8,9},{9,8},{10,11... | collective-permute-start | bytes 1544 | tf_op jit(solution)/shard_map/ppermute | solution.py:46
